TPU v7x, 32 devices: a whole 2x2x4 slice. The times are simulated.
32 devices in a mesh: peer: 8 (over z, y), grp: 4 (over x, core).
Axes of the slice: x: 2, y: 2, z: 4, core: 2. Of those that a mesh axis runs over, the one named last changes fastest.
Arguments:
- tokens: bfloat16 [4096, 2048], P(('peer', 'grp')), may hold values from -6 to 6
- cotangent: bfloat16 [4096, 2048], P(('peer', 'grp')), may hold values from -6 to 6
- expert_ids: int32 [4096, 4], P(('peer', 'grp')), may hold values from 0 to 31, all different within a row; in each aligned block of 128 rows (0 to 127, 128 to 255, ...) at most 32 rows name the same one
- route_prob: float32 [4096, 4], P(('peer', 'grp')), may hold values from 0.1 to 1
- w_gate: bfloat16 [8, 2048, 704], P('peer', None, 'grp'), may hold values from -0.125 to 0.125
- w_up: bfloat16 [8, 2048, 704], P('peer', None, 'grp'), may hold values from -0.125 to 0.125
- w_down: bfloat16 [8, 704, 2048], P('peer', 'grp'), may hold values from -0.21875 to 0.21875
- student_logits: bfloat16 [8, 8, 151936], P('peer', None, 'grp'), may hold values from -24 to 252
- stale_logits: bfloat16 [8, 8, 151936], P('peer', None, 'grp'), may hold values from -24 to 252
- labels: int32 [8, 8], P('peer'), may hold values from 0 to 151935
Outputs:
- layer_out: bfloat16 [4096, 2048], P(('peer', 'grp'))
- input_grad: bfloat16 [4096, 2048], P(('peer', 'grp'))
- prob_grad: float32 [4096, 4], P(('peer', 'grp'))
- distill_loss: float32 [8, 8], P('peer')
- logit_grad: bfloat16 [8, 8, 151936], P('peer', None, 'grp')
Inputs may be any that keep to these rules, and one draw needn't show every extreme that they name: `expert_ids`: each row names 4 different experts; the rows of one device name any one expert at most 32 times.
All inputs are finite; a program needn't handle non-finite values.
Results may differ from a plain program's by a relative error of at most 0.0064.
Values may be sent and summed in bfloat16 or wider, within the bound.
No kernel may reach another device: no remote copies, remote signals or barrier semaphores. Data moves between devices by JAX's collectives and lax.ppermute only.
A program may use at most 64 MiB of HBM per device.

v0:
```python
import jax
import jax.numpy as jnp
from jax import lax
from jax.sharding import PartitionSpec as P

PIECES = 4
CAP = 32


def joined(value, axis, combine):
    everything = jax.tree.map(lambda part: lax.all_gather(part, axis), value)
    leading = jax.tree.map(lambda part: part[0], everything)

    def lap(k, so_far):
        return combine(so_far, jax.tree.map(lambda part: part[k], everything))

    return lax.fori_loop(1, lax.axis_size(axis), lap, leading)


def from_behind(value, axis, steps):
    count = lax.axis_size(axis)
    pairs = [(source, (source + steps) % count) for source in range(count)]
    return lax.ppermute(value, axis, pairs)


def slot_tables(expert_ids, n_window, capacity):
    window_iota = lax.broadcasted_iota(jnp.int32, (1, 1, n_window), 2)
    member = jnp.sum((expert_ids[:, :, None] == window_iota).astype(jnp.int32), axis=1)
    position = jnp.cumsum(member, axis=0) - member
    slot_iota = lax.broadcasted_iota(jnp.int32, (1, capacity, 1), 1)
    select = (position.T[:, None, :] == slot_iota) & (member.T[:, None, :] > 0)
    return (position, select)


def forward_piece(slot_rows, gate_cols, up_cols, down_rows):
    gate_act = jnp.dot(slot_rows, gate_cols, preferred_element_type=jnp.float32)
    up_act = jnp.dot(slot_rows, up_cols, preferred_element_type=jnp.float32)
    hidden = (gate_act * jax.nn.sigmoid(gate_act) * up_act).astype(jnp.bfloat16)
    piece_out = jnp.dot(hidden, down_rows, preferred_element_type=jnp.float32).astype(jnp.bfloat16)
    return (piece_out, gate_act, up_act)


def backward_piece(scaled_rows, gate_act, up_act, gate_cols, up_cols, down_rows):
    contract = (((1,), (1,)), ((), ()))
    grad_hidden = lax.dot_general(
        scaled_rows, down_rows, contract, preferred_element_type=jnp.float32
    )
    sigmoid_gate = jax.nn.sigmoid(gate_act)
    grad_gate = (
        grad_hidden * up_act * sigmoid_gate * (1.0 + gate_act * (1.0 - sigmoid_gate))
    ).astype(jnp.bfloat16)
    grad_up = (grad_hidden * gate_act * sigmoid_gate).astype(jnp.bfloat16)
    piece_grad = lax.dot_general(grad_gate, gate_cols, contract, preferred_element_type=jnp.float32)
    piece_grad = piece_grad + lax.dot_general(
        grad_up, up_cols, contract, preferred_element_type=jnp.float32
    )
    return piece_grad.astype(jnp.bfloat16)


def join_stats(first_side, second_side):
    max_one, sum_one, tmax_one, tsum_one, cross_one, label_one = first_side
    max_two, sum_two, tmax_two, tsum_two, cross_two, label_two = second_side
    max_both = jnp.maximum(max_one, max_two)
    tmax_both = jnp.maximum(tmax_one, tmax_two)
    scale_one = jnp.exp(tmax_one - tmax_both)
    scale_two = jnp.exp(tmax_two - tmax_both)
    sum_both = sum_one * jnp.exp(max_one - max_both) + sum_two * jnp.exp(max_two - max_both)
    tsum_both = tsum_one * scale_one + tsum_two * scale_two
    cross_both = cross_one * scale_one + cross_two * scale_two
    return (max_both, sum_both, tmax_both, tsum_both, cross_both, label_one + label_two)


def distill(student_logits, teacher_now, labels):
    student = student_logits[0].astype(jnp.float32)
    teacher = teacher_now[0].astype(jnp.float32)
    shard_width = student.shape[1]
    vocab_ids = lax.axis_index("grp") * shard_width + lax.broadcasted_iota(
        jnp.int32, student.shape, 1
    )
    label_hit = vocab_ids == labels[0][:, None]
    label_logit = jnp.sum(jnp.where(label_hit, student, 0.0), axis=1)
    local_smax = jnp.max(student, axis=1)
    local_tmax = jnp.max(teacher, axis=1)
    student_exp = jnp.sum(jnp.exp(student - local_smax[:, None]), axis=1)
    teacher_exp = jnp.exp(teacher - local_tmax[:, None])
    teacher_sum = jnp.sum(teacher_exp, axis=1)
    cross_sum = jnp.sum(teacher_exp * (teacher - student), axis=1)
    max_student, student_sum, max_teacher, teacher_sum, cross_sum, label_logit = joined(
        (local_smax, student_exp, local_tmax, teacher_sum, cross_sum, label_logit),
        "grp",
        join_stats,
    )
    lse_student = max_student + jnp.log(student_sum)
    lse_teacher = max_teacher + jnp.log(teacher_sum)
    distill_loss = 2.0 * lse_student - label_logit + cross_sum / teacher_sum - lse_teacher
    teacher_prob = jnp.exp(teacher - lse_teacher[:, None])
    logit_grad = (
        2.0 * jnp.exp(student - lse_student[:, None]) - label_hit.astype(jnp.float32) - teacher_prob
    ).astype(jnp.bfloat16)
    return (distill_loss[None], logit_grad[None])


def body(
    tokens,
    cotangent,
    expert_ids,
    route_prob,
    w_gate,
    w_up,
    w_down,
    student_logits,
    stale_logits,
    labels,
):
    group_size = lax.axis_size("grp")
    n_window = group_size // PIECES
    gate_cols = w_gate[0]
    up_cols = w_up[0]
    down_rows = w_down[0]
    model_width = tokens.shape[1]
    half_cap = CAP // 2
    position, select = slot_tables(expert_ids, n_window, CAP)
    select_bf = select.astype(jnp.bfloat16)
    window_iota = lax.broadcasted_iota(jnp.int32, (1, 1, n_window), 2)
    token_prob = jnp.sum(
        route_prob[:, :, None] * (expert_ids[:, :, None] == window_iota).astype(jnp.float32), axis=1
    )
    slot_prob = jnp.einsum(
        "ect,te->ec", select.astype(jnp.float32), token_prob, precision=lax.Precision.HIGHEST
    )
    slot_rows = jnp.einsum(
        "ect,td->ecd", select_bf, tokens, preferred_element_type=jnp.float32
    ).astype(jnp.bfloat16)
    slot_cot = jnp.einsum("ect,td->ecd", select_bf, cotangent, preferred_element_type=jnp.float32)
    slot_scaled = (slot_prob[:, :, None] * slot_cot).astype(jnp.bfloat16)
    send_rows = jnp.repeat(slot_rows, PIECES, axis=0).reshape(group_size, 2, half_cap, model_width)
    send_scaled = jnp.repeat(slot_scaled, PIECES, axis=0).reshape(
        group_size, 2, half_cap, model_width
    )
    recv_rows = lax.all_to_all(send_rows, "grp", split_axis=0, concat_axis=0, tiled=True)
    recv_scaled = lax.all_to_all(send_scaled, "grp", split_axis=0, concat_axis=0, tiled=True)
    item_count = recv_rows.shape[1]
    flat_rows = recv_rows.reshape(-1, model_width)
    flat_scaled = recv_scaled.reshape(-1, model_width)
    piece_out, gate_act, up_act = forward_piece(flat_rows, gate_cols, up_cols, down_rows)
    piece_out = piece_out.reshape(group_size, item_count, half_cap, model_width)
    piece_grad = backward_piece(flat_scaled, gate_act, up_act, gate_cols, up_cols, down_rows)
    piece_grad = piece_grad.reshape(group_size, item_count, half_cap, model_width)
    back_out = lax.all_to_all(piece_out, "grp", split_axis=0, concat_axis=0, tiled=True)
    back_grad = lax.all_to_all(piece_grad, "grp", split_axis=0, concat_axis=0, tiled=True)
    back_out, back_grad = (back_out, back_grad)
    expert_out = jnp.sum(
        back_out.astype(jnp.float32).reshape(n_window, PIECES, CAP, model_width), axis=1
    )
    expert_grad = jnp.sum(
        back_grad.astype(jnp.float32).reshape(n_window, PIECES, CAP, model_width), axis=1
    )
    in_window = expert_ids < n_window
    safe_ids = jnp.where(in_window, expert_ids, 0)
    slot_index = jnp.take_along_axis(position, safe_ids, axis=1)
    flat_index = safe_ids * CAP + slot_index
    out_rows = jnp.where(
        in_window[:, :, None],
        jnp.take(expert_out.reshape(-1, model_width), flat_index, axis=0),
        0.0,
    )
    grad_rows = jnp.where(
        in_window[:, :, None],
        jnp.take(expert_grad.reshape(-1, model_width), flat_index, axis=0),
        0.0,
    )
    layer_out = jnp.sum(route_prob[:, :, None] * out_rows, axis=1).astype(jnp.bfloat16)
    prob_grad = jnp.sum(cotangent.astype(jnp.float32)[:, None, :] * out_rows, axis=2)
    input_grad = jnp.sum(grad_rows, axis=1).astype(jnp.bfloat16)
    teacher_now = from_behind(stale_logits, "peer", 1)
    distill_loss, logit_grad = distill(student_logits, teacher_now, labels)
    return (layer_out, input_grad, prob_grad, distill_loss, logit_grad)


def solution(mesh):
    placed = (
        P(("peer", "grp"), None),
        P(("peer", "grp"), None),
        P(("peer", "grp"), None),
        P(("peer", "grp"), None),
        P("peer", None, "grp"),
        P("peer", None, "grp"),
        P("peer", "grp", None),
        P("peer", None, "grp"),
        P("peer", None, "grp"),
        P("peer", None),
    )
    return jax.shard_map(
        body,
        mesh=mesh,
        in_specs=placed,
        out_specs=(
            P(("peer", "grp"), None),
            P(("peer", "grp"), None),
            P(("peer", "grp"), None),
            P("peer", None),
            P("peer", None, "grp"),
        ),
        check_vma=False,
    )
```

profile of v0, /device:TPU:0, one launch (start us, length us, event | category | flops | bytes accessed | tf_op | source)
XLA Modules:
  0.0 88.1 jit_solution(13793682521302028346)
XLA Ops:
  0.6 0.0 copy-start
  0.6 3.0 %collective-permute-start = (bf16[1,8,37984]{2,1,0:T(8,128)(2,1)}, bf16[1,8,37984]{2,1,0:T(8,128)(2,1)S(1)}, u32[]{:S(2)}, u32[]{:S(2)}) collective-permute-start(bf16[1,8,37984]{2,1,0:T(8,128)(2,1)} %param.22), channel_id=1, source_target_pairs={{0,4},{4,8},{8,12},{12,16},{16,20},{20,24},{24,28},{28,0},{1,5},{5... | collective-permute-start | bytes 1823240 | tf_op jit(solution)/shard_map/ppermute | solution.py:23
  3.7 0.7 select_reduce_fusion
  4.4 0.1 copy.42
  4.6 0.2 reduce_window_sum.13
  4.7 0.1 fusion.64
  4.8 0.0 copy-start.8
  4.9 1.2 %convolution_convert_fusion.1 = bf16[32,2048]{1,0:T(8,128)(2,1)S(1)} fusion(bf16[128,2048]{1,0:T(8,128)(2,1)} %param.14, s32[128]{0:T(128)S(1)} %sub.111, pred[128]{0:T(512)(128)(4,1)S(1)} %broadcast_compare_fusion.2), kind=kOutput, calls=%fused_computation.36 | convolution fusion | flops 16850944 | bytes 656000 | tf_op jit(solution)/shard_map/ect,td->ecd/dot_general | solution.py:131
  6.1 0.8 broadcast_in_dim.63
  7.0 3.5 %all-to-all-start = ((bf16[4,2,16,2048]{3,2,1,0:T(8,128)(2,1)}), bf16[4,2,16,2048]{3,2,1,0:T(8,128)(2,1)S(1)}, u32[]{:S(2)}, u32[]{:S(2)}) async-start(bf16[4,2,16,2048]{3,2,1,0:T(8,128)(2,1)} %broadcast_in_dim.63), calls=%async_computation | async-start | bytes 1048576 | tf_op jit(solution)/shard_map/all_to_all | solution.py:140
  10.5 0.1 copy.44
  10.6 0.1 reshape.285
  10.7 0.0 copy-start.11
  10.8 3.4 %gather_fusion = s32[512]{0:T(512)S(1)} fusion(s32[128,1]{1,0:T(8,128)S(1)} %get-tuple-element.386, s32[512]{0:T(512)S(1)} %reshape.285), kind=kCustom, calls=%fused_computation.2 | custom fusion | bytes 8192 | tf_op jit(solution)/shard_map/jit(take_along_axis)/gather | solution.py:160
  14.2 0.1 reshape.288
  14.3 0.1 copy.45
  14.4 0.1 copy.47
  14.5 0.1 reshape.348
  14.6 0.4 reduce_max.36
  15.1 0.6 dynamic-slice
  16.3 0.1 convert_dynamic-update-slice_fusion.1
  16.4 0.7 copy.40
  17.2 0.1 copy.41
  17.3 0.1 copy.46
  17.5 1.2 %convert_element_type.89 = f32[128,2048]{1,0:T(8,128)} convert(bf16[128,2048]{1,0:T(8,128)(2,1)S(1)} %copy-done.5) | non-fusion elementwise | flops 262144 | bytes 1572864 | tf_op jit(solution)/shard_map/convert_element_type | solution.py:173
  18.6 0.1 convolution_bitcast_fusion
  18.7 0.2 fusion.17
  19.0 0.2 all-to-all-done
  19.2 0.8 broadcast_in_dim.67
  20.1 4.3 %all-to-all-start.2 = ((bf16[4,2,16,2048]{3,2,1,0:T(8,128)(2,1)}), bf16[4,2,16,2048]{3,2,1,0:T(8,128)(2,1)}, u32[]{:S(2)}, u32[]{:S(2)}) async-start(bf16[4,2,16,2048]{3,2,1,0:T(8,128)(2,1)} %broadcast_in_dim.67), calls=%async_computation.2 | async-start | bytes 1048576 | tf_op jit(solution)/shard_map/all_to_all | solution.py:141
  24.3 0.4 fusion.43
  24.7 1.0 %fusion.39 = f32[128,176]{0,1:T(8,128)} fusion(bf16[128,2048]{1,0:T(8,128)(2,1)S(1)} %bitcast.127, bf16[1,2048,176]{1,2,0:T(8,128)(2,1)S(1)} %copy-done.3), kind=kOutput, calls=%fused_computation.65 | convolution fusion | flops 92274688 | bytes 1335296 | tf_op jit(solution)/shard_map/dot_general | solution.py:37
  25.8 7.4 %all-to-all-done.2 = bf16[4,2,16,2048]{3,2,1,0:T(8,128)(2,1)} async-done(((bf16[4,2,16,2048]{3,2,1,0:T(8,128)(2,1)}), bf16[4,2,16,2048]{3,2,1,0:T(8,128)(2,1)}, u32[]{:S(2)}, u32[]{:S(2)}) %all-to-all-start.2) | async-done | bytes 524320 | tf_op jit(solution)/shard_map/all_to_all | solution.py:141
  33.2 1.6 %fusion.35 = f32[128,176]{0,1:T(8,128)S(1)} fusion(bf16[128,2048]{1,0:T(8,128)(2,1)} %bitcast.18, bf16[1,176,2048]{2,1,0:T(8,128)(2,1)} %param.20), kind=kOutput, calls=%fused_computation.61 | convolution fusion | flops 92274688 | bytes 1335296 | tf_op jit(solution)/shard_map/dot_general | solution.py:45
  34.8 0.4 fusion.41
  35.2 1.1 %fusion.16 = bf16[128,2048]{1,0:T(8,128)(2,1)} fusion(f32[128,2048]{1,0:T(8,128)S(1)} %fusion.41, bf16[1,2048,176]{1,2,0:T(8,128)(2,1)S(1)} %copy-done.3, f32[128,176]{0,1:T(8,128)S(1)} %fusion.35, f32[128,176]{0,1:T(8,128)S(1)} %fusion.43), kind=kOutput, calls=%fused_computation.32 | convolution fusion | flops 92934144 | bytes 2473984 | tf_op jit(solution)/shard_map/dot_general | solution.py:54
  36.4 3.6 %all-to-all-start.3 = ((bf16[4,2,16,2048]{3,2,1,0:T(8,128)(2,1)}), bf16[4,2,16,2048]{3,2,1,0:T(8,128)(2,1)S(1)}, u32[]{:S(2)}, u32[]{:S(2)}) async-start(bf16[4,2,16,2048]{3,2,1,0:T(8,128)(2,1)} %bitcast.19), calls=%async_computation.3 | async-start | bytes 1048576 | tf_op jit(solution)/shard_map/all_to_all | solution.py:150
  40.0 2.0 %convolution_convert_fusion = bf16[128,2048]{1,0:T(8,128)(2,1)} fusion(bf16[1,176,2048]{2,1,0:T(8,128)(2,1)S(1)} %copy-done.4, f32[128,176]{0,1:T(8,128)} %fusion.39, f32[128,176]{0,1:T(8,128)S(1)} %fusion.43), kind=kOutput, calls=%fused_computation.33 | convolution fusion | flops 92672000 | bytes 1425408 | tf_op jit(solution)/shard_map/dot_general | solution.py:39
  42.0 0.4 reduce_max.40
  42.5 0.1 convert_dynamic-update-slice_fusion
  42.6 1.2 %fusion.33 = (f32[8]{0:T(128)S(1)}, f32[8]{0:T(128)S(1)}, f32[8]{0:T(128)S(1)}, f32[8]{0:T(128)S(1)}) fusion(bf16[1,8,37984]{2,1,0:T(8,128)(2,1)S(1)} %collective-permute-done, bf16[1,8,37984]{2,1,0:T(8,128)(2,1)S(1)} %copy-done.1, f32[8]{0:T(128)S(1)} %reduce_max.45, s32[8]{0:T(128)S(1)} %bitcast.137, s32[37984]{0:T(1024)S(1)} %iota_add_fusion, ...), kind=kLoop, calls=%fused_computation.56 | loop fusion | flops 3646432 | bytes 1367648 | tf_op jit(solution)/shard_map/reduce_sum | solution.py:87
  43.7 0.2 dynamic-update-slice.1
  44.0 0.2 dynamic-update-slice.3
  44.2 0.2 dynamic-update-slice.4
  44.4 0.2 dynamic-update-slice.5
  44.6 7.3 %all-reduce.6 = (f32[32]{0:T(128)S(1)}, f32[32]{0:T(128)S(1)}, f32[32]{0:T(128)S(1)}, f32[32]{0:T(128)S(1)}, f32[32]{0:T(128)S(1)}, /*index=5*/f32[32]{0:T(128)S(1)}) all-reduce(f32[32]{0:T(128)S(1)} %convert_dynamic-update-slice_fusion.1, f32[32]{0:T(128)S(1)} %dynamic-update-slice.1, ...), channel_id=2, replica_groups=mesh['peer'=8,'grp'=4] {'grp'}, use_global_device_ids=true, to_apply=%add | all-reduce | flops 192 | bytes 1536
  51.9 0.1 reshape.291
  52.0 0.1 reshape.292
  52.1 0.1 reshape.293
  52.2 0.1 reshape.294
  52.2 0.1 reshape.295
  52.3 0.1 reshape.296
  52.4 0.3 while.25
  52.7 0.5 subtract_bitcast_fusion
  53.2 3.7 %all-to-all-start.1 = ((bf16[4,2,16,2048]{3,2,1,0:T(8,128)(2,1)}), bf16[4,2,16,2048]{3,2,1,0:T(8,128)(2,1)S(1)}, u32[]{:S(2)}, u32[]{:S(2)}) async-start(bf16[4,2,16,2048]{3,2,1,0:T(8,128)(2,1)} %bitcast.128), calls=%async_computation.1 | async-start | bytes 1048576 | tf_op jit(solution)/shard_map/all_to_all | solution.py:149
  56.9 1.4 %fusion.29 = bf16[1,8,37984]{2,1,0:T(8,128)(2,1)} fusion(bf16[1,8,37984]{2,1,0:T(8,128)(2,1)S(1)} %copy-done.1, bf16[1,8,37984]{2,1,0:T(8,128)(2,1)S(1)} %collective-permute-done, f32[8]{0:T(128)S(1)} %get-tuple-element.380, s32[37984]{0:T(1024)S(1)} %iota_add_fusion, f32[8]{0:T(128)S(1)} %get-tuple-element.379, s32[8]{0:T(128)S(1)} %bitcast.138), kind=kLoop, calls=%fused_computation.52 | loop fusion | flops 3038720 | bytes 1975264 | tf_op jit(solution)/shard_map/convert_element_type | solution.py:99
  58.3 0.1 convert_reduce_fusion
  58.4 3.6 %gather_fusion.2 = f32[512,2048]{1,0:T(8,128)} fusion(f32[32,2048]{1,0:T(8,128)S(1)} %bitcast.125, s32[1024]{0:T(1024)S(1)} %pad_clamp_fusion), kind=kCustom, calls=%fused_computation.1.clone | custom fusion | bytes 8390656 | tf_op jit(solution)/shard_map/jit(_take)/gather | solution.py:169
  62.0 5.2 %reshape.355 = f32[128,4,2048]{2,1,0:T(4,128)} reshape(f32[512,2048]{1,0:T(8,128)} %gather_fusion.2) | data formatting | bytes 8388608 | tf_op jit(solution)/shard_map/jit(_take)/gather | solution.py:169
  67.2 0.1 convert_reduce_fusion.1
  67.3 3.6 %gather_fusion.1 = f32[512,2048]{1,0:T(8,128)} fusion(f32[32,2048]{1,0:T(8,128)S(1)} %bitcast.124, s32[1024]{0:T(1024)S(1)} %pad_clamp_fusion), kind=kCustom, calls=%fused_computation.clone | custom fusion | bytes 8390656 | tf_op jit(solution)/shard_map/jit(_take)/gather | solution.py:164
  70.9 5.3 %reshape.351 = f32[128,4,2048]{2,1,0:T(4,128)} reshape(f32[512,2048]{1,0:T(8,128)} %gather_fusion.1) | data formatting | bytes 8388608 | tf_op jit(solution)/shard_map/jit(_take)/gather | solution.py:164
  76.1 11.4 %multiply_reduce_fusion = (f32[128,4]{1,0:T(8,128)S(1)}, bf16[128,2048]{1,0:T(8,128)(2,1)}, bf16[128,2048]{1,0:T(8,128)(2,1)}) fusion(f32[128,4,2048]{2,1,0:T(4,128)} %reshape.351, f32[128,2048]{1,0:T(8,128)S(1)} %copy-done.2, pred[128,4]{1,0:T(8,128)(4,1)S(1)} %copy.46, pred[128,4]{1,0:T(8,128)(4,1)S(1)} %copy.41, f32[128,4]{1,0:T(8,128)S(1)} %copy-done.7, ...), kind=kLoop, calls=%fused_computation.29 | loop fusion | flops 8912384 | bytes 10490880 | tf_op jit(solution)/shard_map/reduce_sum | solution.py:173
  87.5 0.7 copy.50
  (51 shorter events, 0.4 us)
Async XLA Ops:
  0.6 23.7 %copy-start = (bf16[1,2048,176]{1,2,0:T(8,128)(2,1)S(1)}, bf16[1,2048,176]{1,2,0:T(8,128)(2,1)}, u32[]{:S(2)}) copy-start(bf16[1,2048,176]{1,2,0:T(8,128)(2,1)} %param.18) | copy-start | bytes 2162692
  0.6 41.4 %collective-permute-start = (bf16[1,8,37984]{2,1,0:T(8,128)(2,1)}, bf16[1,8,37984]{2,1,0:T(8,128)(2,1)S(1)}, u32[]{:S(2)}, u32[]{:S(2)}) collective-permute-start(bf16[1,8,37984]{2,1,0:T(8,128)(2,1)} %param.22), channel_id=1, source_target_pairs={{0,4},{4,8},{8,12},{12,16},{16,20},{20,24},{24,28},{28,0},{1,5},{5... | collective-permute-start | bytes 1823240 | tf_op jit(solution)/shard_map/ppermute | solution.py:23
  4.8 5.6 %copy-start.8 = (s32[128,4]{0,1:T(4,128)S(1)}, s32[128,4]{0,1:T(4,128)}, u32[]{:S(2)}) copy-start(s32[128,4]{0,1:T(4,128)} %param.16) | copy-start | bytes 6148
  7.0 12.3 %all-to-all-start = ((bf16[4,2,16,2048]{3,2,1,0:T(8,128)(2,1)}), bf16[4,2,16,2048]{3,2,1,0:T(8,128)(2,1)S(1)}, u32[]{:S(2)}, u32[]{:S(2)}) async-start(bf16[4,2,16,2048]{3,2,1,0:T(8,128)(2,1)} %broadcast_in_dim.63), calls=%async_computation | async-start | bytes 1048576 | tf_op jit(solution)/shard_map/all_to_all | solution.py:140
  10.7 3.9 %copy-start.1 = (bf16[1,8,37984]{2,1,0:T(8,128)(2,1)S(1)}, bf16[1,8,37984]{2,1,0:T(8,128)(2,1)}, u32[]{:S(2)}) copy-start(bf16[1,8,37984]{2,1,0:T(8,128)(2,1)} %param.21) | copy-start | bytes 1823236
  10.7 4.3 %copy-start.11 = (u32[32]{0:T(128)S(1)}, u32[32]{0:T(128)}, u32[]{:S(2)}) copy-start(u32[32]{0:T(128)} %constant.107) | copy-start | bytes 388
  10.7 5.7 %copy-start.9 = (f32[128,4]{0,1:T(4,128)S(1)}, f32[128,4]{0,1:T(4,128)}, u32[]{:S(2)}) copy-start(f32[128,4]{0,1:T(4,128)} %param.17) | copy-start | bytes 6148
  14.2 3.3 %copy-start.5 = (bf16[128,2048]{1,0:T(8,128)(2,1)S(1)}, bf16[128,2048]{1,0:T(8,128)(2,1)}, u32[]{:S(2)}) copy-start(bf16[128,2048]{1,0:T(8,128)(2,1)} %param.15) | copy-start | bytes 1572868
  20.1 4.7 %copy-start.3 = (bf16[1,2048,176]{1,2,0:T(8,128)(2,1)S(1)}, bf16[1,2048,176]{1,2,0:T(8,128)(2,1)}, u32[]{:S(2)}) copy-start(bf16[1,2048,176]{1,2,0:T(8,128)(2,1)} %param.19) | copy-start | bytes 2162692
  20.1 13.1 %all-to-all-start.2 = ((bf16[4,2,16,2048]{3,2,1,0:T(8,128)(2,1)}), bf16[4,2,16,2048]{3,2,1,0:T(8,128)(2,1)}, u32[]{:S(2)}, u32[]{:S(2)}) async-start(bf16[4,2,16,2048]{3,2,1,0:T(8,128)(2,1)} %broadcast_in_dim.67), calls=%async_computation.2 | async-start | bytes 1048576 | tf_op jit(solution)/shard_map/all_to_all | solution.py:141
  25.8 9.1 %copy-start.6 = (f32[128,176]{0,1:T(8,128)S(1)}, f32[128,176]{0,1:T(8,128)}, u32[]{:S(2)}) copy-start(f32[128,176]{0,1:T(8,128)} %fusion.39) | copy-start | bytes 270340
  36.4 3.6 %copy-start.4 = (bf16[1,176,2048]{2,1,0:T(8,128)(2,1)S(1)}, bf16[1,176,2048]{2,1,0:T(8,128)(2,1)}, u32[]{:S(2)}) copy-start(bf16[1,176,2048]{2,1,0:T(8,128)(2,1)} %param.20) | copy-start | bytes 2162692
  36.4 16.9 %all-to-all-start.3 = ((bf16[4,2,16,2048]{3,2,1,0:T(8,128)(2,1)}), bf16[4,2,16,2048]{3,2,1,0:T(8,128)(2,1)S(1)}, u32[]{:S(2)}, u32[]{:S(2)}) async-start(bf16[4,2,16,2048]{3,2,1,0:T(8,128)(2,1)} %bitcast.19), calls=%async_computation.3 | async-start | bytes 1048576 | tf_op jit(solution)/shard_map/all_to_all | solution.py:150
  40.0 2.6 %copy-start.10 = (s32[1,8]{1,0:T(1,128)S(1)}, s32[1,8]{1,0:T(1,128)}, u32[]{:S(2)}) copy-start(s32[1,8]{1,0:T(1,128)} %param.23) | copy-start | bytes 100
  53.2 14.0 %all-to-all-start.1 = ((bf16[4,2,16,2048]{3,2,1,0:T(8,128)(2,1)}), bf16[4,2,16,2048]{3,2,1,0:T(8,128)(2,1)S(1)}, u32[]{:S(2)}, u32[]{:S(2)}) async-start(bf16[4,2,16,2048]{3,2,1,0:T(8,128)(2,1)} %bitcast.128), calls=%async_computation.1 | async-start | bytes 1048576 | tf_op jit(solution)/shard_map/all_to_all | solution.py:149
  70.9 5.3 %copy-start.2 = (f32[128,2048]{1,0:T(8,128)S(1)}, f32[128,2048]{1,0:T(8,128)}, u32[]{:S(2)}) copy-start(f32[128,2048]{1,0:T(8,128)} %convert_element_type.89) | copy-start | bytes 3145732
  70.9 5.3 %copy-start.7 = (f32[128,4]{1,0:T(8,128)S(1)}, f32[128,4]{1,0:T(8,128)}, u32[]{:S(2)}) copy-start(f32[128,4]{1,0:T(8,128)} %copy.40) | copy-start | bytes 6148
where the time goes:
time: 88.8 us; the launch traced here: 88.1 us
  local copies, waits for them, and re-layouts  27.1 us (31%)
  other arithmetic  18.1 us (20%)
  starting transfers between devices  18 us (20%)
  matrix products  8.18 us (9%)
  waiting for transfers between devices  7.67 us (9%)
  blocking collectives  7.33 us (8%)
  between operations  1.6 us (2%)
    reduce_sum x1, other arithmetic, body(): jnp.sum(cotangent.astype(jnp.float32)[:, None, :] * out_rows, axis=2)  11.4 us
    gather x2, local copies, waits for them, and re-layouts, body(): jnp.take(expert_out.reshape(-1, model_width), flat_index, axis=0)  8.83 us
    gather x2, local copies, waits for them, and re-layouts, body(): jnp.take(expert_grad.reshape(-1, model_width), flat_index, axis=0)  8.79 us
    all_to_all x1, waiting for transfers between devices, body(): lax.all_to_all(send_scaled, 'grp', split_axis=0, concat_axis=0, tiled=True)  7.41 us
    unnamed x1, blocking collectives  7.33 us
    all_to_all x1, starting transfers between devices, body(): lax.all_to_all(send_scaled, 'grp', split_axis=0, concat_axis=0, tiled=True)  4.26 us
    gather x5, local copies, waits for them, and re-layouts, body(): slot_index = jnp.take_along_axis(position, safe_ids, axis=1)  3.81 us
    all_to_all x1, starting transfers between devices, body(): lax.all_to_all(piece_out, 'grp', split_axis=0, concat_axis=0, tiled=True)  3.65 us
  transfers between devices with their start and end apart: 5, of which 2 were waited for; matrix products, arithmetic and copies ran while one was open for 37% of the time, Pallas kernels for 0%

commit v1 on v0

v1 whole, which is shorter than its diff:
```python
import functools

import jax
import jax.numpy as jnp
from jax import lax
from jax.experimental import pallas as pl
from jax.experimental.pallas import tpu as pltpu
from jax.sharding import PartitionSpec as P

PIECES = 4
CAP = 32
LANES = 128
CHUNK = 2048
NT = (((1,), (1,)), ((), ()))
TN = (((0,), (0,)), ((), ()))


def vmem(count):
    return [pl.BlockSpec(memory_space=pltpu.VMEM)] * count


def params(mib):
    return pltpu.CompilerParams(vmem_limit_bytes=mib * 1024 * 1024)


def swapped(value, axis, bits):
    count = lax.axis_size(axis)
    return lax.ppermute(value, axis, [(k, k ^ bits) for k in range(count)])


def onward(value, axis):
    count = lax.axis_size(axis)
    return lax.ppermute(value, axis, [(k, (k + 1) % count) for k in range(count)])


def prepare_kernel(n_window, ids, prob, tokens, cot, rows, scaled, slot_cot, select, slot_prob):
    all_ids = ids[...]
    count = all_ids.shape[1]
    before = (
        lax.broadcasted_iota(jnp.int32, (count, count), 0)
        < lax.broadcasted_iota(jnp.int32, (count, count), 1)
    ).astype(jnp.float32).astype(jnp.bfloat16)
    slot = lax.broadcasted_iota(jnp.int32, (CAP, count), 0)
    for e in range(n_window):
        part = pl.ds(e * CAP, CAP)
        hit = all_ids == e
        member = jnp.sum(hit.astype(jnp.float32), axis=0, keepdims=True)
        token_prob = jnp.sum(jnp.where(hit, prob[...], 0.0), axis=0, keepdims=True)
        earlier = jnp.dot(
            jnp.broadcast_to(member, (16, count)).astype(jnp.bfloat16),
            before,
            preferred_element_type=jnp.float32,
        )
        position = earlier[:1].astype(jnp.int32)
        chosen = (slot == position) & (member > 0.5)
        chosen_f = chosen.astype(jnp.float32)
        chosen_b = chosen_f.astype(jnp.bfloat16)
        weight = jnp.sum(chosen_f * token_prob, axis=1, keepdims=True)
        rows[part, :] = jnp.dot(
            chosen_b, tokens[...], preferred_element_type=jnp.float32
        ).astype(jnp.bfloat16)
        cot_rows = jnp.dot(chosen_b, cot[...], preferred_element_type=jnp.float32)
        slot_cot[part, :] = cot_rows.astype(jnp.bfloat16)
        scaled[part, :] = (weight * cot_rows).astype(jnp.bfloat16)
        select[part, :] = chosen_f
        slot_prob[part, :] = jnp.broadcast_to(weight, (CAP, LANES))


def prepare(ids, prob, tokens, cot, n_window):
    count, width = tokens.shape
    slots = n_window * CAP
    wide = jax.ShapeDtypeStruct((slots, width), jnp.bfloat16)
    return pl.pallas_call(
        functools.partial(prepare_kernel, n_window),
        out_shape=(
            wide,
            wide,
            wide,
            jax.ShapeDtypeStruct((slots, count), jnp.float32),
            jax.ShapeDtypeStruct((slots, LANES), jnp.float32),
        ),
        in_specs=vmem(4),
        out_specs=tuple(vmem(5)),
        compiler_params=params(8),
        name="prepare",
    )(ids, prob, tokens, cot)


def piece_kernel(rows_a, rows_b, scaled_a, scaled_b, gate_w, up_w, down_w, out_a, grad_a, send):
    half = rows_a.shape[0]
    rows = jnp.concatenate([rows_a[...], rows_b[...]], axis=0)
    gate = lax.dot_general(rows, gate_w[...], NT, preferred_element_type=jnp.float32)
    up = lax.dot_general(rows, up_w[...], NT, preferred_element_type=jnp.float32)
    sig = jax.nn.sigmoid(gate)
    hidden = (gate * sig * up).astype(jnp.bfloat16)
    out = jnp.dot(hidden, down_w[...], preferred_element_type=jnp.float32).astype(jnp.bfloat16)
    out_a[...] = out[:half]
    send[:half, :] = out[half:]
    scaled = jnp.concatenate([scaled_a[...], scaled_b[...]], axis=0)
    grad_hidden = lax.dot_general(scaled, down_w[...], NT, preferred_element_type=jnp.float32)
    grad_gate = (grad_hidden * up * sig * (1.0 + gate * (1.0 - sig))).astype(jnp.bfloat16)
    grad_up = (grad_hidden * gate * sig).astype(jnp.bfloat16)
    grad = jnp.dot(grad_gate, gate_w[...], preferred_element_type=jnp.float32)
    grad = grad + jnp.dot(grad_up, up_w[...], preferred_element_type=jnp.float32)
    grad = grad.astype(jnp.bfloat16)
    grad_a[...] = grad[:half]
    send[half:, :] = grad[half:]


def piece(rows_a, rows_b, scaled_a, scaled_b, gate_w, up_w, down_w):
    half, width = rows_a.shape
    return pl.pallas_call(
        piece_kernel,
        out_shape=(
            jax.ShapeDtypeStruct((half, width), jnp.bfloat16),
            jax.ShapeDtypeStruct((half, width), jnp.bfloat16),
            jax.ShapeDtypeStruct((2 * half, width), jnp.bfloat16),
        ),
        in_specs=vmem(7),
        out_specs=tuple(vmem(3)),
        compiler_params=params(16),
        name="piece",
    )(rows_a, rows_b, scaled_a, scaled_b, gate_w, up_w, down_w)


def spread(select, value, exact):
    high = value.astype(jnp.bfloat16)
    chosen = select.astype(jnp.bfloat16)
    total = lax.dot_general(chosen, high, TN, preferred_element_type=jnp.float32)
    if exact:
        return total
    low = (value - high.astype(jnp.float32)).astype(jnp.bfloat16)
    return total + lax.dot_general(chosen, low, TN, preferred_element_type=jnp.float32)


def combine_kernel(n_window, parts, *refs):
    outs, grads = refs[:parts], refs[parts : 2 * parts]
    ids, select, slot_prob, slot_cot, layer_out, input_grad, prob_grad = refs[2 * parts :]
    exact = n_window == 1
    out = outs[0][...].astype(jnp.float32)
    for other in outs[1:]:
        out = out + other[...].astype(jnp.float32)
    chosen = select[...]
    per_slot = jnp.sum(out * slot_cot[...].astype(jnp.float32), axis=1, keepdims=True)
    spread_prob = chosen * per_slot
    for e in range(n_window):
        per_token = jnp.sum(spread_prob[e * CAP : (e + 1) * CAP], axis=0, keepdims=True)
        kept = jnp.where(ids[...] == e, per_token, 0.0)
        whole = kept if e == 0 else whole + kept
    prob_grad[...] = whole
    weighted = slot_prob[:, :1] * out
    layer_out[...] = spread(chosen, weighted, exact).astype(jnp.bfloat16)
    grad = grads[0][...].astype(jnp.float32)
    for other in grads[1:]:
        grad = grad + other[...].astype(jnp.float32)
    input_grad[...] = spread(chosen, grad, exact).astype(jnp.bfloat16)


def combine(outs, grads, ids, select, slot_prob, slot_cot, n_window):
    parts = len(outs)
    width = outs[0].shape[1]
    topk, count = ids.shape
    return pl.pallas_call(
        functools.partial(combine_kernel, n_window, parts),
        out_shape=(
            jax.ShapeDtypeStruct((count, width), jnp.bfloat16),
            jax.ShapeDtypeStruct((count, width), jnp.bfloat16),
            jax.ShapeDtypeStruct((topk, count), jnp.float32),
        ),
        in_specs=vmem(2 * parts + 4),
        out_specs=tuple(vmem(3)),
        compiler_params=params(12),
        name="combine",
    )(*outs, *grads, ids, select, slot_prob, slot_cot)


def pieces_of(width):
    full = width // CHUNK
    return full, full * CHUNK, width - full * CHUNK


def over_columns(width, carry, step):
    full, start, rest = pieces_of(width)

    def lap(k, so_far):
        return step(pl.multiple_of(k * CHUNK, CHUNK), CHUNK, so_far)

    if full:
        carry = lax.fori_loop(0, full, lap, carry, unroll=True)
    return carry, start, rest


def row_max(ref, width):
    rows = ref.shape[0]

    def step(at, size, so_far):
        return jnp.maximum(so_far, ref[:, pl.ds(at, size)].astype(jnp.float32))

    top, start, rest = over_columns(
        width, jnp.full((rows, CHUNK), -jnp.inf, jnp.float32), step
    )
    top = jnp.max(top, axis=1, keepdims=True)
    if rest:
        tail = ref[:, start : start + rest].astype(jnp.float32)
        top = jnp.maximum(top, jnp.max(tail, axis=1, keepdims=True))
    return top


def columns(values, rows):
    lane = lax.broadcasted_iota(jnp.int32, (rows, LANES), 1)
    tile = jnp.zeros((rows, LANES), jnp.float32)
    for k, value in enumerate(values):
        tile = jnp.where(lane == k, value, tile)
    return tile


def label_column(labels, base):
    rows = labels.shape[1]
    own = lax.broadcasted_iota(jnp.int32, (rows, rows), 0) == lax.broadcasted_iota(
        jnp.int32, (rows, rows), 1
    )
    spread_out = jnp.where(own, jnp.broadcast_to(labels[...], (rows, rows)), 0)
    return jnp.sum(spread_out.astype(jnp.float32), axis=1, keepdims=True).astype(jnp.int32) - base


def student_kernel(base, labels, student, stats):
    rows, width = student.shape
    top = row_max(student, width)
    label = label_column(labels, base[0])

    def step(at, size, so_far):
        total, picked = so_far
        value = student[:, pl.ds(at, size)].astype(jnp.float32)
        here = lax.broadcasted_iota(jnp.int32, (rows, size), 1) == label - at
        return total + jnp.exp(value - top), picked + jnp.where(here, value, 0.0)

    zero = jnp.zeros((rows, CHUNK), jnp.float32)
    (total, picked), start, rest = over_columns(width, (zero, zero), step)
    total = jnp.sum(total, axis=1, keepdims=True)
    picked = jnp.sum(picked, axis=1, keepdims=True)
    if rest:
        none = jnp.zeros((rows, rest), jnp.float32)
        more, seen = step(start, rest, (none, none))
        total = total + jnp.sum(more, axis=1, keepdims=True)
        picked = picked + jnp.sum(seen, axis=1, keepdims=True)
    stats[...] = columns((top, total, picked), rows)


def teacher_kernel(student, teacher, student_stats, stats):
    rows, width = student.shape
    top = row_max(teacher, width)

    def step(at, size, so_far):
        total, cross = so_far
        ours = student[:, pl.ds(at, size)].astype(jnp.float32)
        theirs = teacher[:, pl.ds(at, size)].astype(jnp.float32)
        power = jnp.exp(theirs - top)
        return total + power, cross + power * (theirs - ours)

    zero = jnp.zeros((rows, CHUNK), jnp.float32)
    (total, cross), start, rest = over_columns(width, (zero, zero), step)
    total = jnp.sum(total, axis=1, keepdims=True)
    cross = jnp.sum(cross, axis=1, keepdims=True)
    if rest:
        none = jnp.zeros((rows, rest), jnp.float32)
        more, seen = step(start, rest, (none, none))
        total = total + jnp.sum(more, axis=1, keepdims=True)
        cross = cross + jnp.sum(seen, axis=1, keepdims=True)
    first = student_stats[...]
    stats[...] = columns(
        (first[:, 0:1], first[:, 1:2], first[:, 2:3], top, total, cross), rows
    )


def final_kernel(parts, base, labels, student, teacher, *refs):
    stats, (loss, grad) = refs[:parts], refs[parts:]
    rows, width = student.shape
    label = label_column(labels, base[0])
    tiles = [ref[...] for ref in stats]
    top = functools.reduce(jnp.maximum, tiles)
    smax, tmax = top[:, 0:1], top[:, 3:4]
    ssum = tsum = cross = picked = jnp.zeros((rows, 1), jnp.float32)
    for tile in tiles:
        ssum = ssum + tile[:, 1:2] * jnp.exp(tile[:, 0:1] - smax)
        scale = jnp.exp(tile[:, 3:4] - tmax)
        tsum = tsum + tile[:, 4:5] * scale
        cross = cross + tile[:, 5:6] * scale
        picked = picked + tile[:, 2:3]
    lse_s = smax + jnp.log(ssum)
    lse_t = tmax + jnp.log(tsum)
    value = 2.0 * lse_s - picked + cross / tsum - lse_t
    own = lax.broadcasted_iota(jnp.int32, (rows, rows), 0) == lax.broadcasted_iota(
        jnp.int32, (rows, rows), 1
    )
    loss[...] = jnp.sum(jnp.where(own, value, 0.0), axis=0, keepdims=True)

    def step(at, size, so_far):
        ours = student[:, pl.ds(at, size)].astype(jnp.float32)
        theirs = teacher[:, pl.ds(at, size)].astype(jnp.float32)
        here = lax.broadcasted_iota(jnp.int32, (rows, size), 1) == label - at
        result = (
            2.0 * jnp.exp(ours - lse_s) - here.astype(jnp.float32) - jnp.exp(theirs - lse_t)
        )
        grad[:, pl.ds(at, size)] = result.astype(jnp.bfloat16)
        return so_far

    _, start, rest = over_columns(width, 0, step)
    if rest:
        step(start, rest, 0)


def scalar_spec():
    return pl.BlockSpec(memory_space=pltpu.SMEM)


def distill(student, stale, labels):
    rows, width = student.shape
    teacher = onward(stale, "peer")
    base = (lax.axis_index("grp") * width).astype(jnp.int32).reshape(1)
    tile = jax.ShapeDtypeStruct((rows, LANES), jnp.float32)
    own = pl.pallas_call(
        student_kernel,
        out_shape=tile,
        in_specs=[scalar_spec()] + vmem(2),
        out_specs=vmem(1)[0],
        compiler_params=params(8),
        name="student",
    )(base, labels, student)
    stats = pl.pallas_call(
        teacher_kernel,
        out_shape=tile,
        in_specs=vmem(3),
        out_specs=vmem(1)[0],
        compiler_params=params(8),
        name="teacher",
    )(student, teacher, own)
    count = lax.axis_size("grp")
    others = [
        lax.ppermute(stats, "grp", [(k, (k + s) % count) for k in range(count)])
        for s in range(1, count)
    ]
    loss, grad = pl.pallas_call(
        functools.partial(final_kernel, count),
        out_shape=(
            jax.ShapeDtypeStruct((1, rows), jnp.float32),
            jax.ShapeDtypeStruct((rows, width), jnp.bfloat16),
        ),
        in_specs=[scalar_spec()] + vmem(3 + count),
        out_specs=tuple(vmem(2)),
        compiler_params=params(8),
        name="final",
    )(base, labels, student, teacher, stats, *others)
    return loss, grad


def between_blocks(value, n_window):
    if n_window == 1:
        return value
    groups = [[b + PIECES * a for a in range(n_window)] for b in range(PIECES)]
    return lax.all_to_all(
        value, "grp", split_axis=0, concat_axis=0, tiled=True, axis_index_groups=groups
    )


def layer(tokens, cotangent, ids, prob, gate_w, up_w, down_w, n_window):
    rows, scaled, slot_cot, select, slot_prob = prepare(ids, prob, tokens, cotangent, n_window)
    rows = between_blocks(rows, n_window)
    scaled = between_blocks(scaled, n_window)
    half = rows.shape[0]
    pair = jnp.concatenate([rows, scaled], axis=0)
    far = swapped(pair, "grp", 2)
    near = swapped(pair, "grp", 1)
    far_near = swapped(far, "grp", 1)
    weights = (gate_w, up_w, down_w)
    out_a, grad_a, send_a = piece(rows, near[:half], scaled, near[half:], *weights)
    back_a = swapped(send_a, "grp", 1)
    out_b, grad_b, send_b = piece(far[:half], far_near[:half], far[half:], far_near[half:], *weights)
    back_b = swapped(send_b, "grp", 1)
    keep_b = jnp.concatenate([out_b, grad_b], axis=0)
    sum_b = (keep_b.astype(jnp.float32) + back_b.astype(jnp.float32)).astype(jnp.bfloat16)
    home = swapped(sum_b, "grp", 2)
    outs = [out_a, back_a[:half], home[:half]]
    grads = [grad_a, back_a[half:], home[half:]]
    if n_window > 1:
        total = functools.reduce(jnp.add, [part.astype(jnp.float32) for part in outs])
        outs = [between_blocks(total.astype(jnp.bfloat16), n_window)]
        total = functools.reduce(jnp.add, [part.astype(jnp.float32) for part in grads])
        grads = [between_blocks(total.astype(jnp.bfloat16), n_window)]
    return combine(outs, grads, ids, select, slot_prob, slot_cot, n_window)


def body(
    tokens,
    cotangent,
    expert_ids,
    route_prob,
    w_gate,
    w_up,
    w_down,
    student_logits,
    stale_logits,
    labels,
):
    n_window = lax.axis_size("grp") // PIECES
    distill_loss, logit_grad = distill(student_logits[0], stale_logits[0], labels)
    layer_out, input_grad, prob_grad = layer(
        tokens,
        cotangent,
        expert_ids.T,
        route_prob.T,
        w_gate[0].T,
        w_up[0].T,
        w_down[0],
        n_window,
    )
    return (layer_out, input_grad, prob_grad.T, distill_loss, logit_grad[None])


def solution(mesh):
    placed = (
        P(("peer", "grp"), None),
        P(("peer", "grp"), None),
        P(("peer", "grp"), None),
        P(("peer", "grp"), None),
        P("peer", None, "grp"),
        P("peer", None, "grp"),
        P("peer", "grp", None),
        P("peer", None, "grp"),
        P("peer", None, "grp"),
        P("peer", None),
    )
    return jax.shard_map(
        body,
        mesh=mesh,
        in_specs=placed,
        out_specs=(
            P(("peer", "grp"), None),
            P(("peer", "grp"), None),
            P(("peer", "grp"), None),
            P("peer", None),
            P("peer", None, "grp"),
        ),
        check_vma=False,
    )
```

time: 88.8 us -> 39.5 us (0.44)
  local copies, waits for them, and re-layouts: 27.1 us -> 3.57 us
  other arithmetic: 18.1 us -> 0.06 us
  waiting for transfers between devices: 7.67 us -> 19.4 us
  starting transfers between devices: 18 us -> 7.56 us
  matrix products: 8.18 us -> 0 us
  Pallas kernels: 0 us -> 7.84 us
  blocking collectives: 7.33 us -> 0 us
    gather x9 -> x0, local copies, waits for them, and re-layouts: 21.4 us -> none  [the longest x2 8.83 us: body(): jnp.take(expert_out.reshape(-1, model_width), flat_index, axis=0)]
    ppermute x1 -> x10, waiting for transfers between devices: 0.01 us -> 19.4 us  [the longest x6 10.2 us: swapped(): return lax.ppermute(value, axis, [(k, k ^ bits) for k in range(count)])]
    all_to_all x4 -> x0, starting transfers between devices: 15 us -> none  [the longest x1 4.26 us: body(): lax.all_to_all(send_scaled, 'grp', split_axis=0, concat_axis=0, tiled=True)]
    reduce_sum x6 -> x0, other arithmetic: 13.4 us -> none  [the longest x1 11.4 us: body(): jnp.sum(cotangent.astype(jnp.float32)[:, None, :] * out_rows, axis=2)]
    dot_general x9 -> x0, matrix products: 8.18 us -> none  [the longest x1 2.04 us: forward_piece(): jnp.dot(hidden, down_rows, preferred_element_type=jnp.float32)]
    pallas_call x0 -> x7, Pallas kernels: none -> 7.84 us  [the longest x2 3.38 us: piece(): pl.pallas_call(piece_kernel, out_shape=(jax.ShapeDtypeStruct((half, width...]
    all_to_all x4 -> x0, waiting for transfers between devices: 7.67 us -> none  [the longest x1 7.41 us: body(): lax.all_to_all(send_scaled, 'grp', split_axis=0, concat_axis=0, tiled=True)]
    unnamed x1 -> x0, blocking collectives: 7.33 us -> none
  transfers between devices with their start and end apart: 5 -> 10, of which waited for: 2 -> 6; matrix products, arithmetic and copies ran while one was open for 37% -> 0% of each run, Pallas kernels for 0% -> 16%
where the time goes in v1:
time: 39.5 us; the launch traced here: 39.2 us
  waiting for transfers between devices  19.4 us (49%)
  Pallas kernels  7.84 us (20%)
  starting transfers between devices  7.56 us (19%)
  local copies, waits for them, and re-layouts  3.57 us (9%)
  between operations  0.77 us (2%)
    ppermute x6, waiting for transfers between devices, swapped(): return lax.ppermute(value, axis, [(k, k ^ bits) for k in range(count)])  10.2 us
    ppermute x1, waiting for transfers between devices, onward(): lax.ppermute(value, axis, [(k, (k + 1) % count) for k in range(count)])  7.21 us
    ppermute x6, starting transfers between devices, swapped(): return lax.ppermute(value, axis, [(k, k ^ bits) for k in range(count)])  4.59 us
    unnamed x19, local copies, waits for them, and re-layouts  3.47 us
    pallas_call x2, Pallas kernels, piece(): pl.pallas_call(piece_kernel, out_shape=(jax.ShapeDtypeStruct((half, width...  3.38 us
    ppermute x3, waiting for transfers between devices, distill(): lax.ppermute(stats, 'grp', [(k, (k + s) % count) for k in range(count)])  2.01 us
    pallas_call x1, Pallas kernels, distill(): pl.pallas_call(functools.partial(final_kernel, count), out_shape=(jax.Sha...  1.63 us
    ppermute x1, starting transfers between devices, onward(): lax.ppermute(value, axis, [(k, (k + 1) % count) for k in range(count)])  1.52 us
  transfers between devices with their start and end apart: 10, of which 6 were waited for; matrix products, arithmetic and copies ran while one was open for 0% of the time, Pallas kernels for 16%

profile of v1, /device:TPU:0, one launch (start us, length us, event | category | flops | bytes accessed | tf_op | source)
XLA Modules:
  0.0 39.2 jit_solution(253611199652387351)
XLA Ops:
  0.6 0.0 copy-start.6
  0.6 0.7 %copy-done.6 = s32[128,4]{0,1:T(4,128)S(1)} copy-done((s32[128,4]{0,1:T(4,128)S(1)}, s32[128,4]{0,1:T(4,128)}, u32[]{:S(2)}) %copy-start.6) | copy-done | bytes 2072
  1.3 0.0 copy-start.4
  1.3 1.0 %copy-done.4 = bf16[128,2048]{1,0:T(8,128)(2,1)S(1)} copy-done((bf16[128,2048]{1,0:T(8,128)(2,1)S(1)}, bf16[128,2048]{1,0:T(8,128)(2,1)}, u32[]{:S(2)}) %copy-start.4) | copy-done | bytes 524312
  2.4 0.0 copy-start.5
  2.4 1.0 %copy-done.5 = bf16[128,2048]{1,0:T(8,128)(2,1)S(1)} copy-done((bf16[128,2048]{1,0:T(8,128)(2,1)S(1)}, bf16[128,2048]{1,0:T(8,128)(2,1)}, u32[]{:S(2)}) %copy-start.5) | copy-done | bytes 524312
  3.4 0.0 copy-start.7
  3.4 0.7 %copy-done.7 = f32[128,4]{0,1:T(4,128)S(1)} copy-done((f32[128,4]{0,1:T(4,128)S(1)}, f32[128,4]{0,1:T(4,128)}, u32[]{:S(2)}) %copy-start.7) | copy-done | bytes 2072
  4.1 0.0 copy-start
  4.1 0.0 copy-start.8
  4.1 0.4 %prepare.1 = (bf16[32,2048]{1,0:T(8,128)(2,1)S(1)}, bf16[32,2048]{1,0:T(8,128)(2,1)S(1)}, bf16[32,2048]{1,0:T(8,128)(2,1)S(1)}, f32[32,128]{1,0:T(8,128)S(1)}, f32[32,128]{1,0:T(8,128)S(1)}) custom-call(s32[4,128]{1,0:T(4,128)S(1)} %bitcast.23, f32[4,128]{1,0:T(4,128)S(1)} %bitcast.25, bf16[128,2048]{1,0:T(8,128)(2,1)S(1)} %copy-done.4, ...), custom_call_target="tpu_custom_call" | custom-call | tf_op jit(solution)/shard_map/prepare/pallas_call | solution.py:73
  4.5 0.0 copy-start.3
  4.5 3.0 %collective-permute-start.2 = (bf16[64,2048]{1,0:T(8,128)(2,1)S(1)}, bf16[64,2048]{1,0:T(8,128)(2,1)S(1)}, u32[]{:S(2)}, u32[]{:S(2)}) collective-permute-start(bf16[64,2048]{1,0:T(8,128)(2,1)S(1)} %constant_dynamic-update-slice_fusion), channel_id=1, source_target_pairs={{0,2},{1,3},{2,0},{3,1},{4,6},{5,7},{6,4},{7,5},{8,10},{9,11},{10,... | collective-permute-start | bytes 786440 | tf_op jit(solution)/shard_map/ppermute | solution.py:28
  7.6 0.0 collective-permute-start
  7.6 1.5 %collective-permute-start.6 = (bf16[8,37984]{1,0:T(8,128)(2,1)}, bf16[8,37984]{1,0:T(8,128)(2,1)S(1)}, u32[]{:S(2)}, u32[]{:S(2)}) collective-permute-start(bf16[8,37984]{1,0:T(8,128)(2,1)} %bitcast.26), channel_id=1, source_target_pairs={{0,4},{4,8},{8,12},{12,16},{16,20},{20,24},{24,28},{28,0},{1,5},{5... | collective-permute-start | bytes 1823240 | tf_op jit(solution)/shard_map/ppermute | solution.py:33
  9.1 0.0 copy-done
  9.1 0.0 copy-done.8
  9.1 0.0 copy-start.1
  9.1 0.0 copy-start.2
  9.1 0.6 %student.1.student_stats = f32[8,128]{1,0:T(8,128)S(1)} custom-call(s32[1]{0:T(128)} %bitcast.10.base, s32[1,8]{1,0:T(1,128)S(1)} %copy-done.8, bf16[8,37984]{1,0:T(8,128)(2,1)S(1)} %bitcast.14), custom_call_target="tpu_custom_call" | custom-call | tf_op jit(solution)/shard_map/student/pallas_call | solution.py:321
  9.7 4.2 %collective-permute-done.2 = bf16[64,2048]{1,0:T(8,128)(2,1)S(1)} collective-permute-done((bf16[64,2048]{1,0:T(8,128)(2,1)S(1)}, bf16[64,2048]{1,0:T(8,128)(2,1)S(1)}, u32[]{:S(2)}, u32[]{:S(2)}) %collective-permute-start.2) | collective-permute-done | bytes 262176 | tf_op jit(solution)/shard_map/ppermute | solution.py:28
  13.9 0.0 collective-permute-start.3
  13.9 1.5 %collective-permute-done.3 = bf16[64,2048]{1,0:T(8,128)(2,1)S(1)} collective-permute-done((bf16[64,2048]{1,0:T(8,128)(2,1)S(1)}, bf16[64,2048]{1,0:T(8,128)(2,1)S(1)}, u32[]{:S(2)}, u32[]{:S(2)}) %collective-permute-start.3) | collective-permute-done | bytes 262176 | tf_op jit(solution)/shard_map/ppermute | solution.py:28
  15.4 0.0 copy-done.3
  15.4 0.0 copy-done.1
  15.5 0.0 copy-done.2
  15.5 1.7 %piece.3 = (bf16[32,2048]{1,0:T(8,128)(2,1)S(1)}, bf16[32,2048]{1,0:T(8,128)(2,1)S(1)}, bf16[64,2048]{1,0:T(8,128)(2,1)S(1)}) custom-call(bf16[32,2048]{1,0:T(8,128)(2,1)S(1)} %get-tuple-element.44.rows_a, bf16[32,2048]{1,0:T(8,128)(2,1)S(1)} %get-tuple-element.42.rows_b, bf16[32,2048]{1,0:T(8,128)(2,1)S(1)} %get-tuple-element.43.scaled_a, ...), custom_call_target="tpu_custom_call" | custom-call | tf_op jit(solution)/shard_map/piece/pallas_call | solution.py:112
  17.2 0.2 collective-permute-start.4
  17.4 0.0 collective-permute-done
  17.4 1.7 %piece.2 = (bf16[32,2048]{1,0:T(8,128)(2,1)S(1)}, bf16[32,2048]{1,0:T(8,128)(2,1)S(1)}, bf16[64,2048]{1,0:T(8,128)(2,1)S(1)}) custom-call(bf16[32,2048]{1,0:T(8,128)(2,1)S(1)} %get-tuple-element.21.rows_a, bf16[32,2048]{1,0:T(8,128)(2,1)S(1)} %get-tuple-element.46.rows_b, bf16[32,2048]{1,0:T(8,128)(2,1)S(1)} %get-tuple-element.22.scaled_a, ...), custom_call_target="tpu_custom_call" | custom-call | tf_op jit(solution)/shard_map/piece/pallas_call | solution.py:112
  19.1 0.4 %collective-permute-start.1 = (bf16[64,2048]{1,0:T(8,128)(2,1)S(1)}, bf16[64,2048]{1,0:T(8,128)(2,1)S(1)}, u32[]{:S(2)}, u32[]{:S(2)}) collective-permute-start(bf16[64,2048]{1,0:T(8,128)(2,1)S(1)} %get-tuple-element.24), channel_id=1, source_target_pairs={{0,1},{1,0},{2,3},{3,2},{4,5},{5,4},{6,7},{7,6},{8,9},{9,8},{10,11... | collective-permute-start | bytes 786440 | tf_op jit(solution)/shard_map/ppermute | solution.py:28
  19.5 7.2 %collective-permute-done.6.teacher = bf16[8,37984]{1,0:T(8,128)(2,1)S(1)} collective-permute-done((bf16[8,37984]{1,0:T(8,128)(2,1)}, bf16[8,37984]{1,0:T(8,128)(2,1)S(1)}, u32[]{:S(2)}, u32[]{:S(2)}) %collective-permute-start.6) | collective-permute-done | bytes 607776 | tf_op jit(solution)/shard_map/ppermute | solution.py:33
  26.7 0.5 %teacher.1.refs_0_ = f32[8,128]{1,0:T(8,128)S(1)} custom-call(bf16[8,37984]{1,0:T(8,128)(2,1)S(1)} %bitcast.15, bf16[8,37984]{1,0:T(8,128)(2,1)S(1)} %collective-permute-done.6.teacher, f32[8,128]{1,0:T(8,128)S(1)} %student.1.student_stats), custom_call_target="tpu_custom_call" | custom-call | tf_op jit(solution)/shard_map/teacher/pallas_call | solution.py:329
  27.3 0.1 collective-permute-start.9
  27.4 1.3 %collective-permute-start.8 = (f32[8,128]{1,0:T(8,128)S(1)}, f32[8,128]{1,0:T(8,128)S(1)}, u32[]{:S(2)}, u32[]{:S(2)}) collective-permute-start(f32[8,128]{1,0:T(8,128)S(1)} %teacher.1.refs_0_), channel_id=1, source_target_pairs={{0,2},{1,3},{2,0},{3,1},{4,6},{5,7},{6,4},{7,5},{8,10},{9,11},{10,... | collective-permute-start | bytes 12296 | tf_op jit(solution)/shard_map/ppermute | solution.py:339
  28.7 0.0 collective-permute-start.7
  28.7 0.0 collective-permute-done.4
  28.7 0.1 add_convert_fusion
  28.8 0.9 %collective-permute-start.5 = (bf16[64,2048]{1,0:T(8,128)(2,1)S(1)}, bf16[64,2048]{1,0:T(8,128)(2,1)S(1)}, u32[]{:S(2)}, u32[]{:S(2)}) collective-permute-start(bf16[64,2048]{1,0:T(8,128)(2,1)S(1)} %add_convert_fusion), channel_id=1, source_target_pairs={{0,2},{1,3},{2,0},{3,1},{4,6},{5,7},{6,4},{7,5},{8,10},{9,11},{10,... | collective-permute-start | bytes 786440 | tf_op jit(solution)/shard_map/ppermute | solution.py:28
  29.7 0.0 collective-permute-done.1
  29.7 0.0 collective-permute-done.9.refs_3_
  29.7 1.2 %collective-permute-done.8.refs_2_ = f32[8,128]{1,0:T(8,128)S(1)} collective-permute-done((f32[8,128]{1,0:T(8,128)S(1)}, f32[8,128]{1,0:T(8,128)S(1)}, u32[]{:S(2)}, u32[]{:S(2)}) %collective-permute-start.8) | collective-permute-done | bytes 4128 | tf_op jit(solution)/shard_map/ppermute | solution.py:339
  31.0 0.8 %collective-permute-done.7.refs_1_ = f32[8,128]{1,0:T(8,128)S(1)} collective-permute-done((f32[8,128]{1,0:T(8,128)S(1)}, f32[8,128]{1,0:T(8,128)S(1)}, u32[]{:S(2)}, u32[]{:S(2)}) %collective-permute-start.7) | collective-permute-done | bytes 4128 | tf_op jit(solution)/shard_map/ppermute | solution.py:339
  31.7 1.6 %final.1 = (f32[1,8]{1,0:T(1,128)}, bf16[8,37984]{1,0:T(8,128)(2,1)}) custom-call(s32[1]{0:T(128)} %bitcast.10.base, s32[1,8]{1,0:T(1,128)S(1)} %copy-done.8, bf16[8,37984]{1,0:T(8,128)(2,1)S(1)} %bitcast.16, bf16[8,37984]{1,0:T(8,128)(2,1)S(1)} %collective-permute-done.6.teacher, f32[8,128]{1,0:T(8,128)S(1)} %teacher.1.refs_0_, ...), custom_call_target="tpu_custom_call" | custom-call | tf_op jit(solution)/shard_map/final/pallas_call | solution.py:342
  33.4 4.5 %collective-permute-done.5 = bf16[64,2048]{1,0:T(8,128)(2,1)S(1)} collective-permute-done((bf16[64,2048]{1,0:T(8,128)(2,1)S(1)}, bf16[64,2048]{1,0:T(8,128)(2,1)S(1)}, u32[]{:S(2)}, u32[]{:S(2)}) %collective-permute-start.5) | collective-permute-done | bytes 262176 | tf_op jit(solution)/shard_map/ppermute | solution.py:28
  37.9 1.3 %combine.1 = (bf16[128,2048]{1,0:T(8,128)(2,1)}, bf16[128,2048]{1,0:T(8,128)(2,1)}, f32[4,128]{1,0:T(4,128)}) custom-call(bf16[32,2048]{1,0:T(8,128)(2,1)S(1)} %get-tuple-element.23.refs_0_, bf16[32,2048]{1,0:T(8,128)(2,1)S(1)} %get-tuple-element.40.refs_1_, bf16[32,2048]{1,0:T(8,128)(2,1)S(1)} %get-tuple-element.38.refs_2_, ...), custom_call_target="tpu_custom_call" | custom-call | tf_op jit(solution)/shard_map/combine/pallas_call | solution.py:163
  (7 shorter events, 0.1 us)
Async XLA Ops:
  0.6 0.7 %copy-start.6 = (s32[128,4]{0,1:T(4,128)S(1)}, s32[128,4]{0,1:T(4,128)}, u32[]{:S(2)}) copy-start(s32[128,4]{0,1:T(4,128)} %param.12) | copy-start | bytes 6148
  1.3 1.0 %copy-start.4 = (bf16[128,2048]{1,0:T(8,128)(2,1)S(1)}, bf16[128,2048]{1,0:T(8,128)(2,1)}, u32[]{:S(2)}) copy-start(bf16[128,2048]{1,0:T(8,128)(2,1)} %tokens.1) | copy-start | bytes 1572868
  2.4 1.0 %copy-start.5 = (bf16[128,2048]{1,0:T(8,128)(2,1)S(1)}, bf16[128,2048]{1,0:T(8,128)(2,1)}, u32[]{:S(2)}) copy-start(bf16[128,2048]{1,0:T(8,128)(2,1)} %cot.1) | copy-start | bytes 1572868
  3.4 0.7 %copy-start.7 = (f32[128,4]{0,1:T(4,128)S(1)}, f32[128,4]{0,1:T(4,128)}, u32[]{:S(2)}) copy-start(f32[128,4]{0,1:T(4,128)} %param.13) | copy-start | bytes 6148
  4.1 5.0 %copy-start = (bf16[1,8,37984]{2,1,0:T(8,128)(2,1)S(1)}, bf16[1,8,37984]{2,1,0:T(8,128)(2,1)}, u32[]{:S(2)}) copy-start(bf16[1,8,37984]{2,1,0:T(8,128)(2,1)} %param.17) | copy-start | bytes 1823236
  4.1 5.0 %copy-start.8 = (s32[1,8]{1,0:T(1,128)S(1)}, s32[1,8]{1,0:T(1,128)}, u32[]{:S(2)}) copy-start(s32[1,8]{1,0:T(1,128)} %labels.3) | copy-start | bytes 100
  4.5 10.9 %copy-start.3 = (bf16[1,176,2048]{2,1,0:T(8,128)(2,1)S(1)}, bf16[1,176,2048]{2,1,0:T(8,128)(2,1)}, u32[]{:S(2)}) copy-start(bf16[1,176,2048]{2,1,0:T(8,128)(2,1)} %param.16) | copy-start | bytes 2162692
  4.5 9.3 %collective-permute-start.2 = (bf16[64,2048]{1,0:T(8,128)(2,1)S(1)}, bf16[64,2048]{1,0:T(8,128)(2,1)S(1)}, u32[]{:S(2)}, u32[]{:S(2)}) collective-permute-start(bf16[64,2048]{1,0:T(8,128)(2,1)S(1)} %constant_dynamic-update-slice_fusion), channel_id=1, source_target_pairs={{0,2},{1,3},{2,0},{3,1},{4,6},{5,7},{6,4},{7,5},{8,10},{9,11},{10,... | collective-permute-start | bytes 786440 | tf_op jit(solution)/shard_map/ppermute | solution.py:28
  7.6 9.8 %collective-permute-start = (bf16[64,2048]{1,0:T(8,128)(2,1)S(1)}, bf16[64,2048]{1,0:T(8,128)(2,1)S(1)}, u32[]{:S(2)}, u32[]{:S(2)}) collective-permute-start(bf16[64,2048]{1,0:T(8,128)(2,1)S(1)} %constant_dynamic-update-slice_fusion), channel_id=1, source_target_pairs={{0,1},{1,0},{2,3},{3,2},{4,5},{5,4},{6,7},{7,6},{8,9},{9,8},{10,11... | collective-permute-start | bytes 786440 | tf_op jit(solution)/shard_map/ppermute | solution.py:28
  7.6 19.2 %collective-permute-start.6 = (bf16[8,37984]{1,0:T(8,128)(2,1)}, bf16[8,37984]{1,0:T(8,128)(2,1)S(1)}, u32[]{:S(2)}, u32[]{:S(2)}) collective-permute-start(bf16[8,37984]{1,0:T(8,128)(2,1)} %bitcast.26), channel_id=1, source_target_pairs={{0,4},{4,8},{8,12},{12,16},{16,20},{20,24},{24,28},{28,0},{1,5},{5... | collective-permute-start | bytes 1823240 | tf_op jit(solution)/shard_map/ppermute | solution.py:33
  9.1 6.3 %copy-start.1 = (bf16[1,2048,176]{1,2,0:T(8,128)(2,1)S(1)}, bf16[1,2048,176]{1,2,0:T(8,128)(2,1)}, u32[]{:S(2)}) copy-start(bf16[1,2048,176]{1,2,0:T(8,128)(2,1)} %param.14) | copy-start | bytes 2162692
  9.1 6.4 %copy-start.2 = (bf16[1,2048,176]{1,2,0:T(8,128)(2,1)S(1)}, bf16[1,2048,176]{1,2,0:T(8,128)(2,1)}, u32[]{:S(2)}) copy-start(bf16[1,2048,176]{1,2,0:T(8,128)(2,1)} %param.15) | copy-start | bytes 2162692
  13.9 1.5 %collective-permute-start.3 = (bf16[64,2048]{1,0:T(8,128)(2,1)S(1)}, bf16[64,2048]{1,0:T(8,128)(2,1)S(1)}, u32[]{:S(2)}, u32[]{:S(2)}) collective-permute-start(bf16[64,2048]{1,0:T(8,128)(2,1)S(1)} %collective-permute-done.2), channel_id=1, source_target_pairs={{0,1},{1,0},{2,3},{3,2},{4,5},{5,4},{6,7},{7,6},{8,9},{9,8},{10,11... | collective-permute-start | bytes 786440 | tf_op jit(solution)/shard_map/ppermute | solution.py:28
  17.2 11.6 %collective-permute-start.4 = (bf16[64,2048]{1,0:T(8,128)(2,1)S(1)}, bf16[64,2048]{1,0:T(8,128)(2,1)S(1)}, u32[]{:S(2)}, u32[]{:S(2)}) collective-permute-start(bf16[64,2048]{1,0:T(8,128)(2,1)S(1)} %get-tuple-element.27), channel_id=1, source_target_pairs={{0,1},{1,0},{2,3},{3,2},{4,5},{5,4},{6,7},{7,6},{8,9},{9,8},{10,11... | collective-permute-start | bytes 786440 | tf_op jit(solution)/shard_map/ppermute | solution.py:28
  19.1 10.6 %collective-permute-start.1 = (bf16[64,2048]{1,0:T(8,128)(2,1)S(1)}, bf16[64,2048]{1,0:T(8,128)(2,1)S(1)}, u32[]{:S(2)}, u32[]{:S(2)}) collective-permute-start(bf16[64,2048]{1,0:T(8,128)(2,1)S(1)} %get-tuple-element.24), channel_id=1, source_target_pairs={{0,1},{1,0},{2,3},{3,2},{4,5},{5,4},{6,7},{7,6},{8,9},{9,8},{10,11... | collective-permute-start | bytes 786440 | tf_op jit(solution)/shard_map/ppermute | solution.py:28
  27.3 2.5 %collective-permute-start.9 = (f32[8,128]{1,0:T(8,128)S(1)}, f32[8,128]{1,0:T(8,128)S(1)}, u32[]{:S(2)}, u32[]{:S(2)}) collective-permute-start(f32[8,128]{1,0:T(8,128)S(1)} %teacher.1.refs_0_), channel_id=1, source_target_pairs={{0,3},{1,0},{2,1},{3,2},{4,7},{5,4},{6,5},{7,6},{8,11},{9,8},{10,9... | collective-permute-start | bytes 12296 | tf_op jit(solution)/shard_map/ppermute | solution.py:339
  27.4 3.6 %collective-permute-start.8 = (f32[8,128]{1,0:T(8,128)S(1)}, f32[8,128]{1,0:T(8,128)S(1)}, u32[]{:S(2)}, u32[]{:S(2)}) collective-permute-start(f32[8,128]{1,0:T(8,128)S(1)} %teacher.1.refs_0_), channel_id=1, source_target_pairs={{0,2},{1,3},{2,0},{3,1},{4,6},{5,7},{6,4},{7,5},{8,10},{9,11},{10,... | collective-permute-start | bytes 12296 | tf_op jit(solution)/shard_map/ppermute | solution.py:339
  28.7 3.0 %collective-permute-start.7 = (f32[8,128]{1,0:T(8,128)S(1)}, f32[8,128]{1,0:T(8,128)S(1)}, u32[]{:S(2)}, u32[]{:S(2)}) collective-permute-start(f32[8,128]{1,0:T(8,128)S(1)} %teacher.1.refs_0_), channel_id=1, source_target_pairs={{0,1},{1,2},{2,3},{3,0},{4,5},{5,6},{6,7},{7,4},{8,9},{9,10},{10,1... | collective-permute-start | bytes 12296 | tf_op jit(solution)/shard_map/ppermute | solution.py:339
  28.8 9.1 %collective-permute-start.5 = (bf16[64,2048]{1,0:T(8,128)(2,1)S(1)}, bf16[64,2048]{1,0:T(8,128)(2,1)S(1)}, u32[]{:S(2)}, u32[]{:S(2)}) collective-permute-start(bf16[64,2048]{1,0:T(8,128)(2,1)S(1)} %add_convert_fusion), channel_id=1, source_target_pairs={{0,2},{1,3},{2,0},{3,1},{4,6},{5,7},{6,4},{7,5},{8,10},{9,11},{10,... | collective-permute-start | bytes 786440 | tf_op jit(solution)/shard_map/ppermute | solution.py:28

commit v2 on v1

v2 whole, which is shorter than its diff:
```python
import functools

import jax
import jax.numpy as jnp
from jax import lax
from jax.experimental import pallas as pl
from jax.experimental.pallas import tpu as pltpu
from jax.sharding import PartitionSpec as P


PIECES = 4
CAP = 32
LANES = 128
CHUNK = 2048
NT = (((1,), (1,)), ((), ()))
TN = (((0,), (0,)), ((), ()))


def vmem(count):
    return [pl.BlockSpec(memory_space=pltpu.VMEM)] * count


def hbm(count):
    return [pl.BlockSpec(memory_space=pltpu.HBM)] * count


def in_hbm(*values):
    return [pltpu.with_memory_space_constraint(value, pltpu.HBM) for value in values]


def params(mib):
    return pltpu.CompilerParams(vmem_limit_bytes=mib * 1024 * 1024)


def swapped(value, axis, bits):
    count = lax.axis_size(axis)
    return lax.ppermute(value, axis, [(k, k ^ bits) for k in range(count)])


def onward(value, axis):
    count = lax.axis_size(axis)
    return lax.ppermute(value, axis, [(k, (k + 1) % count) for k in range(count)])


def fetched(sources, buffers, sems):
    copies = [
        pltpu.make_async_copy(source, buffer, sems.at[k])
        for k, (source, buffer) in enumerate(zip(sources, buffers))
    ]
    for copy in copies:
        copy.start()
    return copies


def prepare_kernel(
    n_window,
    ids_hbm,
    prob_hbm,
    tokens_hbm,
    cot_hbm,
    rows,
    scaled,
    slot_cot,
    select,
    slot_prob,
    ids_out,
    ids,
    prob,
    tokens,
    cot,
    sems,
):
    copies = fetched(
        (ids_hbm, prob_hbm, tokens_hbm, cot_hbm), (ids, prob, tokens, cot), sems
    )
    copies[0].wait()
    copies[1].wait()
    all_ids = ids[...]
    ids_out[...] = all_ids
    count = all_ids.shape[1]
    before = (
        lax.broadcasted_iota(jnp.int32, (count, count), 0)
        < lax.broadcasted_iota(jnp.int32, (count, count), 1)
    ).astype(jnp.float32).astype(jnp.bfloat16)
    slot = lax.broadcasted_iota(jnp.int32, (CAP, count), 0)
    for e in range(n_window):
        part = pl.ds(e * CAP, CAP)
        hit = all_ids == e
        member = jnp.sum(hit.astype(jnp.float32), axis=0, keepdims=True)
        token_prob = jnp.sum(jnp.where(hit, prob[...], 0.0), axis=0, keepdims=True)
        earlier = jnp.dot(
            jnp.broadcast_to(member, (16, count)).astype(jnp.bfloat16),
            before,
            preferred_element_type=jnp.float32,
        )
        position = earlier[:1].astype(jnp.int32)
        chosen = (slot == position) & (member > 0.5)
        chosen_f = chosen.astype(jnp.float32)
        chosen_b = chosen_f.astype(jnp.bfloat16)
        weight = jnp.sum(chosen_f * token_prob, axis=1, keepdims=True)
        if e == 0:
            copies[2].wait()
        rows[part, :] = jnp.dot(
            chosen_b, tokens[...], preferred_element_type=jnp.float32
        ).astype(jnp.bfloat16)
        if e == 0:
            copies[3].wait()
        cot_rows = jnp.dot(chosen_b, cot[...], preferred_element_type=jnp.float32)
        slot_cot[part, :] = cot_rows.astype(jnp.bfloat16)
        scaled[part, :] = (weight * cot_rows).astype(jnp.bfloat16)
        select[part, :] = chosen_f
        slot_prob[part, :] = jnp.broadcast_to(weight, (CAP, LANES))


def prepare(ids, prob, tokens, cot, n_window):
    count, width = tokens.shape
    slots = n_window * CAP
    wide = jax.ShapeDtypeStruct((slots, width), jnp.bfloat16)
    return pl.pallas_call(
        functools.partial(prepare_kernel, n_window),
        out_shape=(
            wide,
            wide,
            wide,
            jax.ShapeDtypeStruct((slots, count), jnp.float32),
            jax.ShapeDtypeStruct((slots, LANES), jnp.float32),
            jax.ShapeDtypeStruct(ids.shape, ids.dtype),
        ),
        in_specs=hbm(4),
        out_specs=tuple(vmem(6)),
        scratch_shapes=[
            pltpu.VMEM(ids.shape, ids.dtype),
            pltpu.VMEM(prob.shape, prob.dtype),
            pltpu.VMEM(tokens.shape, tokens.dtype),
            pltpu.VMEM(cot.shape, cot.dtype),
            pltpu.SemaphoreType.DMA((4,)),
        ],
        compiler_params=params(8),
        name="prepare",
    )(*in_hbm(ids, prob, tokens, cot))


def forward_math(rows, gate_w, up_w, down_w):
    gate = lax.dot_general(rows, gate_w[...], NT, preferred_element_type=jnp.float32)
    up = lax.dot_general(rows, up_w[...], NT, preferred_element_type=jnp.float32)
    hidden = (gate * jax.nn.sigmoid(gate) * up).astype(jnp.bfloat16)
    out = jnp.dot(hidden, down_w[...], preferred_element_type=jnp.float32)
    return out.astype(jnp.bfloat16), gate, up


def backward_math(scaled, gate, up, gate_w, up_w, down_w):
    sig = jax.nn.sigmoid(gate)
    grad_hidden = lax.dot_general(scaled, down_w[...], NT, preferred_element_type=jnp.float32)
    grad_gate = (grad_hidden * up * sig * (1.0 + gate * (1.0 - sig))).astype(jnp.bfloat16)
    grad_up = (grad_hidden * gate * sig).astype(jnp.bfloat16)
    grad = jnp.dot(grad_gate, gate_w[...], preferred_element_type=jnp.float32)
    grad = grad + jnp.dot(grad_up, up_w[...], preferred_element_type=jnp.float32)
    return grad.astype(jnp.bfloat16)


def forward_kernel(rows_a, rows_b, gate_w, up_w, down_w, keep, send, gate_ref, up_ref):
    half = rows_a.shape[0]
    rows = jnp.concatenate([rows_a[...], rows_b[...]], axis=0)
    out, gate, up = forward_math(rows, gate_w, up_w, down_w)
    keep[...] = out[:half]
    send[...] = out[half:]
    gate_ref[...] = gate
    up_ref[...] = up


def backward_kernel(scaled_a, scaled_b, gate, up, gate_w, up_w, down_w, keep, send):
    half = scaled_a.shape[0]
    scaled = jnp.concatenate([scaled_a[...], scaled_b[...]], axis=0)
    grad = backward_math(scaled, gate[...], up[...], gate_w, up_w, down_w)
    keep[...] = grad[:half]
    send[...] = grad[half:]


def forward(rows_a, rows_b, weights):
    half, width = rows_a.shape
    hidden = weights[0].shape[0]
    part = jax.ShapeDtypeStruct((half, width), jnp.bfloat16)
    act = jax.ShapeDtypeStruct((2 * half, hidden), jnp.float32)
    return pl.pallas_call(
        forward_kernel,
        out_shape=(part, part, act, act),
        in_specs=vmem(5),
        out_specs=tuple(vmem(4)),
        compiler_params=params(12),
        name="forward",
    )(rows_a, rows_b, *weights)


def backward(scaled_a, scaled_b, gate, up, weights):
    half, width = scaled_a.shape
    part = jax.ShapeDtypeStruct((half, width), jnp.bfloat16)
    return pl.pallas_call(
        backward_kernel,
        out_shape=(part, part),
        in_specs=vmem(7),
        out_specs=tuple(vmem(2)),
        compiler_params=params(12),
        name="backward",
    )(scaled_a, scaled_b, gate, up, *weights)


def spread(select, value, exact):
    high = value.astype(jnp.bfloat16)
    chosen = select.astype(jnp.bfloat16)
    total = lax.dot_general(chosen, high, TN, preferred_element_type=jnp.float32)
    if exact:
        return total
    low = (value - high.astype(jnp.float32)).astype(jnp.bfloat16)
    return total + lax.dot_general(chosen, low, TN, preferred_element_type=jnp.float32)


BLOCK = 512


def summed(refs, part):
    total = refs[0][:, part].astype(jnp.float32)
    for other in refs[1:]:
        total = total + other[:, part].astype(jnp.float32)
    return total


def combine_out_kernel(n_window, parts, *refs):
    outs = refs[:parts]
    ids, select, slot_prob, slot_cot, layer_out, prob_grad, stage, prob_stage, sems = refs[parts:]
    exact = n_window == 1
    chosen = select[...]
    weight = slot_prob[:, :1]
    width = outs[0].shape[1]
    block = min(BLOCK, width)
    blocks = width // block
    copies = []
    per_slot = jnp.zeros((chosen.shape[0], 1), jnp.float32)
    for k in range(blocks):
        part = pl.ds(k * block, block)
        out = summed(outs, part)
        per_slot = per_slot + jnp.sum(
            out * slot_cot[:, part].astype(jnp.float32), axis=1, keepdims=True
        )
        stage[:, part] = spread(chosen, weight * out, exact).astype(jnp.bfloat16)
        copy = pltpu.make_async_copy(stage.at[:, part], layer_out.at[:, part], sems.at[k])
        copy.start()
        copies.append(copy)
    spread_prob = chosen * per_slot
    for e in range(n_window):
        per_token = jnp.sum(spread_prob[e * CAP : (e + 1) * CAP], axis=0, keepdims=True)
        kept = jnp.where(ids[...] == e, per_token, 0.0)
        whole = kept if e == 0 else whole + kept
    prob_stage[...] = whole
    copy = pltpu.make_async_copy(prob_stage, prob_grad, sems.at[blocks])
    copy.start()
    copies.append(copy)
    for copy in copies:
        copy.wait()


def combine_grad_kernel(n_window, parts, *refs):
    grads = refs[:parts]
    select, input_grad, stage, sems = refs[parts:]
    exact = n_window == 1
    chosen = select[...]
    width = grads[0].shape[1]
    block = min(BLOCK, width)
    copies = []
    for k in range(width // block):
        part = pl.ds(k * block, block)
        stage[:, part] = spread(chosen, summed(grads, part), exact).astype(jnp.bfloat16)
        copy = pltpu.make_async_copy(stage.at[:, part], input_grad.at[:, part], sems.at[k])
        copy.start()
        copies.append(copy)
    for copy in copies:
        copy.wait()


def combine_out(outs, ids, select, slot_prob, slot_cot, n_window):
    parts = len(outs)
    width = outs[0].shape[1]
    topk, count = ids.shape
    return pl.pallas_call(
        functools.partial(combine_out_kernel, n_window, parts),
        out_shape=(
            jax.ShapeDtypeStruct((count, width), jnp.bfloat16),
            jax.ShapeDtypeStruct((topk, count), jnp.float32),
        ),
        in_specs=vmem(parts + 4),
        out_specs=tuple(hbm(2)),
        scratch_shapes=[
            pltpu.VMEM((count, width), jnp.bfloat16),
            pltpu.VMEM((topk, count), jnp.float32),
            pltpu.SemaphoreType.DMA((width // min(BLOCK, width) + 1,)),
        ],
        compiler_params=params(12),
        name="combine_out",
    )(*outs, ids, select, slot_prob, slot_cot)


def combine_grad(grads, select, n_window):
    parts = len(grads)
    width = grads[0].shape[1]
    count = select.shape[1]
    return pl.pallas_call(
        functools.partial(combine_grad_kernel, n_window, parts),
        out_shape=jax.ShapeDtypeStruct((count, width), jnp.bfloat16),
        in_specs=vmem(parts + 1),
        out_specs=hbm(1)[0],
        scratch_shapes=[
            pltpu.VMEM((count, width), jnp.bfloat16),
            pltpu.SemaphoreType.DMA((width // min(BLOCK, width),)),
        ],
        compiler_params=params(12),
        name="combine_grad",
    )(*grads, select)


def spans(width, parts):
    step = CHUNK * max(1, width // (parts * CHUNK))
    return [(start, min(step, width - start)) for start in range(0, width, step)]


def chunks(start, size):
    return [(at, min(CHUNK, start + size - at)) for at in range(start, start + size, CHUNK)]


def load(ref, at, size):
    return ref[:, pl.ds(at, size)].astype(jnp.float32)


def row_max(ref, start, size, top):
    full = None
    for at, span in chunks(start, size):
        value = load(ref, at, span)
        if span < CHUNK:
            top = jnp.maximum(top, jnp.max(value, axis=1, keepdims=True))
        else:
            full = value if full is None else jnp.maximum(full, value)
    if full is not None:
        top = jnp.maximum(top, jnp.max(full, axis=1, keepdims=True))
    return top


def row_sums(width, step):
    full = tail = None
    for at, span in chunks(0, width):
        values = step(at, span)
        if span < CHUNK:
            tail = values
        elif full is None:
            full = values
        else:
            full = tuple(one + two for one, two in zip(full, values))
    sums = [jnp.sum(value, axis=1, keepdims=True) for value in (full or tail)]
    if full is not None and tail is not None:
        more = [jnp.sum(value, axis=1, keepdims=True) for value in tail]
        sums = [one + two for one, two in zip(sums, more)]
    return sums


def columns(values, rows):
    lane = lax.broadcasted_iota(jnp.int32, (rows, LANES), 1)
    tile = jnp.zeros((rows, LANES), jnp.float32)
    for k, value in enumerate(values):
        tile = jnp.where(lane == k, value, tile)
    return tile


def diagonal(rows):
    return lax.broadcasted_iota(jnp.int32, (rows, rows), 0) == lax.broadcasted_iota(
        jnp.int32, (rows, rows), 1
    )


def student_kernel(base, labels_hbm, student_hbm, down_hbm, stats, student, down, labels, sems):
    rows, width = student.shape
    parts = spans(width, 4)
    copies = fetched((labels_hbm,), (labels,), sems)
    for k, (start, size) in enumerate(parts):
        part = pl.ds(start, size)
        copy = pltpu.make_async_copy(
            student_hbm.at[:, part], student.at[:, part], sems.at[k + 1]
        )
        copy.start()
        copies.append(copy)
    weight = pltpu.make_async_copy(down_hbm, down, sems.at[len(parts) + 1])
    weight.start()
    copies[0].wait()
    spread_out = jnp.where(diagonal(rows), jnp.broadcast_to(labels[...], (rows, rows)), 0)
    label = jnp.sum(spread_out.astype(jnp.float32), axis=1, keepdims=True).astype(jnp.int32)
    label = label - base[0]
    top = jnp.full((rows, 1), -jnp.inf, jnp.float32)
    for copy, (start, size) in zip(copies[1:], parts):
        copy.wait()
        top = row_max(student, start, size, top)

    def step(at, size):
        value = load(student, at, size)
        here = lax.broadcasted_iota(jnp.int32, (rows, size), 1) == label - at
        return jnp.exp(value - top), jnp.where(here, value, 0.0)

    total, picked = row_sums(width, step)
    zero = jnp.zeros((rows, 1), jnp.float32)
    stats[...] = columns(
        (top, total, picked, zero, zero, zero, label.astype(jnp.float32)), rows
    )
    weight.wait()


def teacher_kernel(student, teacher, student_stats, stats):
    rows, width = student.shape
    top = row_max(teacher, 0, width, jnp.full((rows, 1), -jnp.inf, jnp.float32))

    def step(at, size):
        ours = load(student, at, size)
        theirs = load(teacher, at, size)
        power = jnp.exp(theirs - top)
        return power, power * (theirs - ours)

    total, cross = row_sums(width, step)
    lane = lax.broadcasted_iota(jnp.int32, (rows, LANES), 1)
    tile = student_stats[...]
    tile = jnp.where(lane == 3, top, tile)
    tile = jnp.where(lane == 4, total, tile)
    stats[...] = jnp.where(lane == 5, cross, tile)


def final_kernel(parts, student, teacher, *refs):
    stats, (loss, grad, stage, loss_stage, sems) = refs[:parts], refs[parts:]
    rows, width = student.shape
    tiles = [ref[...] for ref in stats]
    label = tiles[0][:, 6:7].astype(jnp.int32)
    top = functools.reduce(jnp.maximum, tiles)
    smax, tmax = top[:, 0:1], top[:, 3:4]
    ssum = tsum = cross = picked = jnp.zeros((rows, 1), jnp.float32)
    for tile in tiles:
        ssum = ssum + tile[:, 1:2] * jnp.exp(tile[:, 0:1] - smax)
        scale = jnp.exp(tile[:, 3:4] - tmax)
        tsum = tsum + tile[:, 4:5] * scale
        cross = cross + tile[:, 5:6] * scale
        picked = picked + tile[:, 2:3]
    lse_s = smax + jnp.log(ssum)
    lse_t = tmax + jnp.log(tsum)
    value = 2.0 * lse_s - picked + cross / tsum - lse_t
    loss_stage[...] = jnp.sum(jnp.where(diagonal(rows), value, 0.0), axis=0, keepdims=True)
    copies = fetched((loss_stage,), (loss,), sems)
    for k, (start, size) in enumerate(spans(width, 4)):
        for at, span in chunks(start, size):
            here = lax.broadcasted_iota(jnp.int32, (rows, span), 1) == label - at
            result = (
                2.0 * jnp.exp(load(student, at, span) - lse_s)
                - here.astype(jnp.float32)
                - jnp.exp(load(teacher, at, span) - lse_t)
            )
            stage[:, pl.ds(at, span)] = result.astype(jnp.bfloat16)
        part = pl.ds(start, size)
        copy = pltpu.make_async_copy(stage.at[:, part], grad.at[:, part], sems.at[k + 1])
        copy.start()
        copies.append(copy)
    for copy in copies:
        copy.wait()


def distill(student, stale, labels, down_w):
    _, width = student.shape
    teacher = onward(stale, "peer")
    base = (lax.axis_index("grp") * width).astype(jnp.int32).reshape(1)
    own, student, down_w = student_stats(base, labels, student, down_w)
    stats = teacher_stats(student, teacher, own)
    count = lax.axis_size("grp")
    others = []
    for s in range(1, count):
        others.append(
            lax.ppermute(stats, "grp", [(k, (k + s) % count) for k in range(count)])
        )
    loss, grad = finish(student, teacher, [stats, *others])
    return loss, grad, down_w


def student_stats(base, labels, student, down_w):
    rows, width = student.shape
    return pl.pallas_call(
        student_kernel,
        out_shape=(
            jax.ShapeDtypeStruct((rows, LANES), jnp.float32),
            jax.ShapeDtypeStruct(student.shape, student.dtype),
            jax.ShapeDtypeStruct(down_w.shape, down_w.dtype),
        ),
        in_specs=[pl.BlockSpec(memory_space=pltpu.SMEM)] + hbm(3),
        out_specs=tuple(vmem(3)),
        scratch_shapes=[
            pltpu.VMEM(labels.shape, labels.dtype),
            pltpu.SemaphoreType.DMA((len(spans(width, 4)) + 2,)),
        ],
        compiler_params=params(8),
        name="student",
    )(base, *in_hbm(labels, student, down_w))


def teacher_stats(student, teacher, own):
    rows, _ = student.shape
    return pl.pallas_call(
        teacher_kernel,
        out_shape=jax.ShapeDtypeStruct((rows, LANES), jnp.float32),
        in_specs=vmem(3),
        out_specs=vmem(1)[0],
        compiler_params=params(8),
        name="teacher",
    )(student, teacher, own)


def finish(student, teacher, stats):
    rows, width = student.shape
    count = len(stats)
    return pl.pallas_call(
        functools.partial(final_kernel, count),
        out_shape=(
            jax.ShapeDtypeStruct((1, rows), jnp.float32),
            jax.ShapeDtypeStruct((rows, width), jnp.bfloat16),
        ),
        in_specs=vmem(2 + count),
        out_specs=tuple(hbm(2)),
        scratch_shapes=[
            pltpu.VMEM((rows, width), jnp.bfloat16),
            pltpu.VMEM((1, rows), jnp.float32),
            pltpu.SemaphoreType.DMA((len(spans(width, 4)) + 1,)),
        ],
        compiler_params=params(8),
        name="final",
    )(student, teacher, *stats)


def between_blocks(value, n_window):
    if n_window == 1:
        return value
    groups = [[b + PIECES * a for a in range(n_window)] for b in range(PIECES)]
    return lax.all_to_all(
        value, "grp", split_axis=0, concat_axis=0, tiled=True, axis_index_groups=groups
    )


def layer(tokens, cotangent, ids, prob, weights, n_window):
    rows, scaled, slot_cot, select, slot_prob, ids = prepare(ids, prob, tokens, cotangent, n_window)
    rows = between_blocks(rows, n_window)
    scaled = between_blocks(scaled, n_window)
    rows_far = swapped(rows, "grp", 2)
    scaled_far = swapped(scaled, "grp", 2)
    rows_near = swapped(rows, "grp", 1)
    scaled_near = swapped(scaled, "grp", 1)
    rows_cross = swapped(rows_far, "grp", 1)
    scaled_cross = swapped(scaled_far, "grp", 1)

    out_own, out_send, gate, up = forward(rows, rows_near, weights)
    grad_own, grad_send = backward(scaled, scaled_near, gate, up, weights)
    out_back = swapped(out_send, "grp", 1)
    grad_back = swapped(grad_send, "grp", 1)

    out_keep, out_send, gate, up = forward(rows_far, rows_cross, weights)
    out_more = swapped(out_send, "grp", 1)
    grad_keep, grad_send = backward(scaled_far, scaled_cross, gate, up, weights)
    grad_more = swapped(grad_send, "grp", 1)
    out_home = swapped(pair_sum(out_keep, out_more), "grp", 2)
    grad_home = swapped(pair_sum(grad_keep, grad_more), "grp", 2)

    outs = collected([out_own, out_back, out_home], n_window)
    grads = collected([grad_own, grad_back, grad_home], n_window)
    layer_out, prob_grad = combine_out(outs, ids, select, slot_prob, slot_cot, n_window)
    input_grad = combine_grad(grads, select, n_window)
    return layer_out, input_grad, prob_grad


def pair_sum(one, two):
    return (one.astype(jnp.float32) + two.astype(jnp.float32)).astype(jnp.bfloat16)


def collected(parts, n_window):
    if n_window == 1:
        return parts
    total = functools.reduce(jnp.add, [part.astype(jnp.float32) for part in parts])
    return [between_blocks(total.astype(jnp.bfloat16), n_window)]


def body(
    tokens,
    cotangent,
    expert_ids,
    route_prob,
    w_gate,
    w_up,
    w_down,
    student_logits,
    stale_logits,
    labels,
):
    n_window = lax.axis_size("grp") // PIECES
    distill_loss, logit_grad, down_w = distill(
        student_logits[0], stale_logits[0], labels, w_down[0]
    )
    layer_out, input_grad, prob_grad = layer(
        tokens,
        cotangent,
        expert_ids.T,
        route_prob.T,
        (w_gate[0].T, w_up[0].T, down_w),
        n_window,
    )
    return (layer_out, input_grad, prob_grad.T, distill_loss, logit_grad[None])


def solution(mesh):
    placed = (
        P(("peer", "grp"), None),
        P(("peer", "grp"), None),
        P(("peer", "grp"), None),
        P(("peer", "grp"), None),
        P("peer", None, "grp"),
        P("peer", None, "grp"),
        P("peer", "grp", None),
        P("peer", None, "grp"),
        P("peer", None, "grp"),
        P("peer", None),
    )
    return jax.shard_map(
        body,
        mesh=mesh,
        in_specs=placed,
        out_specs=(
            P(("peer", "grp"), None),
            P(("peer", "grp"), None),
            P(("peer", "grp"), None),
            P("peer", None),
            P("peer", None, "grp"),
        ),
        check_vma=False,
    )
```

time: 39.5 us -> 42.7 us (1.081)
  starting transfers between devices: 7.56 us -> 12.4 us
  Pallas kernels: 7.84 us -> 11.4 us
  local copies, waits for them, and re-layouts: 3.57 us -> 0.02 us
  waiting for transfers between devices: 19.4 us -> 17.9 us
    ppermute x1, waiting for transfers between devices: 7.21 us -> 11.6 us  [onward(): lax.ppermute(value, axis, [(k, (k + 1) % count) for k in range(count)])]
    ppermute x6 -> x12, waiting for transfers between devices: 10.2 us -> 6.25 us  [swapped(): return lax.ppermute(value, axis, [(k, k ^ bits) for k in range(count)])]
    unnamed x19 -> x6, local copies, waits for them, and re-layouts: 3.47 us -> 0.02 us
    ppermute x6 -> x12, starting transfers between devices: 4.59 us -> 7.64 us  [swapped(): return lax.ppermute(value, axis, [(k, k ^ bits) for k in range(count)])]
    pallas_call x6 -> x9, Pallas kernels: 7.44 us -> 9.77 us  [the longest x2 1.97 us: backward(): pl.pallas_call(backward_kernel, out_shape=(part, part), in_specs=vmem(7),...]
    ppermute x3, waiting for transfers between devices: 2.01 us -> 0.01 us  [distill(): lax.ppermute(stats, 'grp', [(k, (k + s) % count) for k in range(count)])]
    ppermute x3, starting transfers between devices: 1.45 us -> 2.96 us  [distill(): lax.ppermute(stats, 'grp', [(k, (k + s) % count) for k in range(count)])]
    pallas_call x1, Pallas kernels: 0.4 us -> 1.61 us  [prepare(): pl.pallas_call(functools.partial(prepare_kernel, n_window), out_shape=(wi...]
  transfers between devices with their start and end apart: 10 -> 16, of which waited for: 6 -> 3; matrix products, arithmetic and copies ran while one was open for 0% -> 0% of each run, Pallas kernels for 16% -> 19%
where the time goes in v2:
time: 42.7 us; the launch traced here: 42.6 us
  waiting for transfers between devices  17.9 us (42%)
  starting transfers between devices  12.4 us (29%)
  Pallas kernels  11.4 us (27%)
  between operations  0.83 us (2%)
    ppermute x1, waiting for transfers between devices, onward(): lax.ppermute(value, axis, [(k, (k + 1) % count) for k in range(count)])  11.6 us
    ppermute x12, starting transfers between devices, swapped(): return lax.ppermute(value, axis, [(k, k ^ bits) for k in range(count)])  7.64 us
    ppermute x12, waiting for transfers between devices, swapped(): return lax.ppermute(value, axis, [(k, k ^ bits) for k in range(count)])  6.25 us
    ppermute x3, starting transfers between devices, distill(): lax.ppermute(stats, 'grp', [(k, (k + s) % count) for k in range(count)])  2.96 us
    pallas_call x2, Pallas kernels, backward(): pl.pallas_call(backward_kernel, out_shape=(part, part), in_specs=vmem(7),...  1.97 us
    pallas_call x1, Pallas kernels, student_stats(): pl.pallas_call(student_kernel, out_shape=(jax.ShapeDtypeStruct((rows, LAN...  1.94 us
    ppermute x1, starting transfers between devices, onward(): lax.ppermute(value, axis, [(k, (k + 1) % count) for k in range(count)])  1.76 us
    pallas_call x2, Pallas kernels, forward(): pl.pallas_call(forward_kernel, out_shape=(part, part, act, act), in_specs...  1.62 us
  transfers between devices with their start and end apart: 16, of which 3 were waited for; matrix products, arithmetic and copies ran while one was open for 0% of the time, Pallas kernels for 19%

profile of v2, /device:TPU:0, one launch (start us, length us, event | category | flops | bytes accessed | tf_op | source)
XLA Modules:
  0.0 42.6 jit_solution(14767682082229842576)
XLA Ops:
  0.6 0.0 copy-start.1
  0.6 1.6 %prepare.1 = (bf16[32,2048]{1,0:T(8,128)(2,1)S(1)}, bf16[32,2048]{1,0:T(8,128)(2,1)S(1)}, bf16[32,2048]{1,0:T(8,128)(2,1)S(1)}, f32[32,128]{1,0:T(8,128)S(1)}, f...) custom-call(s32[4,128]{1,0:T(4,128)} %bitcast.24, f32[4,128]{1,0:T(4,128)} %bitcast.25, bf16[128,2048]{1,0:T(8,128)(2,1)} %tokens_hbm.1, ...), custom_call_target="tpu_custom_call" | custom-call | tf_op jit(solution)/shard_map/prepare/pallas_call | solution.py:119
  2.3 0.0 copy-start
  2.3 3.0 %collective-permute-start.2 = (bf16[32,2048]{1,0:T(8,128)(2,1)S(1)}, bf16[32,2048]{1,0:T(8,128)(2,1)S(1)}, u32[]{:S(2)}, u32[]{:S(2)}) collective-permute-start(bf16[32,2048]{1,0:T(8,128)(2,1)S(1)} %get-tuple-element.30.rows_a), channel_id=1, source_target_pairs={{0,2},{1,3},{2,0},{3,1},{4,6},{5,7},{6,4},{7,5},{8,10},{9,11},{10,... | collective-permute-start | bytes 393224 | tf_op jit(solution)/shard_map/ppermute | solution.py:37
  5.3 0.1 collective-permute-start.8
  5.4 4.3 %collective-permute-done.2.rows_a = bf16[32,2048]{1,0:T(8,128)(2,1)S(1)} collective-permute-done((bf16[32,2048]{1,0:T(8,128)(2,1)S(1)}, bf16[32,2048]{1,0:T(8,128)(2,1)S(1)}, u32[]{:S(2)}, u32[]{:S(2)}) %collective-permute-start.2) | collective-permute-done | bytes 131104 | tf_op jit(solution)/shard_map/ppermute | solution.py:37
  9.7 0.0 collective-permute-start.3
  9.7 2.0 %collective-permute-done.8.scaled_a = bf16[32,2048]{1,0:T(8,128)(2,1)S(1)} collective-permute-done((bf16[32,2048]{1,0:T(8,128)(2,1)S(1)}, bf16[32,2048]{1,0:T(8,128)(2,1)S(1)}, u32[]{:S(2)}, u32[]{:S(2)}) %collective-permute-start.8) | collective-permute-done | bytes 131104 | tf_op jit(solution)/shard_map/ppermute | solution.py:37
  11.6 0.0 collective-permute-start.9
  11.6 0.5 %collective-permute-start = (bf16[32,2048]{1,0:T(8,128)(2,1)S(1)}, bf16[32,2048]{1,0:T(8,128)(2,1)S(1)}, u32[]{:S(2)}, u32[]{:S(2)}) collective-permute-start(bf16[32,2048]{1,0:T(8,128)(2,1)S(1)} %get-tuple-element.30.rows_a), channel_id=1, source_target_pairs={{0,1},{1,0},{2,3},{3,2},{4,5},{5,4},{6,7},{7,6},{8,9},{9,8},{10,11... | collective-permute-start | bytes 393224 | tf_op jit(solution)/shard_map/ppermute | solution.py:37
  12.1 0.0 collective-permute-start.6
  12.1 1.9 %student.1 = (f32[8,128]{1,0:T(8,128)S(1)}, bf16[8,37984]{1,0:T(8,128)(2,1)S(1)}, bf16[176,2048]{1,0:T(8,128)(2,1)S(1)}) custom-call(s32[1]{0:T(128)} %bitcast.6.base, s32[1,8]{1,0:T(1,128)} %labels_hbm.1, bf16[8,37984]{1,0:T(8,128)(2,1)} %bitcast.23, bf16[176,2048]{1,0:T(8,128)(2,1)} %bitcast.22), custom_call_target="tpu_custom_call" | custom-call | tf_op jit(solution)/shard_map/student/pallas_call | solution.py:483
  14.1 0.0 collective-permute-done.3.rows_b
  14.1 0.0 copy-done.1
  14.1 0.0 copy-done
  14.1 0.8 %forward.3 = (bf16[32,2048]{1,0:T(8,128)(2,1)S(1)}, bf16[32,2048]{1,0:T(8,128)(2,1)S(1)}, f32[64,176]{1,0:T(8,128)S(1)}, f32[64,176]{1,0:T(8,128)S(1)}) custom-call(bf16[32,2048]{1,0:T(8,128)(2,1)S(1)} %collective-permute-done.2.rows_a, bf16[32,2048]{1,0:T(8,128)(2,1)S(1)} %collective-permute-done.3.rows_b, bf16[176,2048]{1,0:T(8,128)(2,1)S(1)} %bitcast.14, ...), custom_call_target="tpu_custom_call" | custom-call | tf_op jit(solution)/shard_map/forward/pallas_call | solution.py:184
  14.9 0.0 collective-permute-done.9.scaled_b
  14.9 0.0 copy-start.2
  14.9 1.0 %backward.3 = (bf16[32,2048]{1,0:T(8,128)(2,1)S(1)}, bf16[32,2048]{1,0:T(8,128)(2,1)S(1)}) custom-call(bf16[32,2048]{1,0:T(8,128)(2,1)S(1)} %collective-permute-done.8.scaled_a, bf16[32,2048]{1,0:T(8,128)(2,1)S(1)} %collective-permute-done.9.scaled_b, f32[64,176]{1,0:T(8,128)S(1)} %get-tuple-element.46.gate, f32[64,176]{1,0:T(8,128)S(1)} %get-tuple-element.47.up, ...), custom_call_target="tpu_custom_call" | custom-call | tf_op jit(solution)/shard_map/backward/pallas_call | solution.py:197
  15.9 0.6 %collective-permute-start.10 = (bf16[32,2048]{1,0:T(8,128)(2,1)S(1)}, bf16[32,2048]{1,0:T(8,128)(2,1)S(1)}, u32[]{:S(2)}, u32[]{:S(2)}) collective-permute-start(bf16[32,2048]{1,0:T(8,128)(2,1)S(1)} %get-tuple-element.49), channel_id=1, source_target_pairs={{0,1},{1,0},{2,3},{3,2},{4,5},{5,4},{6,7},{7,6},{8,9},{9,8},{10,11... | collective-permute-start | bytes 393224 | tf_op jit(solution)/shard_map/ppermute | solution.py:37
  16.5 0.0 copy-done.2
  16.5 1.8 %collective-permute-start.12 = (bf16[8,37984]{1,0:T(8,128)(2,1)S(1)}, bf16[8,37984]{1,0:T(8,128)(2,1)S(1)}, u32[]{:S(2)}, u32[]{:S(2)}) collective-permute-start(bf16[8,37984]{1,0:T(8,128)(2,1)S(1)} %bitcast.26), channel_id=1, source_target_pairs={{0,4},{4,8},{8,12},{12,16},{16,20},{20,24},{24,28},{28,0},{1,5},{5... | collective-permute-start | bytes 1823240 | tf_op jit(solution)/shard_map/ppermute | solution.py:42
  18.3 0.0 collective-permute-done.rows_b
  18.3 0.8 %forward.2 = (bf16[32,2048]{1,0:T(8,128)(2,1)S(1)}, bf16[32,2048]{1,0:T(8,128)(2,1)S(1)}, f32[64,176]{1,0:T(8,128)S(1)}, f32[64,176]{1,0:T(8,128)S(1)}) custom-call(bf16[32,2048]{1,0:T(8,128)(2,1)S(1)} %get-tuple-element.30.rows_a, bf16[32,2048]{1,0:T(8,128)(2,1)S(1)} %collective-permute-done.rows_b, bf16[176,2048]{1,0:T(8,128)(2,1)S(1)} %bitcast.16, ...), custom_call_target="tpu_custom_call" | custom-call | tf_op jit(solution)/shard_map/forward/pallas_call | solution.py:184
  19.1 0.0 collective-permute-done.6.scaled_b
  19.1 1.0 %backward.2 = (bf16[32,2048]{1,0:T(8,128)(2,1)S(1)}, bf16[32,2048]{1,0:T(8,128)(2,1)S(1)}) custom-call(bf16[32,2048]{1,0:T(8,128)(2,1)S(1)} %get-tuple-element.41.scaled_a, bf16[32,2048]{1,0:T(8,128)(2,1)S(1)} %collective-permute-done.6.scaled_b, f32[64,176]{1,0:T(8,128)S(1)} %get-tuple-element.42.gate, f32[64,176]{1,0:T(8,128)S(1)} %get-tuple-element.43.up, ...), custom_call_target="tpu_custom_call" | custom-call | tf_op jit(solution)/shard_map/backward/pallas_call | solution.py:197
  20.1 0.1 collective-permute-start.7
  20.2 0.5 %collective-permute-start.1 = (bf16[32,2048]{1,0:T(8,128)(2,1)S(1)}, bf16[32,2048]{1,0:T(8,128)(2,1)S(1)}, u32[]{:S(2)}, u32[]{:S(2)}) collective-permute-start(bf16[32,2048]{1,0:T(8,128)(2,1)S(1)} %get-tuple-element.33), channel_id=1, source_target_pairs={{0,1},{1,0},{2,3},{3,2},{4,5},{5,4},{6,7},{7,6},{8,9},{9,8},{10,11... | collective-permute-start | bytes 393224 | tf_op jit(solution)/shard_map/ppermute | solution.py:37
  20.7 0.1 collective-permute-start.4
  20.8 0.0 collective-permute-done.10
  20.8 1.6 %collective-permute-start.11 = (bf16[32,2048]{1,0:T(8,128)(2,1)S(1)}, bf16[32,2048]{1,0:T(8,128)(2,1)S(1)}, u32[]{:S(2)}, u32[]{:S(2)}) collective-permute-start(bf16[32,2048]{1,0:T(8,128)(2,1)S(1)} %add_convert_fusion), channel_id=1, source_target_pairs={{0,2},{1,3},{2,0},{3,1},{4,6},{5,7},{6,4},{7,5},{8,10},{9,11},{10,... | collective-permute-start | bytes 393224 | tf_op jit(solution)/shard_map/ppermute | solution.py:37
  22.4 0.0 collective-permute-done.4
  22.4 1.2 %collective-permute-start.5 = (bf16[32,2048]{1,0:T(8,128)(2,1)S(1)}, bf16[32,2048]{1,0:T(8,128)(2,1)S(1)}, u32[]{:S(2)}, u32[]{:S(2)}) collective-permute-start(bf16[32,2048]{1,0:T(8,128)(2,1)S(1)} %add_convert_fusion.1), channel_id=1, source_target_pairs={{0,2},{1,3},{2,0},{3,1},{4,6},{5,7},{6,4},{7,5},{8,10},{9,11},{10,... | collective-permute-start | bytes 393224 | tf_op jit(solution)/shard_map/ppermute | solution.py:37
  23.6 11.6 %collective-permute-done.12.teacher = bf16[8,37984]{1,0:T(8,128)(2,1)S(1)} collective-permute-done((bf16[8,37984]{1,0:T(8,128)(2,1)S(1)}, bf16[8,37984]{1,0:T(8,128)(2,1)S(1)}, u32[]{:S(2)}, u32[]{:S(2)}) %collective-permute-start.12) | collective-permute-done | bytes 607776 | tf_op jit(solution)/shard_map/ppermute | solution.py:42
  35.3 0.6 %teacher.1.refs_0_ = f32[8,128]{1,0:T(8,128)S(1)} custom-call(bf16[8,37984]{1,0:T(8,128)(2,1)S(1)} %get-tuple-element.51.student, bf16[8,37984]{1,0:T(8,128)(2,1)S(1)} %collective-permute-done.12.teacher, f32[8,128]{1,0:T(8,128)S(1)} %get-tuple-element.52.student_stats), custom_call_target="tpu_custom_call" | custom-call | tf_op jit(solution)/shard_map/teacher/pallas_call | solution.py:503
  35.9 0.0 collective-permute-start.13
  35.9 0.0 collective-permute-done.7.refs_1_
  35.9 1.6 %collective-permute-start.14 = (f32[8,128]{1,0:T(8,128)S(1)}, f32[8,128]{1,0:T(8,128)S(1)}, u32[]{:S(2)}, u32[]{:S(2)}) collective-permute-start(f32[8,128]{1,0:T(8,128)S(1)} %teacher.1.refs_0_), channel_id=1, source_target_pairs={{0,2},{1,3},{2,0},{3,1},{4,6},{5,7},{6,4},{7,5},{8,10},{9,11},{10,... | collective-permute-start | bytes 12296 | tf_op jit(solution)/shard_map/ppermute | solution.py:475
  37.4 0.0 collective-permute-done.11.refs_2_
  37.4 1.4 %collective-permute-start.15 = (f32[8,128]{1,0:T(8,128)S(1)}, f32[8,128]{1,0:T(8,128)S(1)}, u32[]{:S(2)}, u32[]{:S(2)}) collective-permute-start(f32[8,128]{1,0:T(8,128)S(1)} %teacher.1.refs_0_), channel_id=1, source_target_pairs={{0,3},{1,0},{2,1},{3,2},{4,7},{5,4},{6,5},{7,6},{8,11},{9,8},{10,9... | collective-permute-start | bytes 12296 | tf_op jit(solution)/shard_map/ppermute | solution.py:475
  38.8 1.0 %combine_grad.1 = bf16[128,2048]{1,0:T(8,128)(2,1)} custom-call(bf16[32,2048]{1,0:T(8,128)(2,1)S(1)} %get-tuple-element.44.refs_0_, bf16[32,2048]{1,0:T(8,128)(2,1)S(1)} %collective-permute-done.7.refs_1_, bf16[32,2048]{1,0:T(8,128)(2,1)S(1)} %collective-permute-done.11.refs_2_, f32[32,128]{1,0:T(8,128)S(1)} %get-tuple-element.37.refs_4_.refs_3_), custom_call_target="tpu_custom_call" | custom-call | tf_op jit(solution)/shard_map/combine_grad/pallas_call | solution.py:305
  39.9 0.0 collective-permute-done.1.refs_1_
  39.9 0.0 collective-permute-done.5.refs_2_
  39.9 1.1 %combine_out.1 = (bf16[128,2048]{1,0:T(8,128)(2,1)}, f32[4,128]{1,0:T(4,128)}) custom-call(bf16[32,2048]{1,0:T(8,128)(2,1)S(1)} %get-tuple-element.32.refs_0_, bf16[32,2048]{1,0:T(8,128)(2,1)S(1)} %collective-permute-done.1.refs_1_, bf16[32,2048]{1,0:T(8,128)(2,1)S(1)} %collective-permute-done.5.refs_2_, s32[4,128]{1,0:T(4,128)S(1)} %get-tuple-element.36.refs_3_, ...), custom_call_target="tpu_custom_call" | custom-call | tf_op jit(solution)/shard_map/combine_out/pallas_call | solution.py:283
  41.0 0.0 collective-permute-done.13.refs_1_
  41.0 0.0 collective-permute-done.14.refs_2_
  41.0 0.0 collective-permute-done.15.refs_3_
  41.0 1.6 %final.1 = (f32[1,8]{1,0:T(1,128)}, bf16[8,37984]{1,0:T(8,128)(2,1)}) custom-call(bf16[8,37984]{1,0:T(8,128)(2,1)S(1)} %get-tuple-element.51.student, bf16[8,37984]{1,0:T(8,128)(2,1)S(1)} %collective-permute-done.12.teacher, f32[8,128]{1,0:T(8,128)S(1)} %teacher.1.refs_0_, f32[8,128]{1,0:T(8,128)S(1)} %collective-permute-done.13.refs_1_, ...), custom_call_target="tpu_custom_call" | custom-call | tf_op jit(solution)/shard_map/final/pallas_call | solution.py:516
  (2 shorter events, 0.1 us)
Async XLA Ops:
  0.6 13.5 %copy-start.1 = (bf16[1,2048,176]{1,2,0:T(8,128)(2,1)S(1)}, bf16[1,2048,176]{1,2,0:T(8,128)(2,1)}, u32[]{:S(2)}) copy-start(bf16[1,2048,176]{1,2,0:T(8,128)(2,1)} %param.15) | copy-start | bytes 2162692
  2.3 11.8 %copy-start = (bf16[1,2048,176]{1,2,0:T(8,128)(2,1)S(1)}, bf16[1,2048,176]{1,2,0:T(8,128)(2,1)}, u32[]{:S(2)}) copy-start(bf16[1,2048,176]{1,2,0:T(8,128)(2,1)} %param.14) | copy-start | bytes 2162692
  2.3 7.4 %collective-permute-start.2 = (bf16[32,2048]{1,0:T(8,128)(2,1)S(1)}, bf16[32,2048]{1,0:T(8,128)(2,1)S(1)}, u32[]{:S(2)}, u32[]{:S(2)}) collective-permute-start(bf16[32,2048]{1,0:T(8,128)(2,1)S(1)} %get-tuple-element.30.rows_a), channel_id=1, source_target_pairs={{0,2},{1,3},{2,0},{3,1},{4,6},{5,7},{6,4},{7,5},{8,10},{9,11},{10,... | collective-permute-start | bytes 393224 | tf_op jit(solution)/shard_map/ppermute | solution.py:37
  5.3 6.3 %collective-permute-start.8 = (bf16[32,2048]{1,0:T(8,128)(2,1)S(1)}, bf16[32,2048]{1,0:T(8,128)(2,1)S(1)}, u32[]{:S(2)}, u32[]{:S(2)}) collective-permute-start(bf16[32,2048]{1,0:T(8,128)(2,1)S(1)} %get-tuple-element.41.scaled_a), channel_id=1, source_target_pairs={{0,2},{1,3},{2,0},{3,1},{4,6},{5,7},{6,4},{7,5},{8,10},{9,11},{10,... | collective-permute-start | bytes 393224 | tf_op jit(solution)/shard_map/ppermute | solution.py:37
  9.7 4.4 %collective-permute-start.3 = (bf16[32,2048]{1,0:T(8,128)(2,1)S(1)}, bf16[32,2048]{1,0:T(8,128)(2,1)S(1)}, u32[]{:S(2)}, u32[]{:S(2)}) collective-permute-start(bf16[32,2048]{1,0:T(8,128)(2,1)S(1)} %collective-permute-done.2.rows_a), channel_id=1, source_target_pairs={{0,1},{1,0},{2,3},{3,2},{4,5},{5,4},{6,7},{7,6},{8,9},{9,8},{10,11... | collective-permute-start | bytes 393224 | tf_op jit(solution)/shard_map/ppermute | solution.py:37
  11.6 3.3 %collective-permute-start.9 = (bf16[32,2048]{1,0:T(8,128)(2,1)S(1)}, bf16[32,2048]{1,0:T(8,128)(2,1)S(1)}, u32[]{:S(2)}, u32[]{:S(2)}) collective-permute-start(bf16[32,2048]{1,0:T(8,128)(2,1)S(1)} %collective-permute-done.8.scaled_a), channel_id=1, source_target_pairs={{0,1},{1,0},{2,3},{3,2},{4,5},{5,4},{6,7},{7,6},{8,9},{9,8},{10,11... | collective-permute-start | bytes 393224 | tf_op jit(solution)/shard_map/ppermute | solution.py:37
  11.6 6.7 %collective-permute-start = (bf16[32,2048]{1,0:T(8,128)(2,1)S(1)}, bf16[32,2048]{1,0:T(8,128)(2,1)S(1)}, u32[]{:S(2)}, u32[]{:S(2)}) collective-permute-start(bf16[32,2048]{1,0:T(8,128)(2,1)S(1)} %get-tuple-element.30.rows_a), channel_id=1, source_target_pairs={{0,1},{1,0},{2,3},{3,2},{4,5},{5,4},{6,7},{7,6},{8,9},{9,8},{10,11... | collective-permute-start | bytes 393224 | tf_op jit(solution)/shard_map/ppermute | solution.py:37
  12.1 7.0 %collective-permute-start.6 = (bf16[32,2048]{1,0:T(8,128)(2,1)S(1)}, bf16[32,2048]{1,0:T(8,128)(2,1)S(1)}, u32[]{:S(2)}, u32[]{:S(2)}) collective-permute-start(bf16[32,2048]{1,0:T(8,128)(2,1)S(1)} %get-tuple-element.41.scaled_a), channel_id=1, source_target_pairs={{0,1},{1,0},{2,3},{3,2},{4,5},{5,4},{6,7},{7,6},{8,9},{9,8},{10,11... | collective-permute-start | bytes 393224 | tf_op jit(solution)/shard_map/ppermute | solution.py:37
  14.9 1.6 %copy-start.2 = (bf16[1,8,37984]{2,1,0:T(8,128)(2,1)S(1)}, bf16[1,8,37984]{2,1,0:T(8,128)(2,1)}, u32[]{:S(2)}) copy-start(bf16[1,8,37984]{2,1,0:T(8,128)(2,1)} %param.18) | copy-start | bytes 1823236
  15.9 4.8 %collective-permute-start.10 = (bf16[32,2048]{1,0:T(8,128)(2,1)S(1)}, bf16[32,2048]{1,0:T(8,128)(2,1)S(1)}, u32[]{:S(2)}, u32[]{:S(2)}) collective-permute-start(bf16[32,2048]{1,0:T(8,128)(2,1)S(1)} %get-tuple-element.49), channel_id=1, source_target_pairs={{0,1},{1,0},{2,3},{3,2},{4,5},{5,4},{6,7},{7,6},{8,9},{9,8},{10,11... | collective-permute-start | bytes 393224 | tf_op jit(solution)/shard_map/ppermute | solution.py:37
  16.5 18.8 %collective-permute-start.12 = (bf16[8,37984]{1,0:T(8,128)(2,1)S(1)}, bf16[8,37984]{1,0:T(8,128)(2,1)S(1)}, u32[]{:S(2)}, u32[]{:S(2)}) collective-permute-start(bf16[8,37984]{1,0:T(8,128)(2,1)S(1)} %bitcast.26), channel_id=1, source_target_pairs={{0,4},{4,8},{8,12},{12,16},{16,20},{20,24},{24,28},{28,0},{1,5},{5... | collective-permute-start | bytes 1823240 | tf_op jit(solution)/shard_map/ppermute | solution.py:42
  20.1 15.7 %collective-permute-start.7 = (bf16[32,2048]{1,0:T(8,128)(2,1)S(1)}, bf16[32,2048]{1,0:T(8,128)(2,1)S(1)}, u32[]{:S(2)}, u32[]{:S(2)}) collective-permute-start(bf16[32,2048]{1,0:T(8,128)(2,1)S(1)} %get-tuple-element.45), channel_id=1, source_target_pairs={{0,1},{1,0},{2,3},{3,2},{4,5},{5,4},{6,7},{7,6},{8,9},{9,8},{10,11... | collective-permute-start | bytes 393224 | tf_op jit(solution)/shard_map/ppermute | solution.py:37
  20.2 19.7 %collective-permute-start.1 = (bf16[32,2048]{1,0:T(8,128)(2,1)S(1)}, bf16[32,2048]{1,0:T(8,128)(2,1)S(1)}, u32[]{:S(2)}, u32[]{:S(2)}) collective-permute-start(bf16[32,2048]{1,0:T(8,128)(2,1)S(1)} %get-tuple-element.33), channel_id=1, source_target_pairs={{0,1},{1,0},{2,3},{3,2},{4,5},{5,4},{6,7},{7,6},{8,9},{9,8},{10,11... | collective-permute-start | bytes 393224 | tf_op jit(solution)/shard_map/ppermute | solution.py:37
  20.7 1.7 %collective-permute-start.4 = (bf16[32,2048]{1,0:T(8,128)(2,1)S(1)}, bf16[32,2048]{1,0:T(8,128)(2,1)S(1)}, u32[]{:S(2)}, u32[]{:S(2)}) collective-permute-start(bf16[32,2048]{1,0:T(8,128)(2,1)S(1)} %get-tuple-element.35), channel_id=1, source_target_pairs={{0,1},{1,0},{2,3},{3,2},{4,5},{5,4},{6,7},{7,6},{8,9},{9,8},{10,11... | collective-permute-start | bytes 393224 | tf_op jit(solution)/shard_map/ppermute | solution.py:37
  20.8 16.6 %collective-permute-start.11 = (bf16[32,2048]{1,0:T(8,128)(2,1)S(1)}, bf16[32,2048]{1,0:T(8,128)(2,1)S(1)}, u32[]{:S(2)}, u32[]{:S(2)}) collective-permute-start(bf16[32,2048]{1,0:T(8,128)(2,1)S(1)} %add_convert_fusion), channel_id=1, source_target_pairs={{0,2},{1,3},{2,0},{3,1},{4,6},{5,7},{6,4},{7,5},{8,10},{9,11},{10,... | collective-permute-start | bytes 393224 | tf_op jit(solution)/shard_map/ppermute | solution.py:37
  22.4 17.5 %collective-permute-start.5 = (bf16[32,2048]{1,0:T(8,128)(2,1)S(1)}, bf16[32,2048]{1,0:T(8,128)(2,1)S(1)}, u32[]{:S(2)}, u32[]{:S(2)}) collective-permute-start(bf16[32,2048]{1,0:T(8,128)(2,1)S(1)} %add_convert_fusion.1), channel_id=1, source_target_pairs={{0,2},{1,3},{2,0},{3,1},{4,6},{5,7},{6,4},{7,5},{8,10},{9,11},{10,... | collective-permute-start | bytes 393224 | tf_op jit(solution)/shard_map/ppermute | solution.py:37
  35.9 5.1 %collective-permute-start.13 = (f32[8,128]{1,0:T(8,128)S(1)}, f32[8,128]{1,0:T(8,128)S(1)}, u32[]{:S(2)}, u32[]{:S(2)}) collective-permute-start(f32[8,128]{1,0:T(8,128)S(1)} %teacher.1.refs_0_), channel_id=1, source_target_pairs={{0,1},{1,2},{2,3},{3,0},{4,5},{5,6},{6,7},{7,4},{8,9},{9,10},{10,1... | collective-permute-start | bytes 12296 | tf_op jit(solution)/shard_map/ppermute | solution.py:475
  35.9 5.1 %collective-permute-start.14 = (f32[8,128]{1,0:T(8,128)S(1)}, f32[8,128]{1,0:T(8,128)S(1)}, u32[]{:S(2)}, u32[]{:S(2)}) collective-permute-start(f32[8,128]{1,0:T(8,128)S(1)} %teacher.1.refs_0_), channel_id=1, source_target_pairs={{0,2},{1,3},{2,0},{3,1},{4,6},{5,7},{6,4},{7,5},{8,10},{9,11},{10,... | collective-permute-start | bytes 12296 | tf_op jit(solution)/shard_map/ppermute | solution.py:475
  37.4 3.6 %collective-permute-start.15 = (f32[8,128]{1,0:T(8,128)S(1)}, f32[8,128]{1,0:T(8,128)S(1)}, u32[]{:S(2)}, u32[]{:S(2)}) collective-permute-start(f32[8,128]{1,0:T(8,128)S(1)} %teacher.1.refs_0_), channel_id=1, source_target_pairs={{0,3},{1,0},{2,1},{3,2},{4,7},{5,4},{6,5},{7,6},{8,11},{9,8},{10,9... | collective-permute-start | bytes 12296 | tf_op jit(solution)/shard_map/ppermute | solution.py:475

commit v3 on v2

--- a/solution.py
+++ b/solution.py
@@ -1,4 +1,5 @@
 import functools
+import math
 
 import jax
 import jax.numpy as jnp
@@ -52,31 +53,15 @@
     return copies
 
 
-def prepare_kernel(
-    n_window,
-    ids_hbm,
-    prob_hbm,
-    tokens_hbm,
-    cot_hbm,
-    rows,
-    scaled,
-    slot_cot,
-    select,
-    slot_prob,
-    ids_out,
-    ids,
-    prob,
-    tokens,
-    cot,
-    sems,
-):
-    copies = fetched(
-        (ids_hbm, prob_hbm, tokens_hbm, cot_hbm), (ids, prob, tokens, cot), sems
-    )
+def prepare_kernel(n_window, held, *refs):
+    taken = 4 + held
+    sources, refs = refs[:taken], refs[taken:]
+    rows, scaled, slot_cot, select, slot_prob, ids = refs[:6]
+    kept, (prob, tokens, cot, sems) = refs[6 : 6 + held], refs[6 + held :]
+    copies = fetched(sources, (ids, prob, tokens, cot, *kept), sems)
     copies[0].wait()
     copies[1].wait()
     all_ids = ids[...]
-    ids_out[...] = all_ids
     count = all_ids.shape[1]
     before = (
         lax.broadcasted_iota(jnp.int32, (count, count), 0)
@@ -110,14 +95,16 @@
         scaled[part, :] = (weight * cot_rows).astype(jnp.bfloat16)
         select[part, :] = chosen_f
         slot_prob[part, :] = jnp.broadcast_to(weight, (CAP, LANES))
-
-
-def prepare(ids, prob, tokens, cot, n_window):
+    for copy in copies[4:]:
+        copy.wait()
+
+
+def prepare(ids, prob, tokens, cot, held, n_window):
     count, width = tokens.shape
     slots = n_window * CAP
     wide = jax.ShapeDtypeStruct((slots, width), jnp.bfloat16)
     return pl.pallas_call(
-        functools.partial(prepare_kernel, n_window),
+        functools.partial(prepare_kernel, n_window, len(held)),
         out_shape=(
             wide,
             wide,
@@ -125,19 +112,20 @@
             jax.ShapeDtypeStruct((slots, count), jnp.float32),
             jax.ShapeDtypeStruct((slots, LANES), jnp.float32),
             jax.ShapeDtypeStruct(ids.shape, ids.dtype),
+            *[jax.ShapeDtypeStruct(value.shape, value.dtype) for value in held],
         ),
-        in_specs=hbm(4),
-        out_specs=tuple(vmem(6)),
+        in_specs=hbm(4 + len(held)),
+        out_specs=tuple(vmem(6 + len(held))),
         scratch_shapes=[
-            pltpu.VMEM(ids.shape, ids.dtype),
             pltpu.VMEM(prob.shape, prob.dtype),
             pltpu.VMEM(tokens.shape, tokens.dtype),
             pltpu.VMEM(cot.shape, cot.dtype),
-            pltpu.SemaphoreType.DMA((4,)),
+            pltpu.SemaphoreType.DMA((4 + len(held),)),
         ],
         compiler_params=params(8),
+        cost_estimate=pl.CostEstimate(flops=20000000000, bytes_accessed=0, transcendentals=0),
         name="prepare",
-    )(*in_hbm(ids, prob, tokens, cot))
+    )(*in_hbm(ids, prob, tokens, cot, *held))
 
 
 def forward_math(rows, gate_w, up_w, down_w):
@@ -224,9 +212,10 @@
     return total
 
 
-def combine_out_kernel(n_window, parts, *refs):
-    outs = refs[:parts]
-    ids, select, slot_prob, slot_cot, layer_out, prob_grad, stage, prob_stage, sems = refs[parts:]
+def combine_kernel(n_window, parts, *refs):
+    outs, grads = refs[:parts], refs[parts : 2 * parts]
+    ids, select, slot_prob, slot_cot, layer_out, input_grad, prob_grad = refs[2 * parts : -4]
+    out_stage, grad_stage, prob_stage, sems = refs[-4:]
     exact = n_window == 1
     chosen = select[...]
     weight = slot_prob[:, :1]
@@ -234,6 +223,12 @@
     block = min(BLOCK, width)
     blocks = width // block
     copies = []
+
+    def send(source, target):
+        copy = pltpu.make_async_copy(source, target, sems.at[len(copies)])
+        copy.start()
+        copies.append(copy)
+
     per_slot = jnp.zeros((chosen.shape[0], 1), jnp.float32)
     for k in range(blocks):
         part = pl.ds(k * block, block)
@@ -241,79 +236,42 @@
         per_slot = per_slot + jnp.sum(
             out * slot_cot[:, part].astype(jnp.float32), axis=1, keepdims=True
         )
-        stage[:, part] = spread(chosen, weight * out, exact).astype(jnp.bfloat16)
-        copy = pltpu.make_async_copy(stage.at[:, part], layer_out.at[:, part], sems.at[k])
-        copy.start()
-        copies.append(copy)
+        out_stage[:, part] = spread(chosen, weight * out, exact).astype(jnp.bfloat16)
+        send(out_stage.at[:, part], layer_out.at[:, part])
     spread_prob = chosen * per_slot
     for e in range(n_window):
         per_token = jnp.sum(spread_prob[e * CAP : (e + 1) * CAP], axis=0, keepdims=True)
         kept = jnp.where(ids[...] == e, per_token, 0.0)
         whole = kept if e == 0 else whole + kept
     prob_stage[...] = whole
-    copy = pltpu.make_async_copy(prob_stage, prob_grad, sems.at[blocks])
-    copy.start()
-    copies.append(copy)
+    send(prob_stage, prob_grad)
+    for k in range(blocks):
+        part = pl.ds(k * block, block)
+        grad_stage[:, part] = spread(chosen, summed(grads, part), exact).astype(jnp.bfloat16)
+        send(grad_stage.at[:, part], input_grad.at[:, part])
     for copy in copies:
         copy.wait()
 
 
-def combine_grad_kernel(n_window, parts, *refs):
-    grads = refs[:parts]
-    select, input_grad, stage, sems = refs[parts:]
-    exact = n_window == 1
-    chosen = select[...]
-    width = grads[0].shape[1]
-    block = min(BLOCK, width)
-    copies = []
-    for k in range(width // block):
-        part = pl.ds(k * block, block)
-        stage[:, part] = spread(chosen, summed(grads, part), exact).astype(jnp.bfloat16)
-        copy = pltpu.make_async_copy(stage.at[:, part], input_grad.at[:, part], sems.at[k])
-        copy.start()
-        copies.append(copy)
-    for copy in copies:
-        copy.wait()
-
-
-def combine_out(outs, ids, select, slot_prob, slot_cot, n_window):
+def combine(outs, grads, ids, select, slot_prob, slot_cot, n_window):
     parts = len(outs)
     width = outs[0].shape[1]
     topk, count = ids.shape
-    return pl.pallas_call(
-        functools.partial(combine_out_kernel, n_window, parts),
-        out_shape=(
-            jax.ShapeDtypeStruct((count, width), jnp.bfloat16),
-            jax.ShapeDtypeStruct((topk, count), jnp.float32),
-        ),
-        in_specs=vmem(parts + 4),
-        out_specs=tuple(hbm(2)),
+    wide = jax.ShapeDtypeStruct((count, width), jnp.bfloat16)
+    return pl.pallas_call(
+        functools.partial(combine_kernel, n_window, parts),
+        out_shape=(wide, wide, jax.ShapeDtypeStruct((topk, count), jnp.float32)),
+        in_specs=vmem(2 * parts + 4),
+        out_specs=tuple(hbm(3)),
         scratch_shapes=[
             pltpu.VMEM((count, width), jnp.bfloat16),
+            pltpu.VMEM((count, width), jnp.bfloat16),
             pltpu.VMEM((topk, count), jnp.float32),
-            pltpu.SemaphoreType.DMA((width // min(BLOCK, width) + 1,)),
+            pltpu.SemaphoreType.DMA((2 * (width // min(BLOCK, width)) + 1,)),
         ],
         compiler_params=params(12),
-        name="combine_out",
-    )(*outs, ids, select, slot_prob, slot_cot)
-
-
-def combine_grad(grads, select, n_window):
-    parts = len(grads)
-    width = grads[0].shape[1]
-    count = select.shape[1]
-    return pl.pallas_call(
-        functools.partial(combine_grad_kernel, n_window, parts),
-        out_shape=jax.ShapeDtypeStruct((count, width), jnp.bfloat16),
-        in_specs=vmem(parts + 1),
-        out_specs=hbm(1)[0],
-        scratch_shapes=[
-            pltpu.VMEM((count, width), jnp.bfloat16),
-            pltpu.SemaphoreType.DMA((width // min(BLOCK, width),)),
-        ],
-        compiler_params=params(12),
-        name="combine_grad",
-    )(*grads, select)
+        name="combine",
+    )(*outs, *grads, ids, select, slot_prob, slot_cot)
 
 
 def spans(width, parts):
@@ -373,27 +331,12 @@
     )
 
 
-def student_kernel(base, labels_hbm, student_hbm, down_hbm, stats, student, down, labels, sems):
+def student_kernel(base, labels, student, stats):
     rows, width = student.shape
-    parts = spans(width, 4)
-    copies = fetched((labels_hbm,), (labels,), sems)
-    for k, (start, size) in enumerate(parts):
-        part = pl.ds(start, size)
-        copy = pltpu.make_async_copy(
-            student_hbm.at[:, part], student.at[:, part], sems.at[k + 1]
-        )
-        copy.start()
-        copies.append(copy)
-    weight = pltpu.make_async_copy(down_hbm, down, sems.at[len(parts) + 1])
-    weight.start()
-    copies[0].wait()
     spread_out = jnp.where(diagonal(rows), jnp.broadcast_to(labels[...], (rows, rows)), 0)
     label = jnp.sum(spread_out.astype(jnp.float32), axis=1, keepdims=True).astype(jnp.int32)
     label = label - base[0]
-    top = jnp.full((rows, 1), -jnp.inf, jnp.float32)
-    for copy, (start, size) in zip(copies[1:], parts):
-        copy.wait()
-        top = row_max(student, start, size, top)
+    top = row_max(student, 0, width, jnp.full((rows, 1), -jnp.inf, jnp.float32))
 
     def step(at, size):
         value = load(student, at, size)
@@ -405,7 +348,6 @@
     stats[...] = columns(
         (top, total, picked, zero, zero, zero, label.astype(jnp.float32)), rows
     )
-    weight.wait()
 
 
 def teacher_kernel(student, teacher, student_stats, stats):
@@ -415,8 +357,8 @@
     def step(at, size):
         ours = load(student, at, size)
         theirs = load(teacher, at, size)
-        power = jnp.exp(theirs - top)
-        return power, power * (theirs - ours)
+        high = jnp.exp(theirs - top)
+        return high, high * (theirs - ours)
 
     total, cross = row_sums(width, step)
     lane = lax.broadcasted_iota(jnp.int32, (rows, LANES), 1)
@@ -426,33 +368,60 @@
     stats[...] = jnp.where(lane == 5, cross, tile)
 
 
-def final_kernel(parts, student, teacher, *refs):
-    stats, (loss, grad, stage, loss_stage, sems) = refs[:parts], refs[parts:]
+def joined(one, two):
+    lane = lax.broadcasted_iota(jnp.int32, one.shape, 1)
+    student = lane < 2
+    top_one = jnp.where(student, one[:, 0:1], one[:, 3:4])
+    top_two = jnp.where(student, two[:, 0:1], two[:, 3:4])
+    top = jnp.maximum(top_one, top_two)
+    scaled = one * jnp.exp(top_one - top) + two * jnp.exp(top_two - top)
+    tile = jnp.where((lane == 0) | (lane == 3), top, scaled)
+    tile = jnp.where(lane == 2, one + two, tile)
+    return jnp.where(lane == 6, one, tile)
+
+
+def joined_all(tiles):
+    while len(tiles) > 1:
+        pairs = [joined(*tiles[k : k + 2]) for k in range(0, len(tiles) - 1, 2)]
+        tiles = pairs + tiles[2 * len(pairs) :]
+    return tiles[0]
+
+
+def join_kernel(*refs):
+    refs[-1][...] = joined_all([ref[...] for ref in refs[:-1]])
+
+
+def join(tiles):
+    return pl.pallas_call(
+        join_kernel,
+        out_shape=jax.ShapeDtypeStruct(tiles[0].shape, tiles[0].dtype),
+        in_specs=vmem(len(tiles)),
+        out_specs=vmem(1)[0],
+        compiler_params=params(1),
+        name="join",
+    )(*tiles)
+
+
+def final_kernel(student, teacher, *refs):
+    tiles, (loss, grad, stage, loss_stage, sems) = refs[:-5], refs[-5:]
     rows, width = student.shape
-    tiles = [ref[...] for ref in stats]
+    tile = joined_all([ref[...] for ref in tiles])
+    smax, ssum, picked = tile[:, 0:1], tile[:, 1:2], tile[:, 2:3]
+    tmax, tsum, cross = tile[:, 3:4], tile[:, 4:5], tile[:, 5:6]
     label = tiles[0][:, 6:7].astype(jnp.int32)
-    top = functools.reduce(jnp.maximum, tiles)
-    smax, tmax = top[:, 0:1], top[:, 3:4]
-    ssum = tsum = cross = picked = jnp.zeros((rows, 1), jnp.float32)
-    for tile in tiles:
-        ssum = ssum + tile[:, 1:2] * jnp.exp(tile[:, 0:1] - smax)
-        scale = jnp.exp(tile[:, 3:4] - tmax)
-        tsum = tsum + tile[:, 4:5] * scale
-        cross = cross + tile[:, 5:6] * scale
-        picked = picked + tile[:, 2:3]
     lse_s = smax + jnp.log(ssum)
     lse_t = tmax + jnp.log(tsum)
+    half_s = lse_s - math.log(2.0)
     value = 2.0 * lse_s - picked + cross / tsum - lse_t
     loss_stage[...] = jnp.sum(jnp.where(diagonal(rows), value, 0.0), axis=0, keepdims=True)
     copies = fetched((loss_stage,), (loss,), sems)
-    for k, (start, size) in enumerate(spans(width, 4)):
+    for k, (start, size) in enumerate(spans(width, 20)):
         for at, span in chunks(start, size):
             here = lax.broadcasted_iota(jnp.int32, (rows, span), 1) == label - at
-            result = (
-                2.0 * jnp.exp(load(student, at, span) - lse_s)
-                - here.astype(jnp.float32)
-                - jnp.exp(load(teacher, at, span) - lse_t)
-            )
+            part = pl.ds(at, span)
+            twice = jnp.exp(load(student, at, span) - half_s)
+            result = twice - jnp.exp(load(teacher, at, span) - lse_t)
+            result = jnp.where(here, result - 1.0, result)
             stage[:, pl.ds(at, span)] = result.astype(jnp.bfloat16)
         part = pl.ds(start, size)
         copy = pltpu.make_async_copy(stage.at[:, part], grad.at[:, part], sems.at[k + 1])
@@ -462,40 +431,37 @@
         copy.wait()
 
 
-def distill(student, stale, labels, down_w):
-    _, width = student.shape
-    teacher = onward(stale, "peer")
-    base = (lax.axis_index("grp") * width).astype(jnp.int32).reshape(1)
-    own, student, down_w = student_stats(base, labels, student, down_w)
+def distill(student, teacher, labels):
+    base = (lax.axis_index("grp") * student.shape[1]).astype(jnp.int32).reshape(1)
+    own = student_stats(base, labels, student)
     stats = teacher_stats(student, teacher, own)
-    count = lax.axis_size("grp")
-    others = []
-    for s in range(1, count):
-        others.append(
-            lax.ppermute(stats, "grp", [(k, (k + s) % count) for k in range(count)])
-        )
-    loss, grad = finish(student, teacher, [stats, *others])
-    return loss, grad, down_w
-
-
-def student_stats(base, labels, student, down_w):
-    rows, width = student.shape
+    tiles = exchanged(stats, 1)
+    bits = 4
+    while bits < lax.axis_size("grp"):
+        stats = join(tiles)
+        tiles = exchanged(stats, bits)
+        bits = 4 * bits
+    loss, grad = finish(student, teacher, tiles)
+    return loss, grad
+
+
+def exchanged(tile, bits):
+    tiles = [tile]
+    for k in (1, 2, 3):
+        if k * bits < lax.axis_size("grp"):
+            tiles.append(swapped(tile, "grp", k * bits))
+    return tiles
+
+
+def student_stats(base, labels, student):
     return pl.pallas_call(
         student_kernel,
-        out_shape=(
-            jax.ShapeDtypeStruct((rows, LANES), jnp.float32),
-            jax.ShapeDtypeStruct(student.shape, student.dtype),
-            jax.ShapeDtypeStruct(down_w.shape, down_w.dtype),
-        ),
-        in_specs=[pl.BlockSpec(memory_space=pltpu.SMEM)] + hbm(3),
-        out_specs=tuple(vmem(3)),
-        scratch_shapes=[
-            pltpu.VMEM(labels.shape, labels.dtype),
-            pltpu.SemaphoreType.DMA((len(spans(width, 4)) + 2,)),
-        ],
+        out_shape=jax.ShapeDtypeStruct((student.shape[0], LANES), jnp.float32),
+        in_specs=[pl.BlockSpec(memory_space=pltpu.SMEM)] + vmem(2),
+        out_specs=vmem(1)[0],
         compiler_params=params(8),
         name="student",
-    )(base, *in_hbm(labels, student, down_w))
+    )(base, labels, student)
 
 
 def teacher_stats(student, teacher, own):
@@ -510,25 +476,24 @@
     )(student, teacher, own)
 
 
-def finish(student, teacher, stats):
+def finish(student, teacher, tiles):
     rows, width = student.shape
-    count = len(stats)
-    return pl.pallas_call(
-        functools.partial(final_kernel, count),
+    return pl.pallas_call(
+        final_kernel,
         out_shape=(
             jax.ShapeDtypeStruct((1, rows), jnp.float32),
             jax.ShapeDtypeStruct((rows, width), jnp.bfloat16),
         ),
-        in_specs=vmem(2 + count),
+        in_specs=vmem(2 + len(tiles)),
         out_specs=tuple(hbm(2)),
         scratch_shapes=[
             pltpu.VMEM((rows, width), jnp.bfloat16),
             pltpu.VMEM((1, rows), jnp.float32),
-            pltpu.SemaphoreType.DMA((len(spans(width, 4)) + 1,)),
+            pltpu.SemaphoreType.DMA((len(spans(width, 20)) + 1,)),
         ],
         compiler_params=params(8),
         name="final",
-    )(student, teacher, *stats)
+    )(student, teacher, *tiles)
 
 
 def between_blocks(value, n_window):
@@ -540,8 +505,7 @@
     )
 
 
-def layer(tokens, cotangent, ids, prob, weights, n_window):
-    rows, scaled, slot_cot, select, slot_prob, ids = prepare(ids, prob, tokens, cotangent, n_window)
+def layer(rows, scaled, slot_cot, select, slot_prob, ids, weights, n_window):
     rows = between_blocks(rows, n_window)
     scaled = between_blocks(scaled, n_window)
     rows_far = swapped(rows, "grp", 2)
@@ -565,9 +529,7 @@
 
     outs = collected([out_own, out_back, out_home], n_window)
     grads = collected([grad_own, grad_back, grad_home], n_window)
-    layer_out, prob_grad = combine_out(outs, ids, select, slot_prob, slot_cot, n_window)
-    input_grad = combine_grad(grads, select, n_window)
-    return layer_out, input_grad, prob_grad
+    return combine(outs, grads, ids, select, slot_prob, slot_cot, n_window)
 
 
 def pair_sum(one, two):
@@ -594,17 +556,14 @@
     labels,
 ):
     n_window = lax.axis_size("grp") // PIECES
-    distill_loss, logit_grad, down_w = distill(
-        student_logits[0], stale_logits[0], labels, w_down[0]
+    teacher = onward(stale_logits[0], "peer")
+    held = (labels,)
+    *slots, labels = prepare(
+        expert_ids.T, route_prob.T, tokens, cotangent, held, n_window
     )
-    layer_out, input_grad, prob_grad = layer(
-        tokens,
-        cotangent,
-        expert_ids.T,
-        route_prob.T,
-        (w_gate[0].T, w_up[0].T, down_w),
-        n_window,
-    )
+    gate_w, up_w, down_w, student = (w_gate[0].T, w_up[0].T, w_down[0], student_logits[0])
+    layer_out, input_grad, prob_grad = layer(*slots, (gate_w, up_w, down_w), n_window)
+    distill_loss, logit_grad = distill(student, teacher, labels)
     return (layer_out, input_grad, prob_grad.T, distill_loss, logit_grad[None])
 
 

time: 42.7 us -> 38.5 us (0.902)
  Pallas kernels: 11.4 us -> 9.36 us
  waiting for transfers between devices: 17.9 us -> 16.7 us
  starting transfers between devices: 12.4 us -> 11.4 us
    ppermute x3 -> x0, starting transfers between devices: 2.96 us -> none  [distill(): lax.ppermute(stats, 'grp', [(k, (k + s) % count) for k in range(count)])]
    pallas_call x5 -> x4, Pallas kernels: 7.23 us -> 5.21 us  [the longest x1 1.7 us: prepare(): pl.pallas_call(functools.partial(prepare_kernel, n_window, len(held)), ou...]
    ppermute x12 -> x15, starting transfers between devices: 7.64 us -> 9.62 us  [swapped(): return lax.ppermute(value, axis, [(k, k ^ bits) for k in range(count)])]
    ppermute x1, waiting for transfers between devices: 11.6 us -> 10 us  [onward(): lax.ppermute(value, axis, [(k, (k + 1) % count) for k in range(count)])]
    ppermute x12 -> x15, waiting for transfers between devices: 6.25 us -> 6.69 us  [swapped(): return lax.ppermute(value, axis, [(k, k ^ bits) for k in range(count)])]
  transfers between devices with their start and end apart: 16 -> 16, of which waited for: 3 -> 4; matrix products, arithmetic and copies ran while one was open for 0% -> 0% of each run, Pallas kernels for 19% -> 16%
where the time goes in v3:
time: 38.5 us; the launch traced here: 38.3 us
  waiting for transfers between devices  16.7 us (43%)
  starting transfers between devices  11.4 us (30%)
  Pallas kernels  9.36 us (24%)
  between operations  0.79 us (2%)
    ppermute x1, waiting for transfers between devices, onward(): lax.ppermute(value, axis, [(k, (k + 1) % count) for k in range(count)])  10 us
    ppermute x15, starting transfers between devices, swapped(): return lax.ppermute(value, axis, [(k, k ^ bits) for k in range(count)])  9.62 us
    ppermute x15, waiting for transfers between devices, swapped(): return lax.ppermute(value, axis, [(k, k ^ bits) for k in range(count)])  6.69 us
    pallas_call x2, Pallas kernels, backward(): pl.pallas_call(backward_kernel, out_shape=(part, part), in_specs=vmem(7),...  1.97 us
    ppermute x1, starting transfers between devices, onward(): lax.ppermute(value, axis, [(k, (k + 1) % count) for k in range(count)])  1.76 us
    pallas_call x1, Pallas kernels, prepare(): pl.pallas_call(functools.partial(prepare_kernel, n_window, len(held)), ou...  1.7 us
    pallas_call x1, Pallas kernels, finish(): pl.pallas_call(final_kernel, out_shape=(jax.ShapeDtypeStruct((1, rows), j...  1.64 us
    pallas_call x2, Pallas kernels, forward(): pl.pallas_call(forward_kernel, out_shape=(part, part, act, act), in_specs...  1.63 us
  transfers between devices with their start and end apart: 16, of which 4 were waited for; matrix products, arithmetic and copies ran while one was open for 0% of the time, Pallas kernels for 16%

profile of v3, /device:TPU:0, one launch (start us, length us, event | category | flops | bytes accessed | tf_op | source)
XLA Modules:
  0.0 38.3 jit_solution(10629704188724549669)
XLA Ops:
  0.6 0.0 copy-start
  0.6 0.0 copy-start.1
  0.7 0.0 copy-start.2
  0.7 1.7 %prepare.1 = (bf16[32,2048]{1,0:T(8,128)(2,1)S(1)}, bf16[32,2048]{1,0:T(8,128)(2,1)S(1)}, bf16[32,2048]{1,0:T(8,128)(2,1)S(1)}, f32[32,128]{1,0:T(8,128)S(1)}, f...) custom-call(s32[4,128]{1,0:T(4,128)} %bitcast.31, f32[4,128]{1,0:T(4,128)} %bitcast.32, ...), custom_call_target="tpu_custom_call" | custom-call | flops 20000000000 | tf_op jit(solution)/shard_map/prepare/pallas_call | solution.py:106
  2.4 3.0 %collective-permute-start.2 = (bf16[32,2048]{1,0:T(8,128)(2,1)S(1)}, bf16[32,2048]{1,0:T(8,128)(2,1)S(1)}, u32[]{:S(2)}, u32[]{:S(2)}) collective-permute-start(bf16[32,2048]{1,0:T(8,128)(2,1)S(1)} %get-tuple-element.29.rows_a), channel_id=1, source_target_pairs={{0,2},{1,3},{2,0},{3,1},{4,6},{5,7},{6,4},{7,5},{8,10},{9,11},{10,... | collective-permute-start | bytes 393224 | tf_op jit(solution)/shard_map/ppermute | solution.py:38
  5.4 0.1 collective-permute-start.8
  5.5 4.3 %collective-permute-done.2.rows_a = bf16[32,2048]{1,0:T(8,128)(2,1)S(1)} collective-permute-done((bf16[32,2048]{1,0:T(8,128)(2,1)S(1)}, bf16[32,2048]{1,0:T(8,128)(2,1)S(1)}, u32[]{:S(2)}, u32[]{:S(2)}) %collective-permute-start.2) | collective-permute-done | bytes 131104 | tf_op jit(solution)/shard_map/ppermute | solution.py:38
  9.8 0.0 collective-permute-start.3
  9.8 0.5 %collective-permute-start = (bf16[32,2048]{1,0:T(8,128)(2,1)S(1)}, bf16[32,2048]{1,0:T(8,128)(2,1)S(1)}, u32[]{:S(2)}, u32[]{:S(2)}) collective-permute-start(bf16[32,2048]{1,0:T(8,128)(2,1)S(1)} %get-tuple-element.29.rows_a), channel_id=1, source_target_pairs={{0,1},{1,0},{2,3},{3,2},{4,5},{5,4},{6,7},{7,6},{8,9},{9,8},{10,11... | collective-permute-start | bytes 393224 | tf_op jit(solution)/shard_map/ppermute | solution.py:38
  10.3 0.0 collective-permute-start.6
  10.3 1.4 %collective-permute-done.8.scaled_a = bf16[32,2048]{1,0:T(8,128)(2,1)S(1)} collective-permute-done((bf16[32,2048]{1,0:T(8,128)(2,1)S(1)}, bf16[32,2048]{1,0:T(8,128)(2,1)S(1)}, u32[]{:S(2)}, u32[]{:S(2)}) %collective-permute-start.8) | collective-permute-done | bytes 131104 | tf_op jit(solution)/shard_map/ppermute | solution.py:38
  11.7 0.0 collective-permute-start.9
  11.7 0.0 collective-permute-done.3.rows_b
  11.7 0.0 copy-done
  11.7 0.0 copy-done.1
  11.7 0.0 copy-done.2
  11.7 0.0 copy-start.4
  11.8 0.8 %forward.3 = (bf16[32,2048]{1,0:T(8,128)(2,1)S(1)}, bf16[32,2048]{1,0:T(8,128)(2,1)S(1)}, f32[64,176]{1,0:T(8,128)S(1)}, f32[64,176]{1,0:T(8,128)S(1)}) custom-call(bf16[32,2048]{1,0:T(8,128)(2,1)S(1)} %collective-permute-done.2.rows_a, bf16[32,2048]{1,0:T(8,128)(2,1)S(1)} %collective-permute-done.3.rows_b, bf16[176,2048]{1,0:T(8,128)(2,1)S(1)} %bitcast.14, ...), custom_call_target="tpu_custom_call" | custom-call | tf_op jit(solution)/shard_map/forward/pallas_call | solution.py:172
  12.6 0.6 %collective-permute-start.4 = (bf16[32,2048]{1,0:T(8,128)(2,1)S(1)}, bf16[32,2048]{1,0:T(8,128)(2,1)S(1)}, u32[]{:S(2)}, u32[]{:S(2)}) collective-permute-start(bf16[32,2048]{1,0:T(8,128)(2,1)S(1)} %get-tuple-element.33), channel_id=1, source_target_pairs={{0,1},{1,0},{2,3},{3,2},{4,5},{5,4},{6,7},{7,6},{8,9},{9,8},{10,11... | collective-permute-start | bytes 393224 | tf_op jit(solution)/shard_map/ppermute | solution.py:38
  13.2 0.0 copy-done.4
  13.2 1.8 %collective-permute-start.12 = (bf16[8,37984]{1,0:T(8,128)(2,1)S(1)}, bf16[8,37984]{1,0:T(8,128)(2,1)S(1)}, u32[]{:S(2)}, u32[]{:S(2)}) collective-permute-start(bf16[8,37984]{1,0:T(8,128)(2,1)S(1)} %bitcast.29), channel_id=1, source_target_pairs={{0,4},{4,8},{8,12},{12,16},{16,20},{20,24},{24,28},{28,0},{1,5},{5... | collective-permute-start | bytes 1823240 | tf_op jit(solution)/shard_map/ppermute | solution.py:43
  14.9 0.0 collective-permute-done.rows_b
  14.9 0.8 %forward.2 = (bf16[32,2048]{1,0:T(8,128)(2,1)S(1)}, bf16[32,2048]{1,0:T(8,128)(2,1)S(1)}, f32[64,176]{1,0:T(8,128)S(1)}, f32[64,176]{1,0:T(8,128)S(1)}) custom-call(bf16[32,2048]{1,0:T(8,128)(2,1)S(1)} %get-tuple-element.29.rows_a, bf16[32,2048]{1,0:T(8,128)(2,1)S(1)} %collective-permute-done.rows_b, bf16[176,2048]{1,0:T(8,128)(2,1)S(1)} %bitcast.15, ...), custom_call_target="tpu_custom_call" | custom-call | tf_op jit(solution)/shard_map/forward/pallas_call | solution.py:172
  15.7 0.1 collective-permute-start.1
  15.8 0.0 collective-permute-done.6.scaled_b
  15.8 1.0 %backward.2 = (bf16[32,2048]{1,0:T(8,128)(2,1)S(1)}, bf16[32,2048]{1,0:T(8,128)(2,1)S(1)}) custom-call(bf16[32,2048]{1,0:T(8,128)(2,1)S(1)} %get-tuple-element.34.scaled_a, bf16[32,2048]{1,0:T(8,128)(2,1)S(1)} %collective-permute-done.6.scaled_b, f32[64,176]{1,0:T(8,128)S(1)} %get-tuple-element.35.gate, f32[64,176]{1,0:T(8,128)S(1)} %get-tuple-element.36.up, ...), custom_call_target="tpu_custom_call" | custom-call | tf_op jit(solution)/shard_map/backward/pallas_call | solution.py:185
  16.8 0.6 %collective-permute-start.7 = (bf16[32,2048]{1,0:T(8,128)(2,1)S(1)}, bf16[32,2048]{1,0:T(8,128)(2,1)S(1)}, u32[]{:S(2)}, u32[]{:S(2)}) collective-permute-start(bf16[32,2048]{1,0:T(8,128)(2,1)S(1)} %get-tuple-element.38), channel_id=1, source_target_pairs={{0,1},{1,0},{2,3},{3,2},{4,5},{5,4},{6,7},{7,6},{8,9},{9,8},{10,11... | collective-permute-start | bytes 393224 | tf_op jit(solution)/shard_map/ppermute | solution.py:38
  17.4 0.0 collective-permute-done.9.scaled_b
  17.4 1.0 %backward.3 = (bf16[32,2048]{1,0:T(8,128)(2,1)S(1)}, bf16[32,2048]{1,0:T(8,128)(2,1)S(1)}) custom-call(bf16[32,2048]{1,0:T(8,128)(2,1)S(1)} %collective-permute-done.8.scaled_a, bf16[32,2048]{1,0:T(8,128)(2,1)S(1)} %collective-permute-done.9.scaled_b, f32[64,176]{1,0:T(8,128)S(1)} %get-tuple-element.39.gate, f32[64,176]{1,0:T(8,128)S(1)} %get-tuple-element.40.up, ...), custom_call_target="tpu_custom_call" | custom-call | tf_op jit(solution)/shard_map/backward/pallas_call | solution.py:185
  18.4 0.0 copy-start.3
  18.4 0.1 collective-permute-start.10
  18.5 0.0 collective-permute-done.4
  18.5 1.6 %collective-permute-start.5 = (bf16[32,2048]{1,0:T(8,128)(2,1)S(1)}, bf16[32,2048]{1,0:T(8,128)(2,1)S(1)}, u32[]{:S(2)}, u32[]{:S(2)}) collective-permute-start(bf16[32,2048]{1,0:T(8,128)(2,1)S(1)} %add_convert_fusion.1), channel_id=1, source_target_pairs={{0,2},{1,3},{2,0},{3,1},{4,6},{5,7},{6,4},{7,5},{8,10},{9,11},{10,... | collective-permute-start | bytes 393224 | tf_op jit(solution)/shard_map/ppermute | solution.py:38
  20.1 0.0 collective-permute-done.10
  20.1 1.3 %collective-permute-start.11 = (bf16[32,2048]{1,0:T(8,128)(2,1)S(1)}, bf16[32,2048]{1,0:T(8,128)(2,1)S(1)}, u32[]{:S(2)}, u32[]{:S(2)}) collective-permute-start(bf16[32,2048]{1,0:T(8,128)(2,1)S(1)} %add_convert_fusion), channel_id=1, source_target_pairs={{0,2},{1,3},{2,0},{3,1},{4,6},{5,7},{6,4},{7,5},{8,10},{9,11},{10,... | collective-permute-start | bytes 393224 | tf_op jit(solution)/shard_map/ppermute | solution.py:38
  21.4 0.0 copy-done.3
  21.4 0.6 %student.1.student_stats = f32[8,128]{1,0:T(8,128)S(1)} custom-call(s32[1]{0:T(128)} %bitcast.12.base, s32[1,8]{1,0:T(1,128)S(1)} %get-tuple-element.50.labels, bf16[8,37984]{1,0:T(8,128)(2,1)S(1)} %bitcast.26), custom_call_target="tpu_custom_call" | custom-call | tf_op jit(solution)/shard_map/student/pallas_call | solution.py:457
  22.0 10.0 %collective-permute-done.12.teacher = bf16[8,37984]{1,0:T(8,128)(2,1)S(1)} collective-permute-done((bf16[8,37984]{1,0:T(8,128)(2,1)S(1)}, bf16[8,37984]{1,0:T(8,128)(2,1)S(1)}, u32[]{:S(2)}, u32[]{:S(2)}) %collective-permute-start.12) | collective-permute-done | bytes 607776 | tf_op jit(solution)/shard_map/ppermute | solution.py:43
  32.0 0.6 %teacher.1.refs_0_ = f32[8,128]{1,0:T(8,128)S(1)} custom-call(bf16[8,37984]{1,0:T(8,128)(2,1)S(1)} %bitcast.27, bf16[8,37984]{1,0:T(8,128)(2,1)S(1)} %collective-permute-done.12.teacher, f32[8,128]{1,0:T(8,128)S(1)} %student.1.student_stats), custom_call_target="tpu_custom_call" | custom-call | tf_op jit(solution)/shard_map/teacher/pallas_call | solution.py:469
  32.6 0.5 %collective-permute-start.15 = (f32[8,128]{1,0:T(8,128)S(1)}, f32[8,128]{1,0:T(8,128)S(1)}, u32[]{:S(2)}, u32[]{:S(2)}) collective-permute-start(f32[8,128]{1,0:T(8,128)S(1)} %teacher.1.refs_0_), channel_id=1, source_target_pairs={{0,3},{1,2},{2,1},{3,0},{4,7},{5,6},{6,5},{7,4},{8,11},{9,10},{10,... | collective-permute-start | bytes 12296 | tf_op jit(solution)/shard_map/ppermute | solution.py:38
  33.1 0.0 collective-permute-done.1.refs_1_
  33.1 1.1 %collective-permute-start.14 = (f32[8,128]{1,0:T(8,128)S(1)}, f32[8,128]{1,0:T(8,128)S(1)}, u32[]{:S(2)}, u32[]{:S(2)}) collective-permute-start(f32[8,128]{1,0:T(8,128)S(1)} %teacher.1.refs_0_), channel_id=1, source_target_pairs={{0,2},{1,3},{2,0},{3,1},{4,6},{5,7},{6,4},{7,5},{8,10},{9,11},{10,... | collective-permute-start | bytes 12296 | tf_op jit(solution)/shard_map/ppermute | solution.py:38
  34.1 0.0 collective-permute-done.7.refs_4_
  34.2 0.3 collective-permute-start.13
  34.4 0.0 collective-permute-done.5.refs_2_
  34.4 0.0 collective-permute-done.11.refs_5_
  34.5 1.3 %combine.1 = (bf16[128,2048]{1,0:T(8,128)(2,1)}, bf16[128,2048]{1,0:T(8,128)(2,1)}, f32[4,128]{1,0:T(4,128)}) custom-call(bf16[32,2048]{1,0:T(8,128)(2,1)S(1)} %get-tuple-element.30.refs_0_, bf16[32,2048]{1,0:T(8,128)(2,1)S(1)} %collective-permute-done.1.refs_1_, bf16[32,2048]{1,0:T(8,128)(2,1)S(1)} %collective-permute-done.5.refs_2_, ...), custom_call_target="tpu_custom_call" | custom-call | tf_op jit(solution)/shard_map/combine/pallas_call | solution.py:261
  35.7 0.0 collective-permute-done.15.refs_3_
  35.8 0.9 %collective-permute-done.14.refs_2_ = f32[8,128]{1,0:T(8,128)S(1)} collective-permute-done((f32[8,128]{1,0:T(8,128)S(1)}, f32[8,128]{1,0:T(8,128)S(1)}, u32[]{:S(2)}, u32[]{:S(2)}) %collective-permute-start.14) | collective-permute-done | bytes 4128 | tf_op jit(solution)/shard_map/ppermute | solution.py:38
  36.7 0.0 collective-permute-done.13.refs_1_
  36.7 1.6 %final.1 = (f32[1,8]{1,0:T(1,128)}, bf16[8,37984]{1,0:T(8,128)(2,1)}) custom-call(bf16[8,37984]{1,0:T(8,128)(2,1)S(1)} %bitcast.28, bf16[8,37984]{1,0:T(8,128)(2,1)S(1)} %collective-permute-done.12.teacher, f32[8,128]{1,0:T(8,128)S(1)} %teacher.1.refs_0_, f32[8,128]{1,0:T(8,128)S(1)} %collective-permute-done.13.refs_1_, ...), custom_call_target="tpu_custom_call" | custom-call | tf_op jit(solution)/shard_map/final/pallas_call | solution.py:481
  (2 shorter events, 0.1 us)
Async XLA Ops:
  0.6 11.1 %copy-start = (bf16[1,2048,176]{1,2,0:T(8,128)(2,1)S(1)}, bf16[1,2048,176]{1,2,0:T(8,128)(2,1)}, u32[]{:S(2)}) copy-start(bf16[1,2048,176]{1,2,0:T(8,128)(2,1)} %param.14) | copy-start | bytes 2162692
  0.6 11.1 %copy-start.1 = (bf16[1,2048,176]{1,2,0:T(8,128)(2,1)S(1)}, bf16[1,2048,176]{1,2,0:T(8,128)(2,1)}, u32[]{:S(2)}) copy-start(bf16[1,2048,176]{1,2,0:T(8,128)(2,1)} %param.15) | copy-start | bytes 2162692
  0.7 11.1 %copy-start.2 = (bf16[1,176,2048]{2,1,0:T(8,128)(2,1)S(1)}, bf16[1,176,2048]{2,1,0:T(8,128)(2,1)}, u32[]{:S(2)}) copy-start(bf16[1,176,2048]{2,1,0:T(8,128)(2,1)} %param.16) | copy-start | bytes 2162692
  2.4 7.4 %collective-permute-start.2 = (bf16[32,2048]{1,0:T(8,128)(2,1)S(1)}, bf16[32,2048]{1,0:T(8,128)(2,1)S(1)}, u32[]{:S(2)}, u32[]{:S(2)}) collective-permute-start(bf16[32,2048]{1,0:T(8,128)(2,1)S(1)} %get-tuple-element.29.rows_a), channel_id=1, source_target_pairs={{0,2},{1,3},{2,0},{3,1},{4,6},{5,7},{6,4},{7,5},{8,10},{9,11},{10,... | collective-permute-start | bytes 393224 | tf_op jit(solution)/shard_map/ppermute | solution.py:38
  5.4 6.3 %collective-permute-start.8 = (bf16[32,2048]{1,0:T(8,128)(2,1)S(1)}, bf16[32,2048]{1,0:T(8,128)(2,1)S(1)}, u32[]{:S(2)}, u32[]{:S(2)}) collective-permute-start(bf16[32,2048]{1,0:T(8,128)(2,1)S(1)} %get-tuple-element.34.scaled_a), channel_id=1, source_target_pairs={{0,2},{1,3},{2,0},{3,1},{4,6},{5,7},{6,4},{7,5},{8,10},{9,11},{10,... | collective-permute-start | bytes 393224 | tf_op jit(solution)/shard_map/ppermute | solution.py:38
  9.8 2.0 %collective-permute-start.3 = (bf16[32,2048]{1,0:T(8,128)(2,1)S(1)}, bf16[32,2048]{1,0:T(8,128)(2,1)S(1)}, u32[]{:S(2)}, u32[]{:S(2)}) collective-permute-start(bf16[32,2048]{1,0:T(8,128)(2,1)S(1)} %collective-permute-done.2.rows_a), channel_id=1, source_target_pairs={{0,1},{1,0},{2,3},{3,2},{4,5},{5,4},{6,7},{7,6},{8,9},{9,8},{10,11... | collective-permute-start | bytes 393224 | tf_op jit(solution)/shard_map/ppermute | solution.py:38
  9.8 5.2 %collective-permute-start = (bf16[32,2048]{1,0:T(8,128)(2,1)S(1)}, bf16[32,2048]{1,0:T(8,128)(2,1)S(1)}, u32[]{:S(2)}, u32[]{:S(2)}) collective-permute-start(bf16[32,2048]{1,0:T(8,128)(2,1)S(1)} %get-tuple-element.29.rows_a), channel_id=1, source_target_pairs={{0,1},{1,0},{2,3},{3,2},{4,5},{5,4},{6,7},{7,6},{8,9},{9,8},{10,11... | collective-permute-start | bytes 393224 | tf_op jit(solution)/shard_map/ppermute | solution.py:38
  10.3 5.6 %collective-permute-start.6 = (bf16[32,2048]{1,0:T(8,128)(2,1)S(1)}, bf16[32,2048]{1,0:T(8,128)(2,1)S(1)}, u32[]{:S(2)}, u32[]{:S(2)}) collective-permute-start(bf16[32,2048]{1,0:T(8,128)(2,1)S(1)} %get-tuple-element.34.scaled_a), channel_id=1, source_target_pairs={{0,1},{1,0},{2,3},{3,2},{4,5},{5,4},{6,7},{7,6},{8,9},{9,8},{10,11... | collective-permute-start | bytes 393224 | tf_op jit(solution)/shard_map/ppermute | solution.py:38
  11.7 5.7 %collective-permute-start.9 = (bf16[32,2048]{1,0:T(8,128)(2,1)S(1)}, bf16[32,2048]{1,0:T(8,128)(2,1)S(1)}, u32[]{:S(2)}, u32[]{:S(2)}) collective-permute-start(bf16[32,2048]{1,0:T(8,128)(2,1)S(1)} %collective-permute-done.8.scaled_a), channel_id=1, source_target_pairs={{0,1},{1,0},{2,3},{3,2},{4,5},{5,4},{6,7},{7,6},{8,9},{9,8},{10,11... | collective-permute-start | bytes 393224 | tf_op jit(solution)/shard_map/ppermute | solution.py:38
  11.7 1.4 %copy-start.4 = (bf16[1,8,37984]{2,1,0:T(8,128)(2,1)S(1)}, bf16[1,8,37984]{2,1,0:T(8,128)(2,1)}, u32[]{:S(2)}) copy-start(bf16[1,8,37984]{2,1,0:T(8,128)(2,1)} %param.18) | copy-start | bytes 1823236
  12.6 5.9 %collective-permute-start.4 = (bf16[32,2048]{1,0:T(8,128)(2,1)S(1)}, bf16[32,2048]{1,0:T(8,128)(2,1)S(1)}, u32[]{:S(2)}, u32[]{:S(2)}) collective-permute-start(bf16[32,2048]{1,0:T(8,128)(2,1)S(1)} %get-tuple-element.33), channel_id=1, source_target_pairs={{0,1},{1,0},{2,3},{3,2},{4,5},{5,4},{6,7},{7,6},{8,9},{9,8},{10,11... | collective-permute-start | bytes 393224 | tf_op jit(solution)/shard_map/ppermute | solution.py:38
  13.2 18.9 %collective-permute-start.12 = (bf16[8,37984]{1,0:T(8,128)(2,1)S(1)}, bf16[8,37984]{1,0:T(8,128)(2,1)S(1)}, u32[]{:S(2)}, u32[]{:S(2)}) collective-permute-start(bf16[8,37984]{1,0:T(8,128)(2,1)S(1)} %bitcast.29), channel_id=1, source_target_pairs={{0,4},{4,8},{8,12},{12,16},{16,20},{20,24},{24,28},{28,0},{1,5},{5... | collective-permute-start | bytes 1823240 | tf_op jit(solution)/shard_map/ppermute | solution.py:43
  15.7 17.4 %collective-permute-start.1 = (bf16[32,2048]{1,0:T(8,128)(2,1)S(1)}, bf16[32,2048]{1,0:T(8,128)(2,1)S(1)}, u32[]{:S(2)}, u32[]{:S(2)}) collective-permute-start(bf16[32,2048]{1,0:T(8,128)(2,1)S(1)} %get-tuple-element.31), channel_id=1, source_target_pairs={{0,1},{1,0},{2,3},{3,2},{4,5},{5,4},{6,7},{7,6},{8,9},{9,8},{10,11... | collective-permute-start | bytes 393224 | tf_op jit(solution)/shard_map/ppermute | solution.py:38
  16.8 17.3 %collective-permute-start.7 = (bf16[32,2048]{1,0:T(8,128)(2,1)S(1)}, bf16[32,2048]{1,0:T(8,128)(2,1)S(1)}, u32[]{:S(2)}, u32[]{:S(2)}) collective-permute-start(bf16[32,2048]{1,0:T(8,128)(2,1)S(1)} %get-tuple-element.38), channel_id=1, source_target_pairs={{0,1},{1,0},{2,3},{3,2},{4,5},{5,4},{6,7},{7,6},{8,9},{9,8},{10,11... | collective-permute-start | bytes 393224 | tf_op jit(solution)/shard_map/ppermute | solution.py:38
  18.4 3.0 %copy-start.3 = (bf16[1,8,37984]{2,1,0:T(8,128)(2,1)S(1)}, bf16[1,8,37984]{2,1,0:T(8,128)(2,1)}, u32[]{:S(2)}) copy-start(bf16[1,8,37984]{2,1,0:T(8,128)(2,1)} %param.17) | copy-start | bytes 1823236
  18.4 1.7 %collective-permute-start.10 = (bf16[32,2048]{1,0:T(8,128)(2,1)S(1)}, bf16[32,2048]{1,0:T(8,128)(2,1)S(1)}, u32[]{:S(2)}, u32[]{:S(2)}) collective-permute-start(bf16[32,2048]{1,0:T(8,128)(2,1)S(1)} %get-tuple-element.42), channel_id=1, source_target_pairs={{0,1},{1,0},{2,3},{3,2},{4,5},{5,4},{6,7},{7,6},{8,9},{9,8},{10,11... | collective-permute-start | bytes 393224 | tf_op jit(solution)/shard_map/ppermute | solution.py:38
  18.5 15.9 %collective-permute-start.5 = (bf16[32,2048]{1,0:T(8,128)(2,1)S(1)}, bf16[32,2048]{1,0:T(8,128)(2,1)S(1)}, u32[]{:S(2)}, u32[]{:S(2)}) collective-permute-start(bf16[32,2048]{1,0:T(8,128)(2,1)S(1)} %add_convert_fusion.1), channel_id=1, source_target_pairs={{0,2},{1,3},{2,0},{3,1},{4,6},{5,7},{6,4},{7,5},{8,10},{9,11},{10,... | collective-permute-start | bytes 393224 | tf_op jit(solution)/shard_map/ppermute | solution.py:38
  20.1 14.3 %collective-permute-start.11 = (bf16[32,2048]{1,0:T(8,128)(2,1)S(1)}, bf16[32,2048]{1,0:T(8,128)(2,1)S(1)}, u32[]{:S(2)}, u32[]{:S(2)}) collective-permute-start(bf16[32,2048]{1,0:T(8,128)(2,1)S(1)} %add_convert_fusion), channel_id=1, source_target_pairs={{0,2},{1,3},{2,0},{3,1},{4,6},{5,7},{6,4},{7,5},{8,10},{9,11},{10,... | collective-permute-start | bytes 393224 | tf_op jit(solution)/shard_map/ppermute | solution.py:38
  32.6 3.2 %collective-permute-start.15 = (f32[8,128]{1,0:T(8,128)S(1)}, f32[8,128]{1,0:T(8,128)S(1)}, u32[]{:S(2)}, u32[]{:S(2)}) collective-permute-start(f32[8,128]{1,0:T(8,128)S(1)} %teacher.1.refs_0_), channel_id=1, source_target_pairs={{0,3},{1,2},{2,1},{3,0},{4,7},{5,6},{6,5},{7,4},{8,11},{9,10},{10,... | collective-permute-start | bytes 12296 | tf_op jit(solution)/shard_map/ppermute | solution.py:38
  33.1 3.6 %collective-permute-start.14 = (f32[8,128]{1,0:T(8,128)S(1)}, f32[8,128]{1,0:T(8,128)S(1)}, u32[]{:S(2)}, u32[]{:S(2)}) collective-permute-start(f32[8,128]{1,0:T(8,128)S(1)} %teacher.1.refs_0_), channel_id=1, source_target_pairs={{0,2},{1,3},{2,0},{3,1},{4,6},{5,7},{6,4},{7,5},{8,10},{9,11},{10,... | collective-permute-start | bytes 12296 | tf_op jit(solution)/shard_map/ppermute | solution.py:38
  34.2 2.6 %collective-permute-start.13 = (f32[8,128]{1,0:T(8,128)S(1)}, f32[8,128]{1,0:T(8,128)S(1)}, u32[]{:S(2)}, u32[]{:S(2)}) collective-permute-start(f32[8,128]{1,0:T(8,128)S(1)} %teacher.1.refs_0_), channel_id=1, source_target_pairs={{0,1},{1,0},{2,3},{3,2},{4,5},{5,4},{6,7},{7,6},{8,9},{9,8},{10,11... | collective-permute-start | bytes 12296 | tf_op jit(solution)/shard_map/ppermute | solution.py:38

commit v4 on v3

--- a/solution.py
+++ b/solution.py
@@ -1,5 +1,4 @@
 import functools
-import math
 
 import jax
 import jax.numpy as jnp
@@ -213,15 +212,13 @@
 
 
 def combine_kernel(n_window, parts, *refs):
-    outs, grads = refs[:parts], refs[parts : 2 * parts]
-    ids, select, slot_prob, slot_cot, layer_out, input_grad, prob_grad = refs[2 * parts : -4]
-    out_stage, grad_stage, prob_stage, sems = refs[-4:]
+    outs = refs[:parts]
+    ids, select, slot_prob, slot_cot, layer_out, prob_grad, stage, prob_stage, sems = refs[parts:]
     exact = n_window == 1
     chosen = select[...]
     weight = slot_prob[:, :1]
     width = outs[0].shape[1]
     block = min(BLOCK, width)
-    blocks = width // block
     copies = []
 
     def send(source, target):
@@ -230,14 +227,14 @@
         copies.append(copy)
 
     per_slot = jnp.zeros((chosen.shape[0], 1), jnp.float32)
-    for k in range(blocks):
+    for k in range(width // block):
         part = pl.ds(k * block, block)
         out = summed(outs, part)
         per_slot = per_slot + jnp.sum(
             out * slot_cot[:, part].astype(jnp.float32), axis=1, keepdims=True
         )
-        out_stage[:, part] = spread(chosen, weight * out, exact).astype(jnp.bfloat16)
-        send(out_stage.at[:, part], layer_out.at[:, part])
+        stage[:, part] = spread(chosen, weight * out, exact).astype(jnp.bfloat16)
+        send(stage.at[:, part], layer_out.at[:, part])
     spread_prob = chosen * per_slot
     for e in range(n_window):
         per_token = jnp.sum(spread_prob[e * CAP : (e + 1) * CAP], axis=0, keepdims=True)
@@ -245,38 +242,30 @@
         whole = kept if e == 0 else whole + kept
     prob_stage[...] = whole
     send(prob_stage, prob_grad)
-    for k in range(blocks):
-        part = pl.ds(k * block, block)
-        grad_stage[:, part] = spread(chosen, summed(grads, part), exact).astype(jnp.bfloat16)
-        send(grad_stage.at[:, part], input_grad.at[:, part])
     for copy in copies:
         copy.wait()
 
 
-def combine(outs, grads, ids, select, slot_prob, slot_cot, n_window):
+def combine(outs, ids, select, slot_prob, slot_cot, n_window):
     parts = len(outs)
     width = outs[0].shape[1]
     topk, count = ids.shape
-    wide = jax.ShapeDtypeStruct((count, width), jnp.bfloat16)
     return pl.pallas_call(
         functools.partial(combine_kernel, n_window, parts),
-        out_shape=(wide, wide, jax.ShapeDtypeStruct((topk, count), jnp.float32)),
-        in_specs=vmem(2 * parts + 4),
-        out_specs=tuple(hbm(3)),
+        out_shape=(
+            jax.ShapeDtypeStruct((count, width), jnp.bfloat16),
+            jax.ShapeDtypeStruct((topk, count), jnp.float32),
+        ),
+        in_specs=vmem(parts + 4),
+        out_specs=tuple(hbm(2)),
         scratch_shapes=[
             pltpu.VMEM((count, width), jnp.bfloat16),
-            pltpu.VMEM((count, width), jnp.bfloat16),
             pltpu.VMEM((topk, count), jnp.float32),
-            pltpu.SemaphoreType.DMA((2 * (width // min(BLOCK, width)) + 1,)),
+            pltpu.SemaphoreType.DMA((width // min(BLOCK, width) + 1,)),
         ],
         compiler_params=params(12),
         name="combine",
-    )(*outs, *grads, ids, select, slot_prob, slot_cot)
-
-
-def spans(width, parts):
-    step = CHUNK * max(1, width // (parts * CHUNK))
-    return [(start, min(step, width - start)) for start in range(0, width, step)]
+    )(*outs, ids, select, slot_prob, slot_cot)
 
 
 def chunks(start, size):
@@ -287,17 +276,20 @@
     return ref[:, pl.ds(at, size)].astype(jnp.float32)
 
 
-def row_max(ref, start, size, top):
-    full = None
-    for at, span in chunks(start, size):
-        value = load(ref, at, span)
+def row_max(ref, width):
+    full, tail = None, None
+    for at, span in chunks(0, width):
+        value = ref[:, pl.ds(at, span)]
         if span < CHUNK:
-            top = jnp.maximum(top, jnp.max(value, axis=1, keepdims=True))
+            tail = value
         else:
             full = value if full is None else jnp.maximum(full, value)
-    if full is not None:
-        top = jnp.maximum(top, jnp.max(full, axis=1, keepdims=True))
-    return top
+    tops = [
+        jnp.max(value.astype(jnp.float32), axis=1, keepdims=True)
+        for value in (full, tail)
+        if value is not None
+    ]
+    return functools.reduce(jnp.maximum, tops)
 
 
 def row_sums(width, step):
@@ -331,64 +323,105 @@
     )
 
 
-def student_kernel(base, labels, student, stats):
+def student_kernel(base, labels, student, stats, power, hit):
     rows, width = student.shape
     spread_out = jnp.where(diagonal(rows), jnp.broadcast_to(labels[...], (rows, rows)), 0)
     label = jnp.sum(spread_out.astype(jnp.float32), axis=1, keepdims=True).astype(jnp.int32)
     label = label - base[0]
-    top = row_max(student, 0, width, jnp.full((rows, 1), -jnp.inf, jnp.float32))
+    top = row_max(student, width)
 
     def step(at, size):
         value = load(student, at, size)
         here = lax.broadcasted_iota(jnp.int32, (rows, size), 1) == label - at
-        return jnp.exp(value - top), jnp.where(here, value, 0.0)
+        high = jnp.exp(value - top)
+        power[:, pl.ds(at, size)] = high
+        hit[:, pl.ds(at, size)] = here.astype(jnp.float32)
+        return high, jnp.where(here, value, 0.0)
 
     total, picked = row_sums(width, step)
     zero = jnp.zeros((rows, 1), jnp.float32)
-    stats[...] = columns(
-        (top, total, picked, zero, zero, zero, label.astype(jnp.float32)), rows
-    )
+    stats[:rows, :] = columns((top,), rows)
+    stats[rows:, :] = columns((total, zero, zero, picked), rows)
+
+
+def lanes_of(value):
+    return [value[:, k : k + LANES] for k in range(0, value.shape[1], LANES)]
+
+
+def added(values):
+    while len(values) > 1:
+        pairs = [one + two for one, two in zip(values[::2], values[1::2])]
+        values = pairs + values[2 * len(pairs) :]
+    return values[0]
 
 
 def teacher_kernel(student, teacher, student_stats, stats):
     rows, width = student.shape
-    top = row_max(teacher, 0, width, jnp.full((rows, 1), -jnp.inf, jnp.float32))
-
-    def step(at, size):
-        ours = load(student, at, size)
-        theirs = load(teacher, at, size)
-        high = jnp.exp(theirs - top)
-        return high, high * (theirs - ours)
-
-    total, cross = row_sums(width, step)
+    top = None
+    for at, span in chunks(0, width):
+        ours, theirs = lanes_of(load(student, at, span)), lanes_of(load(teacher, at, span))
+        ragged = span % LANES
+        if ragged:
+            pad = jnp.full((rows, LANES - ragged), -jnp.inf, jnp.float32)
+            theirs[-1] = jnp.concatenate([theirs[-1], pad], axis=1)
+            ours[-1] = jnp.concatenate([ours[-1], jnp.zeros_like(pad)], axis=1)
+        high = functools.reduce(jnp.maximum, theirs)
+        if top is None:
+            total = cross = jnp.zeros((rows, LANES), jnp.float32)
+        else:
+            high = jnp.maximum(top, high)
+            shrink = jnp.exp(top - high)
+            total, cross = total * shrink, cross * shrink
+        top = high
+        powers = [jnp.exp(their - top) for their in theirs]
+        gaps = [their - our for our, their in zip(ours, theirs)]
+        if ragged:
+            gaps[-1] = jnp.where(powers[-1] > 0.0, gaps[-1], 0.0)
+        total = total + added(powers)
+        cross = cross + added([power * gap for power, gap in zip(powers, gaps)])
+    high = jnp.max(top, axis=1, keepdims=True)
+    shrink = jnp.exp(top - high)
+    total = jnp.sum(total * shrink, axis=1, keepdims=True)
+    cross = jnp.sum(cross * shrink, axis=1, keepdims=True)
+    top = high
     lane = lax.broadcasted_iota(jnp.int32, (rows, LANES), 1)
-    tile = student_stats[...]
-    tile = jnp.where(lane == 3, top, tile)
-    tile = jnp.where(lane == 4, total, tile)
-    stats[...] = jnp.where(lane == 5, cross, tile)
-
-
-def joined(one, two):
-    lane = lax.broadcasted_iota(jnp.int32, one.shape, 1)
-    student = lane < 2
-    top_one = jnp.where(student, one[:, 0:1], one[:, 3:4])
-    top_two = jnp.where(student, two[:, 0:1], two[:, 3:4])
-    top = jnp.maximum(top_one, top_two)
-    scaled = one * jnp.exp(top_one - top) + two * jnp.exp(top_two - top)
-    tile = jnp.where((lane == 0) | (lane == 3), top, scaled)
-    tile = jnp.where(lane == 2, one + two, tile)
-    return jnp.where(lane == 6, one, tile)
-
-
-def joined_all(tiles):
-    while len(tiles) > 1:
-        pairs = [joined(*tiles[k : k + 2]) for k in range(0, len(tiles) - 1, 2)]
-        tiles = pairs + tiles[2 * len(pairs) :]
-    return tiles[0]
+    theirs = (lane == 1) | (lane == 2)
+    stats[:rows, :] = jnp.where(theirs, top, student_stats[:rows, :])
+    value = jnp.where(lane == 1, total, student_stats[rows:, :])
+    stats[rows:, :] = jnp.where(lane == 2, cross, value)
+
+
+def power_kernel(teacher, stats, power):
+    top = stats[: teacher.shape[0], 1:2]
+    for at, span in chunks(0, teacher.shape[1]):
+        power[:, pl.ds(at, span)] = jnp.exp(load(teacher, at, span) - top)
+
+
+def teacher_power(teacher, stats):
+    return pl.pallas_call(
+        power_kernel,
+        out_shape=jax.ShapeDtypeStruct(teacher.shape, jnp.float32),
+        in_specs=vmem(2),
+        out_specs=vmem(1)[0],
+        compiler_params=params(8),
+        name="power",
+    )(teacher, stats)
+
+
+def joined(tiles):
+    rows = tiles[0].shape[0] // 2
+    tops = [tile[:rows, :] for tile in tiles]
+    top = functools.reduce(jnp.maximum, tops)
+    parts = [tile[rows:, :] * jnp.exp(one - top) for tile, one in zip(tiles, tops)]
+    return top, functools.reduce(jnp.add, parts)
 
 
 def join_kernel(*refs):
-    refs[-1][...] = joined_all([ref[...] for ref in refs[:-1]])
+    tiles, out = refs[:-1], refs[-1]
+    rows = out.shape[0] // 2
+    top, value = joined(tiles)
+    out[:rows, :] = top
+    out[rows:, :] = value
 
 
 def join(tiles):
@@ -402,47 +435,54 @@
     )(*tiles)
 
 
-def final_kernel(student, teacher, *refs):
-    tiles, (loss, grad, stage, loss_stage, sems) = refs[:-5], refs[-5:]
+def final_kernel(n_window, parts, student, teacher, hit, own, *refs):
+    grads, select = refs[:parts], refs[parts]
+    loss, logit_grad, input_grad, logit_stage, input_stage, loss_stage, sems = refs[-7:]
+    tiles = refs[parts + 1 : -7]
     rows, width = student.shape
-    tile = joined_all([ref[...] for ref in tiles])
-    smax, ssum, picked = tile[:, 0:1], tile[:, 1:2], tile[:, 2:3]
-    tmax, tsum, cross = tile[:, 3:4], tile[:, 4:5], tile[:, 5:6]
-    label = tiles[0][:, 6:7].astype(jnp.int32)
-    lse_s = smax + jnp.log(ssum)
-    lse_t = tmax + jnp.log(tsum)
-    half_s = lse_s - math.log(2.0)
-    value = 2.0 * lse_s - picked + cross / tsum - lse_t
-    loss_stage[...] = jnp.sum(jnp.where(diagonal(rows), value, 0.0), axis=0, keepdims=True)
-    copies = fetched((loss_stage,), (loss,), sems)
-    for k, (start, size) in enumerate(spans(width, 20)):
-        for at, span in chunks(start, size):
-            here = lax.broadcasted_iota(jnp.int32, (rows, span), 1) == label - at
-            part = pl.ds(at, span)
-            twice = jnp.exp(load(student, at, span) - half_s)
-            result = twice - jnp.exp(load(teacher, at, span) - lse_t)
-            result = jnp.where(here, result - 1.0, result)
-            stage[:, pl.ds(at, span)] = result.astype(jnp.bfloat16)
-        part = pl.ds(start, size)
-        copy = pltpu.make_async_copy(stage.at[:, part], grad.at[:, part], sems.at[k + 1])
-        copy.start()
-        copies.append(copy)
-    for copy in copies:
-        copy.wait()
+    chosen = select[...]
+    model_width = grads[0].shape[1]
+    block = min(BLOCK, model_width)
+    for k in range(model_width // block):
+        part = pl.ds(k * block, block)
+        value = spread(chosen, summed(grads, part), n_window == 1)
+        input_stage[:, part] = value.astype(jnp.bfloat16)
+    input_copy = pltpu.make_async_copy(input_stage, input_grad, sems.at[2])
+    input_copy.start()
+    top, value = joined(tiles)
+    lse = top + jnp.log(value)
+    scale = jnp.exp(own[:rows, :] - lse)
+    scale_s = 2.0 * scale[:, 0:1]
+    scale_t = scale[:, 1:2]
+    for at, span in chunks(0, width):
+        part = pl.ds(at, span)
+        result = student[:, part] * scale_s - teacher[:, part] * scale_t - hit[:, part]
+        logit_stage[:, part] = result.astype(jnp.bfloat16)
+    logit_copy = pltpu.make_async_copy(logit_stage, logit_grad, sems.at[0])
+    logit_copy.start()
+    picked, cross = value[:, 3:4], value[:, 2:3]
+    total = 2.0 * lse[:, 0:1] - picked + cross / value[:, 1:2] - lse[:, 1:2]
+    loss_stage[...] = jnp.sum(jnp.where(diagonal(rows), total, 0.0), axis=0, keepdims=True)
+    loss_copy = pltpu.make_async_copy(loss_stage, loss, sems.at[1])
+    loss_copy.start()
+    input_copy.wait()
+    logit_copy.wait()
+    loss_copy.wait()
 
 
 def distill(student, teacher, labels):
     base = (lax.axis_index("grp") * student.shape[1]).astype(jnp.int32).reshape(1)
-    own = student_stats(base, labels, student)
+    own, power_s, hit = student_stats(base, labels, student)
     stats = teacher_stats(student, teacher, own)
+    first = stats
     tiles = exchanged(stats, 1)
+    power_t = teacher_power(teacher, stats)
     bits = 4
     while bits < lax.axis_size("grp"):
         stats = join(tiles)
         tiles = exchanged(stats, bits)
         bits = 4 * bits
-    loss, grad = finish(student, teacher, tiles)
-    return loss, grad
+    return (power_s, power_t, hit, first), tiles
 
 
 def exchanged(tile, bits):
@@ -456,9 +496,13 @@
 def student_stats(base, labels, student):
     return pl.pallas_call(
         student_kernel,
-        out_shape=jax.ShapeDtypeStruct((student.shape[0], LANES), jnp.float32),
+        out_shape=(
+            jax.ShapeDtypeStruct((2 * student.shape[0], LANES), jnp.float32),
+            jax.ShapeDtypeStruct(student.shape, jnp.float32),
+            jax.ShapeDtypeStruct(student.shape, jnp.float32),
+        ),
         in_specs=[pl.BlockSpec(memory_space=pltpu.SMEM)] + vmem(2),
-        out_specs=vmem(1)[0],
+        out_specs=tuple(vmem(3)),
         compiler_params=params(8),
         name="student",
     )(base, labels, student)
@@ -468,7 +512,7 @@
     rows, _ = student.shape
     return pl.pallas_call(
         teacher_kernel,
-        out_shape=jax.ShapeDtypeStruct((rows, LANES), jnp.float32),
+        out_shape=jax.ShapeDtypeStruct((2 * rows, LANES), jnp.float32),
         in_specs=vmem(3),
         out_specs=vmem(1)[0],
         compiler_params=params(8),
@@ -476,24 +520,28 @@
     )(student, teacher, own)
 
 
-def finish(student, teacher, tiles):
-    rows, width = student.shape
-    return pl.pallas_call(
-        final_kernel,
+def finish(kept, tiles, grads, select, n_window):
+    student = kept[0]
+    rows = student.shape[0]
+    wide = (select.shape[1], grads[0].shape[1])
+    return pl.pallas_call(
+        functools.partial(final_kernel, n_window, len(grads)),
         out_shape=(
             jax.ShapeDtypeStruct((1, rows), jnp.float32),
-            jax.ShapeDtypeStruct((rows, width), jnp.bfloat16),
+            jax.ShapeDtypeStruct(student.shape, jnp.bfloat16),
+            jax.ShapeDtypeStruct(wide, jnp.bfloat16),
         ),
-        in_specs=vmem(2 + len(tiles)),
-        out_specs=tuple(hbm(2)),
+        in_specs=vmem(len(kept) + len(grads) + 1 + len(tiles)),
+        out_specs=tuple(hbm(3)),
         scratch_shapes=[
-            pltpu.VMEM((rows, width), jnp.bfloat16),
+            pltpu.VMEM(student.shape, jnp.bfloat16),
+            pltpu.VMEM(wide, jnp.bfloat16),
             pltpu.VMEM((1, rows), jnp.float32),
-            pltpu.SemaphoreType.DMA((len(spans(width, 20)) + 1,)),
+            pltpu.SemaphoreType.DMA((3,)),
         ],
         compiler_params=params(8),
         name="final",
-    )(student, teacher, *tiles)
+    )(*kept, *grads, select, *tiles)
 
 
 def between_blocks(value, n_window):
@@ -529,7 +577,8 @@
 
     outs = collected([out_own, out_back, out_home], n_window)
     grads = collected([grad_own, grad_back, grad_home], n_window)
-    return combine(outs, grads, ids, select, slot_prob, slot_cot, n_window)
+    layer_out, prob_grad = combine(outs, ids, select, slot_prob, slot_cot, n_window)
+    return layer_out, prob_grad, grads, select
 
 
 def pair_sum(one, two):
@@ -562,8 +611,9 @@
         expert_ids.T, route_prob.T, tokens, cotangent, held, n_window
     )
     gate_w, up_w, down_w, student = (w_gate[0].T, w_up[0].T, w_down[0], student_logits[0])
-    layer_out, input_grad, prob_grad = layer(*slots, (gate_w, up_w, down_w), n_window)
-    distill_loss, logit_grad = distill(student, teacher, labels)
+    layer_out, prob_grad, grads, select = layer(*slots, (gate_w, up_w, down_w), n_window)
+    kept, tiles = distill(student, teacher, labels)
+    distill_loss, logit_grad, input_grad = finish(kept, tiles, grads, select, n_window)
     return (layer_out, input_grad, prob_grad.T, distill_loss, logit_grad[None])
 
 

time: 38.5 us -> 38.2 us (level)
    pallas_call x3 -> x4, Pallas kernels: 2.78 us -> 2.87 us  [the longest x1 1.36 us: finish(): pl.pallas_call(functools.partial(final_kernel, n_window, len(grads)), out...]
where the time goes in v4:
time: 38.2 us; the launch traced here: 38 us
  waiting for transfers between devices  16.5 us (43%)
  starting transfers between devices  11.4 us (30%)
  Pallas kernels  9.23 us (24%)
  between operations  0.8 us (2%)
    ppermute x1, waiting for transfers between devices, onward(): lax.ppermute(value, axis, [(k, (k + 1) % count) for k in range(count)])  9.83 us
    ppermute x15, starting transfers between devices, swapped(): return lax.ppermute(value, axis, [(k, k ^ bits) for k in range(count)])  9.61 us
    ppermute x15, waiting for transfers between devices, swapped(): return lax.ppermute(value, axis, [(k, k ^ bits) for k in range(count)])  6.68 us
    pallas_call x2, Pallas kernels, backward(): pl.pallas_call(backward_kernel, out_shape=(part, part), in_specs=vmem(7),...  1.97 us
    ppermute x1, starting transfers between devices, onward(): lax.ppermute(value, axis, [(k, (k + 1) % count) for k in range(count)])  1.77 us
    pallas_call x1, Pallas kernels, prepare(): pl.pallas_call(functools.partial(prepare_kernel, n_window, len(held)), ou...  1.7 us
    pallas_call x2, Pallas kernels, forward(): pl.pallas_call(forward_kernel, out_shape=(part, part, act, act), in_specs...  1.62 us
    pallas_call x1, Pallas kernels, finish(): pl.pallas_call(functools.partial(final_kernel, n_window, len(grads)), out...  1.36 us
  transfers between devices with their start and end apart: 16, of which 4 were waited for; matrix products, arithmetic and copies ran while one was open for 0% of the time, Pallas kernels for 16%

profile of v4, /device:TPU:0, one launch (start us, length us, event | category | flops | bytes accessed | tf_op | source)
XLA Modules:
  0.0 38.0 jit_solution(6608125166464445022)
XLA Ops:
  0.6 0.0 copy-start
  0.6 0.0 copy-start.1
  0.7 0.0 copy-start.2
  0.7 1.7 %prepare.1 = (bf16[32,2048]{1,0:T(8,128)(2,1)S(1)}, bf16[32,2048]{1,0:T(8,128)(2,1)S(1)}, bf16[32,2048]{1,0:T(8,128)(2,1)S(1)}, f32[32,128]{1,0:T(8,128)S(1)}, f...) custom-call(s32[4,128]{1,0:T(4,128)} %bitcast.30, f32[4,128]{1,0:T(4,128)} %bitcast.31, ...), custom_call_target="tpu_custom_call" | custom-call | flops 20000000000 | tf_op jit(solution)/shard_map/prepare/pallas_call | solution.py:105
  2.4 3.0 %collective-permute-start.2 = (bf16[32,2048]{1,0:T(8,128)(2,1)S(1)}, bf16[32,2048]{1,0:T(8,128)(2,1)S(1)}, u32[]{:S(2)}, u32[]{:S(2)}) collective-permute-start(bf16[32,2048]{1,0:T(8,128)(2,1)S(1)} %get-tuple-element.32.rows_a), channel_id=1, source_target_pairs={{0,2},{1,3},{2,0},{3,1},{4,6},{5,7},{6,4},{7,5},{8,10},{9,11},{10,... | collective-permute-start | bytes 393224 | tf_op jit(solution)/shard_map/ppermute | solution.py:37
  5.4 0.1 collective-permute-start.9
  5.5 4.3 %collective-permute-done.2.rows_a = bf16[32,2048]{1,0:T(8,128)(2,1)S(1)} collective-permute-done((bf16[32,2048]{1,0:T(8,128)(2,1)S(1)}, bf16[32,2048]{1,0:T(8,128)(2,1)S(1)}, u32[]{:S(2)}, u32[]{:S(2)}) %collective-permute-start.2) | collective-permute-done | bytes 131104 | tf_op jit(solution)/shard_map/ppermute | solution.py:37
  9.8 0.0 collective-permute-start.3
  9.8 0.5 %collective-permute-start = (bf16[32,2048]{1,0:T(8,128)(2,1)S(1)}, bf16[32,2048]{1,0:T(8,128)(2,1)S(1)}, u32[]{:S(2)}, u32[]{:S(2)}) collective-permute-start(bf16[32,2048]{1,0:T(8,128)(2,1)S(1)} %get-tuple-element.32.rows_a), channel_id=1, source_target_pairs={{0,1},{1,0},{2,3},{3,2},{4,5},{5,4},{6,7},{7,6},{8,9},{9,8},{10,11... | collective-permute-start | bytes 393224 | tf_op jit(solution)/shard_map/ppermute | solution.py:37
  10.3 0.0 collective-permute-start.7
  10.3 1.4 %collective-permute-done.9.scaled_a = bf16[32,2048]{1,0:T(8,128)(2,1)S(1)} collective-permute-done((bf16[32,2048]{1,0:T(8,128)(2,1)S(1)}, bf16[32,2048]{1,0:T(8,128)(2,1)S(1)}, u32[]{:S(2)}, u32[]{:S(2)}) %collective-permute-start.9) | collective-permute-done | bytes 131104 | tf_op jit(solution)/shard_map/ppermute | solution.py:37
  11.7 0.0 collective-permute-start.10
  11.7 0.0 collective-permute-done.3.rows_b
  11.7 0.0 copy-start.4
  11.7 0.0 copy-done
  11.7 0.0 copy-done.1
  11.7 0.0 copy-done.2
  11.8 0.8 %forward.3 = (bf16[32,2048]{1,0:T(8,128)(2,1)S(1)}, bf16[32,2048]{1,0:T(8,128)(2,1)S(1)}, f32[64,176]{1,0:T(8,128)S(1)}, f32[64,176]{1,0:T(8,128)S(1)}) custom-call(bf16[32,2048]{1,0:T(8,128)(2,1)S(1)} %collective-permute-done.2.rows_a, bf16[32,2048]{1,0:T(8,128)(2,1)S(1)} %collective-permute-done.3.rows_b, bf16[176,2048]{1,0:T(8,128)(2,1)S(1)} %bitcast.14, ...), custom_call_target="tpu_custom_call" | custom-call | tf_op jit(solution)/shard_map/forward/pallas_call | solution.py:171
  12.6 0.6 %collective-permute-start.4 = (bf16[32,2048]{1,0:T(8,128)(2,1)S(1)}, bf16[32,2048]{1,0:T(8,128)(2,1)S(1)}, u32[]{:S(2)}, u32[]{:S(2)}) collective-permute-start(bf16[32,2048]{1,0:T(8,128)(2,1)S(1)} %get-tuple-element.36), channel_id=1, source_target_pairs={{0,1},{1,0},{2,3},{3,2},{4,5},{5,4},{6,7},{7,6},{8,9},{9,8},{10,11... | collective-permute-start | bytes 393224 | tf_op jit(solution)/shard_map/ppermute | solution.py:37
  13.1 0.0 copy-done.4
  13.1 1.8 %collective-permute-start.6 = (bf16[8,37984]{1,0:T(8,128)(2,1)S(1)}, bf16[8,37984]{1,0:T(8,128)(2,1)S(1)}, u32[]{:S(2)}, u32[]{:S(2)}) collective-permute-start(bf16[8,37984]{1,0:T(8,128)(2,1)S(1)} %bitcast.28), channel_id=1, source_target_pairs={{0,4},{4,8},{8,12},{12,16},{16,20},{20,24},{24,28},{28,0},{1,5},{5... | collective-permute-start | bytes 1823240 | tf_op jit(solution)/shard_map/ppermute | solution.py:42
  14.9 0.0 collective-permute-done.rows_b
  14.9 0.8 %forward.2 = (bf16[32,2048]{1,0:T(8,128)(2,1)S(1)}, bf16[32,2048]{1,0:T(8,128)(2,1)S(1)}, f32[64,176]{1,0:T(8,128)S(1)}, f32[64,176]{1,0:T(8,128)S(1)}) custom-call(bf16[32,2048]{1,0:T(8,128)(2,1)S(1)} %get-tuple-element.32.rows_a, bf16[32,2048]{1,0:T(8,128)(2,1)S(1)} %collective-permute-done.rows_b, bf16[176,2048]{1,0:T(8,128)(2,1)S(1)} %bitcast.15, ...), custom_call_target="tpu_custom_call" | custom-call | tf_op jit(solution)/shard_map/forward/pallas_call | solution.py:171
  15.7 0.1 collective-permute-start.1
  15.8 0.0 collective-permute-done.7.scaled_b
  15.8 1.0 %backward.2 = (bf16[32,2048]{1,0:T(8,128)(2,1)S(1)}, bf16[32,2048]{1,0:T(8,128)(2,1)S(1)}) custom-call(bf16[32,2048]{1,0:T(8,128)(2,1)S(1)} %get-tuple-element.46.scaled_a, bf16[32,2048]{1,0:T(8,128)(2,1)S(1)} %collective-permute-done.7.scaled_b, f32[64,176]{1,0:T(8,128)S(1)} %get-tuple-element.47.gate, f32[64,176]{1,0:T(8,128)S(1)} %get-tuple-element.48.up, ...), custom_call_target="tpu_custom_call" | custom-call | tf_op jit(solution)/shard_map/backward/pallas_call | solution.py:184
  16.8 0.6 %collective-permute-start.8 = (bf16[32,2048]{1,0:T(8,128)(2,1)S(1)}, bf16[32,2048]{1,0:T(8,128)(2,1)S(1)}, u32[]{:S(2)}, u32[]{:S(2)}) collective-permute-start(bf16[32,2048]{1,0:T(8,128)(2,1)S(1)} %get-tuple-element.50), channel_id=1, source_target_pairs={{0,1},{1,0},{2,3},{3,2},{4,5},{5,4},{6,7},{7,6},{8,9},{9,8},{10,11... | collective-permute-start | bytes 393224 | tf_op jit(solution)/shard_map/ppermute | solution.py:37
  17.4 0.0 collective-permute-done.10.scaled_b
  17.4 0.0 copy-start.3
  17.4 1.0 %backward.3 = (bf16[32,2048]{1,0:T(8,128)(2,1)S(1)}, bf16[32,2048]{1,0:T(8,128)(2,1)S(1)}) custom-call(bf16[32,2048]{1,0:T(8,128)(2,1)S(1)} %collective-permute-done.9.scaled_a, bf16[32,2048]{1,0:T(8,128)(2,1)S(1)} %collective-permute-done.10.scaled_b, f32[64,176]{1,0:T(8,128)S(1)} %get-tuple-element.51.gate, f32[64,176]{1,0:T(8,128)S(1)} %get-tuple-element.52.up, ...), custom_call_target="tpu_custom_call" | custom-call | tf_op jit(solution)/shard_map/backward/pallas_call | solution.py:184
  18.4 0.1 collective-permute-start.11
  18.5 0.0 collective-permute-done.4
  18.5 1.6 %collective-permute-start.5 = (bf16[32,2048]{1,0:T(8,128)(2,1)S(1)}, bf16[32,2048]{1,0:T(8,128)(2,1)S(1)}, u32[]{:S(2)}, u32[]{:S(2)}) collective-permute-start(bf16[32,2048]{1,0:T(8,128)(2,1)S(1)} %add_convert_fusion.1), channel_id=1, source_target_pairs={{0,2},{1,3},{2,0},{3,1},{4,6},{5,7},{6,4},{7,5},{8,10},{9,11},{10,... | collective-permute-start | bytes 393224 | tf_op jit(solution)/shard_map/ppermute | solution.py:37
  20.1 0.0 collective-permute-done.11
  20.1 1.3 %collective-permute-start.12 = (bf16[32,2048]{1,0:T(8,128)(2,1)S(1)}, bf16[32,2048]{1,0:T(8,128)(2,1)S(1)}, u32[]{:S(2)}, u32[]{:S(2)}) collective-permute-start(bf16[32,2048]{1,0:T(8,128)(2,1)S(1)} %add_convert_fusion), channel_id=1, source_target_pairs={{0,2},{1,3},{2,0},{3,1},{4,6},{5,7},{6,4},{7,5},{8,10},{9,11},{10,... | collective-permute-start | bytes 393224 | tf_op jit(solution)/shard_map/ppermute | solution.py:37
  21.4 0.0 copy-done.3
  21.4 0.8 %student.1 = (f32[16,128]{1,0:T(8,128)S(1)}, f32[8,37984]{1,0:T(8,128)S(1)}, f32[8,37984]{1,0:T(8,128)S(1)}) custom-call(s32[1]{0:T(128)} %bitcast.9.base, s32[1,8]{1,0:T(1,128)S(1)} %get-tuple-element.42.labels, bf16[8,37984]{1,0:T(8,128)(2,1)S(1)} %bitcast.26), custom_call_target="tpu_custom_call" | custom-call | tf_op jit(solution)/shard_map/student/pallas_call | solution.py:497
  22.2 9.8 %collective-permute-done.6.teacher = bf16[8,37984]{1,0:T(8,128)(2,1)S(1)} collective-permute-done((bf16[8,37984]{1,0:T(8,128)(2,1)S(1)}, bf16[8,37984]{1,0:T(8,128)(2,1)S(1)}, u32[]{:S(2)}, u32[]{:S(2)}) %collective-permute-start.6) | collective-permute-done | bytes 607776 | tf_op jit(solution)/shard_map/ppermute | solution.py:42
  32.0 0.5 %teacher.1.stats.own.refs_4_ = f32[16,128]{1,0:T(8,128)S(1)} custom-call(bf16[8,37984]{1,0:T(8,128)(2,1)S(1)} %bitcast.27, bf16[8,37984]{1,0:T(8,128)(2,1)S(1)} %collective-permute-done.6.teacher, f32[16,128]{1,0:T(8,128)S(1)} %get-tuple-element.44.student_stats), custom_call_target="tpu_custom_call" | custom-call | tf_op jit(solution)/shard_map/teacher/pallas_call | solution.py:513
  32.5 0.5 %collective-permute-start.15 = (f32[16,128]{1,0:T(8,128)S(1)}, f32[16,128]{1,0:T(8,128)S(1)}, u32[]{:S(2)}, u32[]{:S(2)}) collective-permute-start(f32[16,128]{1,0:T(8,128)S(1)} %teacher.1.stats.own.refs_4_), channel_id=1, source_target_pairs={{0,3},{1,2},{2,1},{3,0},{4,7},{5,6},{6,5},{7,4},{8,11},{9,10},{10,... | collective-permute-start | bytes 24584 | tf_op jit(solution)/shard_map/ppermute | solution.py:37
  33.0 0.0 collective-permute-done.1.refs_1_
  33.0 1.1 %collective-permute-start.14 = (f32[16,128]{1,0:T(8,128)S(1)}, f32[16,128]{1,0:T(8,128)S(1)}, u32[]{:S(2)}, u32[]{:S(2)}) collective-permute-start(f32[16,128]{1,0:T(8,128)S(1)} %teacher.1.stats.own.refs_4_), channel_id=1, source_target_pairs={{0,2},{1,3},{2,0},{3,1},{4,6},{5,7},{6,4},{7,5},{8,10},{9,11},{10,... | collective-permute-start | bytes 24584 | tf_op jit(solution)/shard_map/ppermute | solution.py:37
  34.1 0.0 collective-permute-done.5.refs_2_
  34.1 0.3 collective-permute-start.13
  34.4 1.1 %combine.1 = (bf16[128,2048]{1,0:T(8,128)(2,1)}, f32[4,128]{1,0:T(4,128)}) custom-call(bf16[32,2048]{1,0:T(8,128)(2,1)S(1)} %get-tuple-element.33.refs_0_, bf16[32,2048]{1,0:T(8,128)(2,1)S(1)} %collective-permute-done.1.refs_1_, bf16[32,2048]{1,0:T(8,128)(2,1)S(1)} %collective-permute-done.5.refs_2_, s32[4,128]{1,0:T(4,128)S(1)} %get-tuple-element.37.refs_3_, ...), custom_call_target="tpu_custom_call" | custom-call | tf_op jit(solution)/shard_map/combine/pallas_call | solution.py:253
  35.4 0.2 power.1.teacher
  35.7 0.0 collective-permute-done.8.refs_1_
  35.7 0.0 collective-permute-done.12.refs_2_
  35.7 0.0 collective-permute-done.15.refs_7_
  35.7 0.9 %collective-permute-done.14.refs_6_ = f32[16,128]{1,0:T(8,128)S(1)} collective-permute-done((f32[16,128]{1,0:T(8,128)S(1)}, f32[16,128]{1,0:T(8,128)S(1)}, u32[]{:S(2)}, u32[]{:S(2)}) %collective-permute-start.14) | collective-permute-done | bytes 8224 | tf_op jit(solution)/shard_map/ppermute | solution.py:37
  36.6 0.0 collective-permute-done.13.refs_5_
  36.6 1.4 %final.1 = (f32[1,8]{1,0:T(1,128)}, bf16[8,37984]{1,0:T(8,128)(2,1)}, bf16[128,2048]{1,0:T(8,128)(2,1)}) custom-call(f32[8,37984]{1,0:T(8,128)S(1)} %get-tuple-element.43.student, f32[8,37984]{1,0:T(8,128)S(1)} %power.1.teacher, f32[8,37984]{1,0:T(8,128)S(1)} %get-tuple-element.45.hit, f32[16,128]{1,0:T(8,128)S(1)} %teacher.1.stats.own.refs_4_, ...), custom_call_target="tpu_custom_call" | custom-call | tf_op jit(solution)/shard_map/final/pallas_call | solution.py:527
  (2 shorter events, 0.1 us)
Async XLA Ops:
  0.6 11.1 %copy-start = (bf16[1,2048,176]{1,2,0:T(8,128)(2,1)S(1)}, bf16[1,2048,176]{1,2,0:T(8,128)(2,1)}, u32[]{:S(2)}) copy-start(bf16[1,2048,176]{1,2,0:T(8,128)(2,1)} %param.14) | copy-start | bytes 2162692
  0.6 11.1 %copy-start.1 = (bf16[1,2048,176]{1,2,0:T(8,128)(2,1)S(1)}, bf16[1,2048,176]{1,2,0:T(8,128)(2,1)}, u32[]{:S(2)}) copy-start(bf16[1,2048,176]{1,2,0:T(8,128)(2,1)} %param.15) | copy-start | bytes 2162692
  0.7 11.1 %copy-start.2 = (bf16[1,176,2048]{2,1,0:T(8,128)(2,1)S(1)}, bf16[1,176,2048]{2,1,0:T(8,128)(2,1)}, u32[]{:S(2)}) copy-start(bf16[1,176,2048]{2,1,0:T(8,128)(2,1)} %param.16) | copy-start | bytes 2162692
  2.4 7.4 %collective-permute-start.2 = (bf16[32,2048]{1,0:T(8,128)(2,1)S(1)}, bf16[32,2048]{1,0:T(8,128)(2,1)S(1)}, u32[]{:S(2)}, u32[]{:S(2)}) collective-permute-start(bf16[32,2048]{1,0:T(8,128)(2,1)S(1)} %get-tuple-element.32.rows_a), channel_id=1, source_target_pairs={{0,2},{1,3},{2,0},{3,1},{4,6},{5,7},{6,4},{7,5},{8,10},{9,11},{10,... | collective-permute-start | bytes 393224 | tf_op jit(solution)/shard_map/ppermute | solution.py:37
  5.4 6.3 %collective-permute-start.9 = (bf16[32,2048]{1,0:T(8,128)(2,1)S(1)}, bf16[32,2048]{1,0:T(8,128)(2,1)S(1)}, u32[]{:S(2)}, u32[]{:S(2)}) collective-permute-start(bf16[32,2048]{1,0:T(8,128)(2,1)S(1)} %get-tuple-element.46.scaled_a), channel_id=1, source_target_pairs={{0,2},{1,3},{2,0},{3,1},{4,6},{5,7},{6,4},{7,5},{8,10},{9,11},{10,... | collective-permute-start | bytes 393224 | tf_op jit(solution)/shard_map/ppermute | solution.py:37
  9.8 2.0 %collective-permute-start.3 = (bf16[32,2048]{1,0:T(8,128)(2,1)S(1)}, bf16[32,2048]{1,0:T(8,128)(2,1)S(1)}, u32[]{:S(2)}, u32[]{:S(2)}) collective-permute-start(bf16[32,2048]{1,0:T(8,128)(2,1)S(1)} %collective-permute-done.2.rows_a), channel_id=1, source_target_pairs={{0,1},{1,0},{2,3},{3,2},{4,5},{5,4},{6,7},{7,6},{8,9},{9,8},{10,11... | collective-permute-start | bytes 393224 | tf_op jit(solution)/shard_map/ppermute | solution.py:37
  9.8 5.2 %collective-permute-start = (bf16[32,2048]{1,0:T(8,128)(2,1)S(1)}, bf16[32,2048]{1,0:T(8,128)(2,1)S(1)}, u32[]{:S(2)}, u32[]{:S(2)}) collective-permute-start(bf16[32,2048]{1,0:T(8,128)(2,1)S(1)} %get-tuple-element.32.rows_a), channel_id=1, source_target_pairs={{0,1},{1,0},{2,3},{3,2},{4,5},{5,4},{6,7},{7,6},{8,9},{9,8},{10,11... | collective-permute-start | bytes 393224 | tf_op jit(solution)/shard_map/ppermute | solution.py:37
  10.3 5.5 %collective-permute-start.7 = (bf16[32,2048]{1,0:T(8,128)(2,1)S(1)}, bf16[32,2048]{1,0:T(8,128)(2,1)S(1)}, u32[]{:S(2)}, u32[]{:S(2)}) collective-permute-start(bf16[32,2048]{1,0:T(8,128)(2,1)S(1)} %get-tuple-element.46.scaled_a), channel_id=1, source_target_pairs={{0,1},{1,0},{2,3},{3,2},{4,5},{5,4},{6,7},{7,6},{8,9},{9,8},{10,11... | collective-permute-start | bytes 393224 | tf_op jit(solution)/shard_map/ppermute | solution.py:37
  11.7 5.6 %collective-permute-start.10 = (bf16[32,2048]{1,0:T(8,128)(2,1)S(1)}, bf16[32,2048]{1,0:T(8,128)(2,1)S(1)}, u32[]{:S(2)}, u32[]{:S(2)}) collective-permute-start(bf16[32,2048]{1,0:T(8,128)(2,1)S(1)} %collective-permute-done.9.scaled_a), channel_id=1, source_target_pairs={{0,1},{1,0},{2,3},{3,2},{4,5},{5,4},{6,7},{7,6},{8,9},{9,8},{10,11... | collective-permute-start | bytes 393224 | tf_op jit(solution)/shard_map/ppermute | solution.py:37
  11.7 1.4 %copy-start.4 = (bf16[1,8,37984]{2,1,0:T(8,128)(2,1)S(1)}, bf16[1,8,37984]{2,1,0:T(8,128)(2,1)}, u32[]{:S(2)}) copy-start(bf16[1,8,37984]{2,1,0:T(8,128)(2,1)} %param.18) | copy-start | bytes 1823236
  12.6 5.9 %collective-permute-start.4 = (bf16[32,2048]{1,0:T(8,128)(2,1)S(1)}, bf16[32,2048]{1,0:T(8,128)(2,1)S(1)}, u32[]{:S(2)}, u32[]{:S(2)}) collective-permute-start(bf16[32,2048]{1,0:T(8,128)(2,1)S(1)} %get-tuple-element.36), channel_id=1, source_target_pairs={{0,1},{1,0},{2,3},{3,2},{4,5},{5,4},{6,7},{7,6},{8,9},{9,8},{10,11... | collective-permute-start | bytes 393224 | tf_op jit(solution)/shard_map/ppermute | solution.py:37
  13.1 18.9 %collective-permute-start.6 = (bf16[8,37984]{1,0:T(8,128)(2,1)S(1)}, bf16[8,37984]{1,0:T(8,128)(2,1)S(1)}, u32[]{:S(2)}, u32[]{:S(2)}) collective-permute-start(bf16[8,37984]{1,0:T(8,128)(2,1)S(1)} %bitcast.28), channel_id=1, source_target_pairs={{0,4},{4,8},{8,12},{12,16},{16,20},{20,24},{24,28},{28,0},{1,5},{5... | collective-permute-start | bytes 1823240 | tf_op jit(solution)/shard_map/ppermute | solution.py:42
  15.7 17.3 %collective-permute-start.1 = (bf16[32,2048]{1,0:T(8,128)(2,1)S(1)}, bf16[32,2048]{1,0:T(8,128)(2,1)S(1)}, u32[]{:S(2)}, u32[]{:S(2)}) collective-permute-start(bf16[32,2048]{1,0:T(8,128)(2,1)S(1)} %get-tuple-element.34), channel_id=1, source_target_pairs={{0,1},{1,0},{2,3},{3,2},{4,5},{5,4},{6,7},{7,6},{8,9},{9,8},{10,11... | collective-permute-start | bytes 393224 | tf_op jit(solution)/shard_map/ppermute | solution.py:37
  16.8 18.9 %collective-permute-start.8 = (bf16[32,2048]{1,0:T(8,128)(2,1)S(1)}, bf16[32,2048]{1,0:T(8,128)(2,1)S(1)}, u32[]{:S(2)}, u32[]{:S(2)}) collective-permute-start(bf16[32,2048]{1,0:T(8,128)(2,1)S(1)} %get-tuple-element.50), channel_id=1, source_target_pairs={{0,1},{1,0},{2,3},{3,2},{4,5},{5,4},{6,7},{7,6},{8,9},{9,8},{10,11... | collective-permute-start | bytes 393224 | tf_op jit(solution)/shard_map/ppermute | solution.py:37
  17.4 4.0 %copy-start.3 = (bf16[1,8,37984]{2,1,0:T(8,128)(2,1)S(1)}, bf16[1,8,37984]{2,1,0:T(8,128)(2,1)}, u32[]{:S(2)}) copy-start(bf16[1,8,37984]{2,1,0:T(8,128)(2,1)} %param.17) | copy-start | bytes 1823236
  18.4 1.7 %collective-permute-start.11 = (bf16[32,2048]{1,0:T(8,128)(2,1)S(1)}, bf16[32,2048]{1,0:T(8,128)(2,1)S(1)}, u32[]{:S(2)}, u32[]{:S(2)}) collective-permute-start(bf16[32,2048]{1,0:T(8,128)(2,1)S(1)} %get-tuple-element.54), channel_id=1, source_target_pairs={{0,1},{1,0},{2,3},{3,2},{4,5},{5,4},{6,7},{7,6},{8,9},{9,8},{10,11... | collective-permute-start | bytes 393224 | tf_op jit(solution)/shard_map/ppermute | solution.py:37
  18.5 15.6 %collective-permute-start.5 = (bf16[32,2048]{1,0:T(8,128)(2,1)S(1)}, bf16[32,2048]{1,0:T(8,128)(2,1)S(1)}, u32[]{:S(2)}, u32[]{:S(2)}) collective-permute-start(bf16[32,2048]{1,0:T(8,128)(2,1)S(1)} %add_convert_fusion.1), channel_id=1, source_target_pairs={{0,2},{1,3},{2,0},{3,1},{4,6},{5,7},{6,4},{7,5},{8,10},{9,11},{10,... | collective-permute-start | bytes 393224 | tf_op jit(solution)/shard_map/ppermute | solution.py:37
  20.1 15.6 %collective-permute-start.12 = (bf16[32,2048]{1,0:T(8,128)(2,1)S(1)}, bf16[32,2048]{1,0:T(8,128)(2,1)S(1)}, u32[]{:S(2)}, u32[]{:S(2)}) collective-permute-start(bf16[32,2048]{1,0:T(8,128)(2,1)S(1)} %add_convert_fusion), channel_id=1, source_target_pairs={{0,2},{1,3},{2,0},{3,1},{4,6},{5,7},{6,4},{7,5},{8,10},{9,11},{10,... | collective-permute-start | bytes 393224 | tf_op jit(solution)/shard_map/ppermute | solution.py:37
  32.5 3.2 %collective-permute-start.15 = (f32[16,128]{1,0:T(8,128)S(1)}, f32[16,128]{1,0:T(8,128)S(1)}, u32[]{:S(2)}, u32[]{:S(2)}) collective-permute-start(f32[16,128]{1,0:T(8,128)S(1)} %teacher.1.stats.own.refs_4_), channel_id=1, source_target_pairs={{0,3},{1,2},{2,1},{3,0},{4,7},{5,6},{6,5},{7,4},{8,11},{9,10},{10,... | collective-permute-start | bytes 24584 | tf_op jit(solution)/shard_map/ppermute | solution.py:37
  33.0 3.7 %collective-permute-start.14 = (f32[16,128]{1,0:T(8,128)S(1)}, f32[16,128]{1,0:T(8,128)S(1)}, u32[]{:S(2)}, u32[]{:S(2)}) collective-permute-start(f32[16,128]{1,0:T(8,128)S(1)} %teacher.1.stats.own.refs_4_), channel_id=1, source_target_pairs={{0,2},{1,3},{2,0},{3,1},{4,6},{5,7},{6,4},{7,5},{8,10},{9,11},{10,... | collective-permute-start | bytes 24584 | tf_op jit(solution)/shard_map/ppermute | solution.py:37
  34.1 2.6 %collective-permute-start.13 = (f32[16,128]{1,0:T(8,128)S(1)}, f32[16,128]{1,0:T(8,128)S(1)}, u32[]{:S(2)}, u32[]{:S(2)}) collective-permute-start(f32[16,128]{1,0:T(8,128)S(1)} %teacher.1.stats.own.refs_4_), channel_id=1, source_target_pairs={{0,1},{1,0},{2,3},{3,2},{4,5},{5,4},{6,7},{7,6},{8,9},{9,8},{10,11... | collective-permute-start | bytes 24584 | tf_op jit(solution)/shard_map/ppermute | solution.py:37

commit v5 on v4

--- a/solution.py
+++ b/solution.py
@@ -52,14 +52,9 @@
     return copies
 
 
-def prepare_kernel(n_window, held, *refs):
-    taken = 4 + held
-    sources, refs = refs[:taken], refs[taken:]
-    rows, scaled, slot_cot, select, slot_prob, ids = refs[:6]
-    kept, (prob, tokens, cot, sems) = refs[6 : 6 + held], refs[6 + held :]
-    copies = fetched(sources, (ids, prob, tokens, cot, *kept), sems)
+def rows_kernel(n_window, ids_hbm, tokens_hbm, rows, select, ids, tokens, sems):
+    copies = fetched((ids_hbm, tokens_hbm), (ids, tokens), sems)
     copies[0].wait()
-    copies[1].wait()
     all_ids = ids[...]
     count = all_ids.shape[1]
     before = (
@@ -71,124 +66,196 @@
         part = pl.ds(e * CAP, CAP)
         hit = all_ids == e
         member = jnp.sum(hit.astype(jnp.float32), axis=0, keepdims=True)
-        token_prob = jnp.sum(jnp.where(hit, prob[...], 0.0), axis=0, keepdims=True)
         earlier = jnp.dot(
             jnp.broadcast_to(member, (16, count)).astype(jnp.bfloat16),
             before,
             preferred_element_type=jnp.float32,
         )
         position = earlier[:1].astype(jnp.int32)
-        chosen = (slot == position) & (member > 0.5)
-        chosen_f = chosen.astype(jnp.float32)
-        chosen_b = chosen_f.astype(jnp.bfloat16)
-        weight = jnp.sum(chosen_f * token_prob, axis=1, keepdims=True)
+        chosen = ((slot == position) & (member > 0.5)).astype(jnp.float32)
+        select[part, :] = chosen
         if e == 0:
-            copies[2].wait()
+            copies[1].wait()
         rows[part, :] = jnp.dot(
-            chosen_b, tokens[...], preferred_element_type=jnp.float32
+            chosen.astype(jnp.bfloat16), tokens[...], preferred_element_type=jnp.float32
         ).astype(jnp.bfloat16)
+
+
+def scaled_kernel(n_window, ids, select, prob_hbm, cot_hbm, labels_hbm, *refs):
+    scaled, slot_cot, slot_prob, labels, prob, cot, sems = refs
+    copies = fetched((prob_hbm, cot_hbm, labels_hbm), (prob, cot, labels), sems)
+    copies[0].wait()
+    for e in range(n_window):
+        part = pl.ds(e * CAP, CAP)
+        hit = ids[...] == e
+        token_prob = jnp.sum(jnp.where(hit, prob[...], 0.0), axis=0, keepdims=True)
+        chosen = select[part, :]
+        weight = jnp.sum(chosen * token_prob, axis=1, keepdims=True)
+        slot_prob[part, :] = jnp.broadcast_to(weight, (CAP, LANES))
         if e == 0:
-            copies[3].wait()
-        cot_rows = jnp.dot(chosen_b, cot[...], preferred_element_type=jnp.float32)
+            copies[1].wait()
+        cot_rows = jnp.dot(
+            chosen.astype(jnp.bfloat16), cot[...], preferred_element_type=jnp.float32
+        )
         slot_cot[part, :] = cot_rows.astype(jnp.bfloat16)
         scaled[part, :] = (weight * cot_rows).astype(jnp.bfloat16)
-        select[part, :] = chosen_f
-        slot_prob[part, :] = jnp.broadcast_to(weight, (CAP, LANES))
-    for copy in copies[4:]:
-        copy.wait()
-
-
-def prepare(ids, prob, tokens, cot, held, n_window):
+    copies[2].wait()
+
+
+def slot_rows(ids, tokens, n_window):
     count, width = tokens.shape
     slots = n_window * CAP
+    return pl.pallas_call(
+        functools.partial(rows_kernel, n_window),
+        out_shape=(
+            jax.ShapeDtypeStruct((slots, width), jnp.bfloat16),
+            jax.ShapeDtypeStruct((slots, count), jnp.float32),
+            jax.ShapeDtypeStruct(ids.shape, ids.dtype),
+        ),
+        in_specs=hbm(2),
+        out_specs=tuple(vmem(3)),
+        scratch_shapes=[
+            pltpu.VMEM(tokens.shape, tokens.dtype),
+            pltpu.SemaphoreType.DMA((2,)),
+        ],
+        compiler_params=params(8),
+        name="slot_rows",
+    )(*in_hbm(ids, tokens))
+
+
+def slot_scaled(ids, select, prob, cot, labels, n_window):
+    slots, width = select.shape[0], cot.shape[1]
     wide = jax.ShapeDtypeStruct((slots, width), jnp.bfloat16)
     return pl.pallas_call(
-        functools.partial(prepare_kernel, n_window, len(held)),
+        functools.partial(scaled_kernel, n_window),
         out_shape=(
             wide,
             wide,
-            wide,
-            jax.ShapeDtypeStruct((slots, count), jnp.float32),
             jax.ShapeDtypeStruct((slots, LANES), jnp.float32),
-            jax.ShapeDtypeStruct(ids.shape, ids.dtype),
-            *[jax.ShapeDtypeStruct(value.shape, value.dtype) for value in held],
+            jax.ShapeDtypeStruct(labels.shape, labels.dtype),
         ),
-        in_specs=hbm(4 + len(held)),
-        out_specs=tuple(vmem(6 + len(held))),
+        in_specs=vmem(2) + hbm(3),
+        out_specs=tuple(vmem(4)),
         scratch_shapes=[
             pltpu.VMEM(prob.shape, prob.dtype),
-            pltpu.VMEM(tokens.shape, tokens.dtype),
             pltpu.VMEM(cot.shape, cot.dtype),
-            pltpu.SemaphoreType.DMA((4 + len(held),)),
+            pltpu.SemaphoreType.DMA((3,)),
         ],
         compiler_params=params(8),
-        cost_estimate=pl.CostEstimate(flops=20000000000, bytes_accessed=0, transcendentals=0),
-        name="prepare",
-    )(*in_hbm(ids, prob, tokens, cot, *held))
-
-
-def forward_math(rows, gate_w, up_w, down_w):
+        name="slot_scaled",
+    )(ids, select, *in_hbm(prob, cot, labels))
+
+
+def forward_half(rows, gate_w, up_w, down_w, act, wait):
+    wait(0)
     gate = lax.dot_general(rows, gate_w[...], NT, preferred_element_type=jnp.float32)
+    wait(1)
     up = lax.dot_general(rows, up_w[...], NT, preferred_element_type=jnp.float32)
+    act[0] = gate
+    act[1] = up
     hidden = (gate * jax.nn.sigmoid(gate) * up).astype(jnp.bfloat16)
-    out = jnp.dot(hidden, down_w[...], preferred_element_type=jnp.float32)
-    return out.astype(jnp.bfloat16), gate, up
-
-
-def backward_math(scaled, gate, up, gate_w, up_w, down_w):
+    wait(2)
+    return jnp.dot(hidden, down_w[...], preferred_element_type=jnp.float32)
+
+
+def backward_half(scaled, act, gate_w, up_w, down_w, wait):
+    gate, up = act[0], act[1]
     sig = jax.nn.sigmoid(gate)
+    wait(2)
     grad_hidden = lax.dot_general(scaled, down_w[...], NT, preferred_element_type=jnp.float32)
     grad_gate = (grad_hidden * up * sig * (1.0 + gate * (1.0 - sig))).astype(jnp.bfloat16)
     grad_up = (grad_hidden * gate * sig).astype(jnp.bfloat16)
+    wait(0)
     grad = jnp.dot(grad_gate, gate_w[...], preferred_element_type=jnp.float32)
-    grad = grad + jnp.dot(grad_up, up_w[...], preferred_element_type=jnp.float32)
-    return grad.astype(jnp.bfloat16)
-
-
-def forward_kernel(rows_a, rows_b, gate_w, up_w, down_w, keep, send, gate_ref, up_ref):
-    half = rows_a.shape[0]
-    rows = jnp.concatenate([rows_a[...], rows_b[...]], axis=0)
-    out, gate, up = forward_math(rows, gate_w, up_w, down_w)
-    keep[...] = out[:half]
-    send[...] = out[half:]
-    gate_ref[...] = gate
-    up_ref[...] = up
-
-
-def backward_kernel(scaled_a, scaled_b, gate, up, gate_w, up_w, down_w, keep, send):
-    half = scaled_a.shape[0]
-    scaled = jnp.concatenate([scaled_a[...], scaled_b[...]], axis=0)
-    grad = backward_math(scaled, gate[...], up[...], gate_w, up_w, down_w)
-    keep[...] = grad[:half]
-    send[...] = grad[half:]
-
-
-def forward(rows_a, rows_b, weights):
-    half, width = rows_a.shape
-    hidden = weights[0].shape[0]
+    wait(1)
+    return grad + jnp.dot(grad_up, up_w[...], preferred_element_type=jnp.float32)
+
+
+def nothing(k):
+    del k
+
+
+def fetching(sources, buffers, sems, order):
+    copies = [
+        pltpu.make_async_copy(source, buffer, sems.at[k])
+        for k, (source, buffer) in enumerate(zip(sources, buffers))
+    ]
+    for k in order:
+        copies[k].start()
+    return lambda k: copies[k].wait()
+
+
+def forward_kernel(flag, own, far, *refs):
+    held, sources, (keep, send, act, total, *buffers, sems) = refs[:3], refs[3:6], refs[6:]
+    half = own.shape[0]
+    wait = fetching(sources, buffers, sems, (0, 1, 2))
+
+    @pl.when(flag[0] >= 0)
+    def _():
+        total[...] = forward_half(both(own, far), *held, act.at[0], nothing)
+
+    @pl.when(flag[0] >= 0)
+    def _():
+        out = total[...] + forward_half(both(own, far), *buffers, act.at[1], wait)
+        out = out.astype(jnp.bfloat16)
+        keep[...] = out[:half]
+        send[...] = out[half:]
+
+
+def both(own, far):
+    return jnp.concatenate([own[...], far[...]], axis=0)
+
+
+def backward_kernel(flag, own, far, act, *refs):
+    held, sources, (keep, send, total, *buffers, sems) = refs[:3], refs[3:6], refs[6:]
+    half = own.shape[0]
+    wait = fetching(sources, buffers, sems, (2, 0, 1))
+
+    @pl.when(flag[0] >= 0)
+    def _():
+        total[...] = backward_half(both(own, far), act.at[0], *held, nothing)
+
+    @pl.when(flag[0] >= 0)
+    def _():
+        grad = total[...] + backward_half(both(own, far), act.at[1], *buffers, wait)
+        grad = grad.astype(jnp.bfloat16)
+        keep[...] = grad[:half]
+        send[...] = grad[half:]
+
+
+def buffers_of(weights):
+    return [pltpu.VMEM(value.shape, value.dtype) for value in weights] + [
+        pltpu.SemaphoreType.DMA((len(weights),))
+    ]
+
+
+def forward(flag, own, far, held, fetched_w):
+    half, width = own.shape
     part = jax.ShapeDtypeStruct((half, width), jnp.bfloat16)
-    act = jax.ShapeDtypeStruct((2 * half, hidden), jnp.float32)
+    act = jax.ShapeDtypeStruct((2, 2, 2 * half, held[0].shape[0]), jnp.float32)
     return pl.pallas_call(
         forward_kernel,
-        out_shape=(part, part, act, act),
-        in_specs=vmem(5),
-        out_specs=tuple(vmem(4)),
-        compiler_params=params(12),
+        out_shape=(part, part, act),
+        in_specs=[pl.BlockSpec(memory_space=pltpu.SMEM)] + vmem(5) + hbm(3),
+        out_specs=tuple(vmem(3)),
+        scratch_shapes=[pltpu.VMEM((2 * half, width), jnp.float32)] + buffers_of(fetched_w),
+        compiler_params=params(16),
         name="forward",
-    )(rows_a, rows_b, *weights)
-
-
-def backward(scaled_a, scaled_b, gate, up, weights):
-    half, width = scaled_a.shape
+    )(flag, own, far, *held, *in_hbm(*fetched_w))
+
+
+def backward(flag, own, far, act, held, fetched_w):
+    half, width = own.shape
     part = jax.ShapeDtypeStruct((half, width), jnp.bfloat16)
     return pl.pallas_call(
         backward_kernel,
         out_shape=(part, part),
-        in_specs=vmem(7),
+        in_specs=[pl.BlockSpec(memory_space=pltpu.SMEM)] + vmem(6) + hbm(3),
         out_specs=tuple(vmem(2)),
-        compiler_params=params(12),
+        scratch_shapes=[pltpu.VMEM((2 * half, width), jnp.float32)] + buffers_of(fetched_w),
+        compiler_params=params(16),
         name="backward",
-    )(scaled_a, scaled_b, gate, up, *weights)
+    )(flag, own, far, act, *held, *in_hbm(*fetched_w))
 
 
 def spread(select, value, exact):
@@ -212,8 +279,9 @@
 
 
 def combine_kernel(n_window, parts, *refs):
-    outs = refs[:parts]
-    ids, select, slot_prob, slot_cot, layer_out, prob_grad, stage, prob_stage, sems = refs[parts:]
+    outs, grads = refs[:parts], refs[parts : 2 * parts]
+    ids, select, slot_prob, slot_cot, layer_out, input_grad, prob_grad = refs[2 * parts : -4]
+    out_stage, grad_stage, prob_stage, sems = refs[-4:]
     exact = n_window == 1
     chosen = select[...]
     weight = slot_prob[:, :1]
@@ -233,8 +301,8 @@
         per_slot = per_slot + jnp.sum(
             out * slot_cot[:, part].astype(jnp.float32), axis=1, keepdims=True
         )
-        stage[:, part] = spread(chosen, weight * out, exact).astype(jnp.bfloat16)
-        send(stage.at[:, part], layer_out.at[:, part])
+        out_stage[:, part] = spread(chosen, weight * out, exact).astype(jnp.bfloat16)
+        send(out_stage.at[:, part], layer_out.at[:, part])
     spread_prob = chosen * per_slot
     for e in range(n_window):
         per_token = jnp.sum(spread_prob[e * CAP : (e + 1) * CAP], axis=0, keepdims=True)
@@ -242,30 +310,33 @@
         whole = kept if e == 0 else whole + kept
     prob_stage[...] = whole
     send(prob_stage, prob_grad)
+    for k in range(width // block):
+        part = pl.ds(k * block, block)
+        grad_stage[:, part] = spread(chosen, summed(grads, part), exact).astype(jnp.bfloat16)
+        send(grad_stage.at[:, part], input_grad.at[:, part])
     for copy in copies:
         copy.wait()
 
 
-def combine(outs, ids, select, slot_prob, slot_cot, n_window):
+def combine(outs, grads, ids, select, slot_prob, slot_cot, n_window):
     parts = len(outs)
     width = outs[0].shape[1]
     topk, count = ids.shape
+    wide = jax.ShapeDtypeStruct((count, width), jnp.bfloat16)
     return pl.pallas_call(
         functools.partial(combine_kernel, n_window, parts),
-        out_shape=(
-            jax.ShapeDtypeStruct((count, width), jnp.bfloat16),
-            jax.ShapeDtypeStruct((topk, count), jnp.float32),
-        ),
-        in_specs=vmem(parts + 4),
-        out_specs=tuple(hbm(2)),
+        out_shape=(wide, wide, jax.ShapeDtypeStruct((topk, count), jnp.float32)),
+        in_specs=vmem(2 * parts + 4),
+        out_specs=tuple(hbm(3)),
         scratch_shapes=[
             pltpu.VMEM((count, width), jnp.bfloat16),
+            pltpu.VMEM((count, width), jnp.bfloat16),
             pltpu.VMEM((topk, count), jnp.float32),
-            pltpu.SemaphoreType.DMA((width // min(BLOCK, width) + 1,)),
+            pltpu.SemaphoreType.DMA((2 * (width // min(BLOCK, width)) + 1,)),
         ],
         compiler_params=params(12),
         name="combine",
-    )(*outs, ids, select, slot_prob, slot_cot)
+    )(*outs, *grads, ids, select, slot_prob, slot_cot)
 
 
 def chunks(start, size):
@@ -323,11 +394,27 @@
     )
 
 
-def student_kernel(base, labels, student, stats, power, hit):
-    rows, width = student.shape
+def label_kernel(base, labels, out):
+    rows = labels.shape[1]
     spread_out = jnp.where(diagonal(rows), jnp.broadcast_to(labels[...], (rows, rows)), 0)
     label = jnp.sum(spread_out.astype(jnp.float32), axis=1, keepdims=True).astype(jnp.int32)
-    label = label - base[0]
+    out[...] = jnp.broadcast_to(label - base[0], out.shape)
+
+
+def label_columns(base, labels):
+    return pl.pallas_call(
+        label_kernel,
+        out_shape=jax.ShapeDtypeStruct((labels.shape[1], LANES), jnp.int32),
+        in_specs=[pl.BlockSpec(memory_space=pltpu.SMEM)] + vmem(1),
+        out_specs=vmem(1)[0],
+        compiler_params=params(1),
+        name="label",
+    )(base, labels)
+
+
+def student_kernel(label_tile, student, stats, power, hit):
+    rows, width = student.shape
+    label = label_tile[:, 0:1]
     top = row_max(student, width)
 
     def step(at, size):
@@ -435,20 +522,9 @@
     )(*tiles)
 
 
-def final_kernel(n_window, parts, student, teacher, hit, own, *refs):
-    grads, select = refs[:parts], refs[parts]
-    loss, logit_grad, input_grad, logit_stage, input_stage, loss_stage, sems = refs[-7:]
-    tiles = refs[parts + 1 : -7]
+def final_kernel(student, teacher, hit, own, *refs):
+    tiles, (loss, grad, stage, loss_stage, sems) = refs[:-5], refs[-5:]
     rows, width = student.shape
-    chosen = select[...]
-    model_width = grads[0].shape[1]
-    block = min(BLOCK, model_width)
-    for k in range(model_width // block):
-        part = pl.ds(k * block, block)
-        value = spread(chosen, summed(grads, part), n_window == 1)
-        input_stage[:, part] = value.astype(jnp.bfloat16)
-    input_copy = pltpu.make_async_copy(input_stage, input_grad, sems.at[2])
-    input_copy.start()
     top, value = joined(tiles)
     lse = top + jnp.log(value)
     scale = jnp.exp(own[:rows, :] - lse)
@@ -457,22 +533,22 @@
     for at, span in chunks(0, width):
         part = pl.ds(at, span)
         result = student[:, part] * scale_s - teacher[:, part] * scale_t - hit[:, part]
-        logit_stage[:, part] = result.astype(jnp.bfloat16)
-    logit_copy = pltpu.make_async_copy(logit_stage, logit_grad, sems.at[0])
-    logit_copy.start()
+        stage[:, part] = result.astype(jnp.bfloat16)
+    grad_copy = pltpu.make_async_copy(stage, grad, sems.at[0])
+    grad_copy.start()
     picked, cross = value[:, 3:4], value[:, 2:3]
     total = 2.0 * lse[:, 0:1] - picked + cross / value[:, 1:2] - lse[:, 1:2]
     loss_stage[...] = jnp.sum(jnp.where(diagonal(rows), total, 0.0), axis=0, keepdims=True)
     loss_copy = pltpu.make_async_copy(loss_stage, loss, sems.at[1])
     loss_copy.start()
-    input_copy.wait()
-    logit_copy.wait()
+    grad_copy.wait()
     loss_copy.wait()
 
 
 def distill(student, teacher, labels):
     base = (lax.axis_index("grp") * student.shape[1]).astype(jnp.int32).reshape(1)
-    own, power_s, hit = student_stats(base, labels, student)
+    label = label_columns(base, labels)
+    own, power_s, hit = student_stats(label, student)
     stats = teacher_stats(student, teacher, own)
     first = stats
     tiles = exchanged(stats, 1)
@@ -493,7 +569,7 @@
     return tiles
 
 
-def student_stats(base, labels, student):
+def student_stats(label, student):
     return pl.pallas_call(
         student_kernel,
         out_shape=(
@@ -501,11 +577,11 @@
             jax.ShapeDtypeStruct(student.shape, jnp.float32),
             jax.ShapeDtypeStruct(student.shape, jnp.float32),
         ),
-        in_specs=[pl.BlockSpec(memory_space=pltpu.SMEM)] + vmem(2),
+        in_specs=vmem(2),
         out_specs=tuple(vmem(3)),
         compiler_params=params(8),
         name="student",
-    )(base, labels, student)
+    )(label, student)
 
 
 def teacher_stats(student, teacher, own):
@@ -520,28 +596,25 @@
     )(student, teacher, own)
 
 
-def finish(kept, tiles, grads, select, n_window):
+def finish(kept, tiles):
     student = kept[0]
     rows = student.shape[0]
-    wide = (select.shape[1], grads[0].shape[1])
-    return pl.pallas_call(
-        functools.partial(final_kernel, n_window, len(grads)),
+    return pl.pallas_call(
+        final_kernel,
         out_shape=(
             jax.ShapeDtypeStruct((1, rows), jnp.float32),
             jax.ShapeDtypeStruct(student.shape, jnp.bfloat16),
-            jax.ShapeDtypeStruct(wide, jnp.bfloat16),
         ),
-        in_specs=vmem(len(kept) + len(grads) + 1 + len(tiles)),
-        out_specs=tuple(hbm(3)),
+        in_specs=vmem(len(kept) + len(tiles)),
+        out_specs=tuple(hbm(2)),
         scratch_shapes=[
             pltpu.VMEM(student.shape, jnp.bfloat16),
-            pltpu.VMEM(wide, jnp.bfloat16),
             pltpu.VMEM((1, rows), jnp.float32),
-            pltpu.SemaphoreType.DMA((3,)),
+            pltpu.SemaphoreType.DMA((2,)),
         ],
         compiler_params=params(8),
         name="final",
-    )(*kept, *grads, select, *tiles)
+    )(*kept, *tiles)
 
 
 def between_blocks(value, n_window):
@@ -553,36 +626,20 @@
     )
 
 
-def layer(rows, scaled, slot_cot, select, slot_prob, ids, weights, n_window):
+def layer(rows, scaled, slot_cot, select, slot_prob, ids, weights, others, n_window):
     rows = between_blocks(rows, n_window)
     scaled = between_blocks(scaled, n_window)
-    rows_far = swapped(rows, "grp", 2)
-    scaled_far = swapped(scaled, "grp", 2)
-    rows_near = swapped(rows, "grp", 1)
-    scaled_near = swapped(scaled, "grp", 1)
-    rows_cross = swapped(rows_far, "grp", 1)
-    scaled_cross = swapped(scaled_far, "grp", 1)
-
-    out_own, out_send, gate, up = forward(rows, rows_near, weights)
-    grad_own, grad_send = backward(scaled, scaled_near, gate, up, weights)
-    out_back = swapped(out_send, "grp", 1)
-    grad_back = swapped(grad_send, "grp", 1)
-
-    out_keep, out_send, gate, up = forward(rows_far, rows_cross, weights)
-    out_more = swapped(out_send, "grp", 1)
-    grad_keep, grad_send = backward(scaled_far, scaled_cross, gate, up, weights)
-    grad_more = swapped(grad_send, "grp", 1)
-    out_home = swapped(pair_sum(out_keep, out_more), "grp", 2)
-    grad_home = swapped(pair_sum(grad_keep, grad_more), "grp", 2)
-
-    outs = collected([out_own, out_back, out_home], n_window)
-    grads = collected([grad_own, grad_back, grad_home], n_window)
-    layer_out, prob_grad = combine(outs, ids, select, slot_prob, slot_cot, n_window)
-    return layer_out, prob_grad, grads, select
-
-
-def pair_sum(one, two):
-    return (one.astype(jnp.float32) + two.astype(jnp.float32)).astype(jnp.bfloat16)
+    rows_far = swapped(rows, "grp", 3)
+    scaled_far = swapped(scaled, "grp", 3)
+    flag = lax.axis_index("grp").astype(jnp.int32).reshape(1)
+    out_keep, out_send, act = forward(flag, rows, rows_far, others, weights)
+    out_home = swapped(out_send, "grp", 3)
+    grad_keep, grad_send = backward(flag, scaled, scaled_far, act, others, weights)
+    grad_home = swapped(grad_send, "grp", 3)
+
+    outs = collected([out_keep, out_home], n_window)
+    grads = collected([grad_keep, grad_home], n_window)
+    return combine(outs, grads, ids, select, slot_prob, slot_cot, n_window)
 
 
 def collected(parts, n_window):
@@ -606,14 +663,19 @@
 ):
     n_window = lax.axis_size("grp") // PIECES
     teacher = onward(stale_logits[0], "peer")
-    held = (labels,)
-    *slots, labels = prepare(
-        expert_ids.T, route_prob.T, tokens, cotangent, held, n_window
+    rows, select, ids = slot_rows(expert_ids.T, tokens, n_window)
+    scaled, slot_cot, slot_prob, labels = slot_scaled(
+        ids, select, route_prob.T, cotangent, labels, n_window
     )
-    gate_w, up_w, down_w, student = (w_gate[0].T, w_up[0].T, w_down[0], student_logits[0])
-    layer_out, prob_grad, grads, select = layer(*slots, (gate_w, up_w, down_w), n_window)
+    slots = (rows, scaled, slot_cot, select, slot_prob, ids)
+    student = student_logits[0]
+    weights = (w_gate[0].T, w_up[0].T, w_down[0])
+    others = []
+    for value in weights:
+        others.append(swapped(value, "grp", 1))
+    layer_out, input_grad, prob_grad = layer(*slots, weights, others, n_window)
     kept, tiles = distill(student, teacher, labels)
-    distill_loss, logit_grad, input_grad = finish(kept, tiles, grads, select, n_window)
+    distill_loss, logit_grad = finish(kept, tiles)
     return (layer_out, input_grad, prob_grad.T, distill_loss, logit_grad[None])
 
 

time: 38.2 us -> 33.5 us (0.88)
  waiting for transfers between devices: 16.5 us -> 5.98 us
  local copies, waits for them, and re-layouts: 0.02 us -> 3.51 us
  Pallas kernels: 9.23 us -> 12.5 us
  starting transfers between devices: 11.4 us -> 10.5 us
    ppermute x1, waiting for transfers between devices: 9.83 us -> 0.01 us  [onward(): lax.ppermute(value, axis, [(k, (k + 1) % count) for k in range(count)])]
    unnamed x10 -> x18, local copies, waits for them, and re-layouts: 0.02 us -> 3.51 us
    pallas_call x6, Pallas kernels: 6.65 us -> 9.86 us  [the longest x1 3.08 us: forward(): pl.pallas_call(forward_kernel, out_shape=(part, part, act), in_specs=[pl....]
    ppermute x15 -> x10, starting transfers between devices: 9.61 us -> 7.92 us  [swapped(): return lax.ppermute(value, axis, [(k, k ^ bits) for k in range(count)])]
    ppermute x1, starting transfers between devices: 1.77 us -> 2.58 us  [onward(): lax.ppermute(value, axis, [(k, (k + 1) % count) for k in range(count)])]
    ppermute x15 -> x10, waiting for transfers between devices: 6.68 us -> 5.98 us  [swapped(): return lax.ppermute(value, axis, [(k, k ^ bits) for k in range(count)])]
  transfers between devices with their start and end apart: 16 -> 11, of which waited for: 4 -> 3; matrix products, arithmetic and copies ran while one was open for 0% -> 0% of each run, Pallas kernels for 16% -> 34%
where the time goes in v5:
time: 33.5 us; the launch traced here: 33.3 us
  Pallas kernels  12.5 us (37%)
  starting transfers between devices  10.5 us (31%)
  waiting for transfers between devices  5.98 us (18%)
  local copies, waits for them, and re-layouts  3.51 us (10%)
  between operations  0.76 us (2%)
    ppermute x10, starting transfers between devices, swapped(): return lax.ppermute(value, axis, [(k, k ^ bits) for k in range(count)])  7.92 us
    ppermute x10, waiting for transfers between devices, swapped(): return lax.ppermute(value, axis, [(k, k ^ bits) for k in range(count)])  5.98 us
    unnamed x18, local copies, waits for them, and re-layouts  3.51 us
    pallas_call x1, Pallas kernels, forward(): pl.pallas_call(forward_kernel, out_shape=(part, part, act), in_specs=[pl....  3.08 us
    pallas_call x1, Pallas kernels, backward(): pl.pallas_call(backward_kernel, out_shape=(part, part), in_specs=[pl.Bloc...  2.91 us
    ppermute x1, starting transfers between devices, onward(): lax.ppermute(value, axis, [(k, (k + 1) % count) for k in range(count)])  2.58 us
    pallas_call x1, Pallas kernels, slot_rows(): pl.pallas_call(functools.partial(rows_kernel, n_window), out_shape=(jax.S...  1.29 us
    pallas_call x1, Pallas kernels, slot_scaled(): pl.pallas_call(functools.partial(scaled_kernel, n_window), out_shape=(wid...  1.29 us
  transfers between devices with their start and end apart: 11, of which 3 were waited for; matrix products, arithmetic and copies ran while one was open for 0% of the time, Pallas kernels for 34%

profile of v5, /device:TPU:0, one launch (start us, length us, event | category | flops | bytes accessed | tf_op | source)
XLA Modules:
  0.0 33.3 jit_solution(781712847532893033)
XLA Ops:
  0.6 0.6 %collective-permute-start.1 = (bf16[176,2048]{1,0:T(8,128)(2,1)}, bf16[176,2048]{1,0:T(8,128)(2,1)S(1)}, u32[]{:S(2)}, u32[]{:S(2)}) collective-permute-start(bf16[176,2048]{1,0:T(8,128)(2,1)} %bitcast.17), channel_id=1, source_target_pairs={{0,1},{1,0},{2,3},{3,2},{4,5},{5,4},{6,7},{7,6},{8,9},{9,8},{10,11... | collective-permute-start | bytes 2162696 | tf_op jit(solution)/shard_map/ppermute | solution.py:37
  1.2 0.1 collective-permute-start.2
  1.3 0.4 %collective-permute-start.3 = (bf16[176,2048]{1,0:T(8,128)(2,1)}, bf16[176,2048]{1,0:T(8,128)(2,1)S(1)}, u32[]{:S(2)}, u32[]{:S(2)}) collective-permute-start(bf16[176,2048]{1,0:T(8,128)(2,1)} %bitcast.23), channel_id=1, source_target_pairs={{0,1},{1,0},{2,3},{3,2},{4,5},{5,4},{6,7},{7,6},{8,9},{9,8},{10,11... | collective-permute-start | bytes 2162696 | tf_op jit(solution)/shard_map/ppermute | solution.py:37
  1.7 2.6 %collective-permute-start.7 = (bf16[8,37984]{1,0:T(8,128)(2,1)}, bf16[8,37984]{1,0:T(8,128)(2,1)S(1)}, u32[]{:S(2)}, u32[]{:S(2)}) collective-permute-start(bf16[8,37984]{1,0:T(8,128)(2,1)} %bitcast.28), channel_id=1, source_target_pairs={{0,4},{4,8},{8,12},{12,16},{16,20},{20,24},{24,28},{28,0},{1,5},{5... | collective-permute-start | bytes 1823240 | tf_op jit(solution)/shard_map/ppermute | solution.py:42
  4.3 1.3 %slot_rows.1 = (bf16[32,2048]{1,0:T(8,128)(2,1)S(1)}, f32[32,128]{1,0:T(8,128)S(1)}, s32[4,128]{1,0:T(4,128)S(1)}) custom-call(s32[4,128]{1,0:T(4,128)} %bitcast.26, bf16[128,2048]{1,0:T(8,128)(2,1)} %tokens_hbm.1), custom_call_target="tpu_custom_call" | custom-call | tf_op jit(solution)/shard_map/slot_rows/pallas_call | solution.py:108
  5.6 1.3 %collective-permute-start = (bf16[32,2048]{1,0:T(8,128)(2,1)S(1)}, bf16[32,2048]{1,0:T(8,128)(2,1)S(1)}, u32[]{:S(2)}, u32[]{:S(2)}) collective-permute-start(bf16[32,2048]{1,0:T(8,128)(2,1)S(1)} %get-tuple-element.25.own), channel_id=1, source_target_pairs={{0,3},{1,2},{2,1},{3,0},{4,7},{5,6},{6,5},{7,4},{8,11},{9,10},{10,... | collective-permute-start | bytes 393224 | tf_op jit(solution)/shard_map/ppermute | solution.py:37
  6.9 1.3 %slot_scaled.1 = (bf16[32,2048]{1,0:T(8,128)(2,1)S(1)}, bf16[32,2048]{1,0:T(8,128)(2,1)S(1)}, f32[32,128]{1,0:T(8,128)S(1)}, s32[1,8]{1,0:T(1,128)S(1)}) custom-call(s32[4,128]{1,0:T(4,128)S(1)} %get-tuple-element.28.ids.refs_4_, f32[32,128]{1,0:T(8,128)S(1)} %get-tuple-element.29.select.refs_5_, f32[4,128]{1,0:T(4,128)} %bitcast.27, ...), custom_call_target="tpu_custom_call" | custom-call | tf_op jit(solution)/shard_map/slot_scaled/pallas_call | solution.py:129
  8.2 0.0 copy-start.3
  8.2 0.6 %copy-done.3 = bf16[32,2048]{1,0:T(8,128)(2,1)} copy-done((bf16[32,2048]{1,0:T(8,128)(2,1)}, bf16[32,2048]{1,0:T(8,128)(2,1)S(1)}, u32[]{:S(2)}) %copy-start.3) | copy-done | bytes 131096
  8.9 2.3 %collective-permute-done.far = bf16[32,2048]{1,0:T(8,128)(2,1)S(1)} collective-permute-done((bf16[32,2048]{1,0:T(8,128)(2,1)S(1)}, bf16[32,2048]{1,0:T(8,128)(2,1)S(1)}, u32[]{:S(2)}, u32[]{:S(2)}) %collective-permute-start) | collective-permute-done | bytes 131104 | tf_op jit(solution)/shard_map/ppermute | solution.py:37
  11.1 1.5 %collective-permute-start.5 = (bf16[32,2048]{1,0:T(8,128)(2,1)S(1)}, bf16[32,2048]{1,0:T(8,128)(2,1)S(1)}, u32[]{:S(2)}, u32[]{:S(2)}) collective-permute-start(bf16[32,2048]{1,0:T(8,128)(2,1)S(1)} %get-tuple-element.30.own), channel_id=1, source_target_pairs={{0,3},{1,2},{2,1},{3,0},{4,7},{5,6},{6,5},{7,4},{8,11},{9,10},{10,... | collective-permute-start | bytes 393224 | tf_op jit(solution)/shard_map/ppermute | solution.py:37
  12.7 0.0 collective-permute-done.1.refs_0_
  12.7 0.0 collective-permute-done.2.refs_1_
  12.7 0.0 collective-permute-done.3.refs_2_
  12.7 3.1 %forward.1 = (bf16[32,2048]{1,0:T(8,128)(2,1)S(1)}, bf16[32,2048]{1,0:T(8,128)(2,1)}, f32[2,2,64,176]{3,2,1,0:T(8,128)S(1)}) custom-call(s32[1]{0:T(128)} %bitcast.flag, bf16[32,2048]{1,0:T(8,128)(2,1)S(1)} %get-tuple-element.25.own, bf16[32,2048]{1,0:T(8,128)(2,1)S(1)} %collective-permute-done.far, bf16[176,2048]{1,0:T(8,128)(2,1)S(1)} %collective-permute-done.1.refs_0_, ...), custom_call_target="tpu_custom_call" | custom-call | tf_op jit(solution)/shard_map/forward/pallas_call | solution.py:236
  15.8 0.0 copy-start.5
  15.8 0.6 %copy-done.5 = bf16[32,2048]{1,0:T(8,128)(2,1)} copy-done((bf16[32,2048]{1,0:T(8,128)(2,1)}, bf16[32,2048]{1,0:T(8,128)(2,1)S(1)}, u32[]{:S(2)}) %copy-start.5) | copy-done | bytes 131096
  16.4 0.0 collective-permute-done.5.far
  16.4 0.0 copy-start.1
  16.4 0.7 %copy-done.1 = bf16[32,2048]{1,0:T(8,128)(2,1)} copy-done((bf16[32,2048]{1,0:T(8,128)(2,1)}, bf16[32,2048]{1,0:T(8,128)(2,1)S(1)}, u32[]{:S(2)}) %copy-start.1) | copy-done | bytes 131096
  17.1 0.0 copy-start.2
  17.1 0.9 %copy-done.2 = bf16[32,2048]{1,0:T(8,128)(2,1)S(1)} copy-done((bf16[32,2048]{1,0:T(8,128)(2,1)S(1)}, bf16[32,2048]{1,0:T(8,128)(2,1)}, u32[]{:S(2)}) %copy-start.2) | copy-done | bytes 131096
  18.0 0.0 copy-start
  18.0 2.9 %backward.1 = (bf16[32,2048]{1,0:T(8,128)(2,1)S(1)}, bf16[32,2048]{1,0:T(8,128)(2,1)}) custom-call(s32[1]{0:T(128)} %bitcast.flag, bf16[32,2048]{1,0:T(8,128)(2,1)S(1)} %get-tuple-element.30.own, bf16[32,2048]{1,0:T(8,128)(2,1)S(1)} %copy-done.2, f32[2,2,64,176]{3,2,1,0:T(8,128)S(1)} %get-tuple-element.31.act, ...), custom_call_target="tpu_custom_call" | custom-call | tf_op jit(solution)/shard_map/backward/pallas_call | solution.py:250
  20.9 0.0 copy-start.7
  20.9 0.6 %copy-done.7 = bf16[32,2048]{1,0:T(8,128)(2,1)} copy-done((bf16[32,2048]{1,0:T(8,128)(2,1)}, bf16[32,2048]{1,0:T(8,128)(2,1)S(1)}, u32[]{:S(2)}) %copy-start.7) | copy-done | bytes 131096
  21.6 1.7 %collective-permute-start.6 = (bf16[32,2048]{1,0:T(8,128)(2,1)}, bf16[32,2048]{1,0:T(8,128)(2,1)S(1)}, u32[]{:S(2)}, u32[]{:S(2)}) collective-permute-start(bf16[32,2048]{1,0:T(8,128)(2,1)} %get-tuple-element.33), channel_id=1, source_target_pairs={{0,3},{1,2},{2,1},{3,0},{4,7},{5,6},{6,5},{7,4},{8,11},{9,10},{10,... | collective-permute-start | bytes 393224 | tf_op jit(solution)/shard_map/ppermute | solution.py:37
  23.3 0.0 collective-permute-start.4
  23.3 0.1 label.1.label_tile
  23.4 0.0 copy-done
  23.4 0.7 %student.1 = (f32[16,128]{1,0:T(8,128)S(1)}, f32[8,37984]{1,0:T(8,128)S(1)}, f32[8,37984]{1,0:T(8,128)S(1)}) custom-call(s32[8,128]{1,0:T(8,128)S(1)} %label.1.label_tile, bf16[8,37984]{1,0:T(8,128)(2,1)S(1)} %bitcast.15), custom_call_target="tpu_custom_call" | custom-call | tf_op jit(solution)/shard_map/student/pallas_call | solution.py:573
  24.1 0.0 collective-permute-done.7.teacher
  24.1 0.5 %teacher.1.stats.own.refs_0_ = f32[16,128]{1,0:T(8,128)S(1)} custom-call(bf16[8,37984]{1,0:T(8,128)(2,1)S(1)} %bitcast.16, bf16[8,37984]{1,0:T(8,128)(2,1)S(1)} %collective-permute-done.7.teacher, f32[16,128]{1,0:T(8,128)S(1)} %get-tuple-element.41.student_stats), custom_call_target="tpu_custom_call" | custom-call | tf_op jit(solution)/shard_map/teacher/pallas_call | solution.py:589
  24.5 1.7 %collective-permute-start.10 = (f32[16,128]{1,0:T(8,128)S(1)}, f32[16,128]{1,0:T(8,128)S(1)}, u32[]{:S(2)}, u32[]{:S(2)}) collective-permute-start(f32[16,128]{1,0:T(8,128)S(1)} %teacher.1.stats.own.refs_0_), channel_id=1, source_target_pairs={{0,3},{1,2},{2,1},{3,0},{4,7},{5,6},{6,5},{7,4},{8,11},{9,10},{10,... | collective-permute-start | bytes 24584 | tf_op jit(solution)/shard_map/ppermute | solution.py:37
  26.3 0.0 collective-permute-start.8
  26.3 0.5 %collective-permute-start.9 = (f32[16,128]{1,0:T(8,128)S(1)}, f32[16,128]{1,0:T(8,128)S(1)}, u32[]{:S(2)}, u32[]{:S(2)}) collective-permute-start(f32[16,128]{1,0:T(8,128)S(1)} %teacher.1.stats.own.refs_0_), channel_id=1, source_target_pairs={{0,2},{1,3},{2,0},{3,1},{4,6},{5,7},{6,4},{7,5},{8,10},{9,11},{10,... | collective-permute-start | bytes 24584 | tf_op jit(solution)/shard_map/ppermute | solution.py:37
  26.8 0.2 power.1.teacher
  27.0 2.7 %collective-permute-done.10.refs_3_ = f32[16,128]{1,0:T(8,128)S(1)} collective-permute-done((f32[16,128]{1,0:T(8,128)S(1)}, f32[16,128]{1,0:T(8,128)S(1)}, u32[]{:S(2)}, u32[]{:S(2)}) %collective-permute-start.10) | collective-permute-done | bytes 8224 | tf_op jit(solution)/shard_map/ppermute | solution.py:37
  29.8 0.0 collective-permute-done.8.refs_1_
  29.8 1.0 %collective-permute-done.9.refs_2_ = f32[16,128]{1,0:T(8,128)S(1)} collective-permute-done((f32[16,128]{1,0:T(8,128)S(1)}, f32[16,128]{1,0:T(8,128)S(1)}, u32[]{:S(2)}, u32[]{:S(2)}) %collective-permute-start.9) | collective-permute-done | bytes 8224 | tf_op jit(solution)/shard_map/ppermute | solution.py:37
  30.7 0.0 copy-start.4
  30.7 0.0 copy-start.6
  30.7 0.0 copy-start.8
  30.7 1.2 %final.1 = (f32[1,8]{1,0:T(1,128)}, bf16[8,37984]{1,0:T(8,128)(2,1)}) custom-call(f32[8,37984]{1,0:T(8,128)S(1)} %get-tuple-element.40.student, f32[8,37984]{1,0:T(8,128)S(1)} %power.1.teacher, f32[8,37984]{1,0:T(8,128)S(1)} %get-tuple-element.42.hit, f32[16,128]{1,0:T(8,128)S(1)} %teacher.1.stats.own.refs_0_, f32[16,128]{1,0:T(8,128)S(1)} %teacher.1.stats.own.refs_0_, ...), custom_call_target="tpu_custom_call" | custom-call | tf_op jit(solution)/shard_map/final/pallas_call | solution.py:602
  31.9 0.0 collective-permute-done.6.refs_3_
  32.0 0.0 collective-permute-done.4.refs_1_
  32.0 0.0 copy-done.4
  32.0 0.0 copy-done.6
  32.0 0.0 copy-done.8
  32.0 1.3 %combine.1 = (bf16[128,2048]{1,0:T(8,128)(2,1)}, bf16[128,2048]{1,0:T(8,128)(2,1)}, f32[4,128]{1,0:T(4,128)}) custom-call(bf16[32,2048]{1,0:T(8,128)(2,1)S(1)} %copy-done.6, bf16[32,2048]{1,0:T(8,128)(2,1)S(1)} %collective-permute-done.4.refs_1_, bf16[32,2048]{1,0:T(8,128)(2,1)S(1)} %copy-done.8, bf16[32,2048]{1,0:T(8,128)(2,1)S(1)} %collective-permute-done.6.refs_3_, ...), custom_call_target="tpu_custom_call" | custom-call | tf_op jit(solution)/shard_map/combine/pallas_call | solution.py:326
Async XLA Ops:
  0.6 12.0 %collective-permute-start.1 = (bf16[176,2048]{1,0:T(8,128)(2,1)}, bf16[176,2048]{1,0:T(8,128)(2,1)S(1)}, u32[]{:S(2)}, u32[]{:S(2)}) collective-permute-start(bf16[176,2048]{1,0:T(8,128)(2,1)} %bitcast.17), channel_id=1, source_target_pairs={{0,1},{1,0},{2,3},{3,2},{4,5},{5,4},{6,7},{7,6},{8,9},{9,8},{10,11... | collective-permute-start | bytes 2162696 | tf_op jit(solution)/shard_map/ppermute | solution.py:37
  1.2 11.5 %collective-permute-start.2 = (bf16[176,2048]{1,0:T(8,128)(2,1)}, bf16[176,2048]{1,0:T(8,128)(2,1)S(1)}, u32[]{:S(2)}, u32[]{:S(2)}) collective-permute-start(bf16[176,2048]{1,0:T(8,128)(2,1)} %bitcast.20), channel_id=1, source_target_pairs={{0,1},{1,0},{2,3},{3,2},{4,5},{5,4},{6,7},{7,6},{8,9},{9,8},{10,11... | collective-permute-start | bytes 2162696 | tf_op jit(solution)/shard_map/ppermute | solution.py:37
  1.3 11.4 %collective-permute-start.3 = (bf16[176,2048]{1,0:T(8,128)(2,1)}, bf16[176,2048]{1,0:T(8,128)(2,1)S(1)}, u32[]{:S(2)}, u32[]{:S(2)}) collective-permute-start(bf16[176,2048]{1,0:T(8,128)(2,1)} %bitcast.23), channel_id=1, source_target_pairs={{0,1},{1,0},{2,3},{3,2},{4,5},{5,4},{6,7},{7,6},{8,9},{9,8},{10,11... | collective-permute-start | bytes 2162696 | tf_op jit(solution)/shard_map/ppermute | solution.py:37
  1.7 22.4 %collective-permute-start.7 = (bf16[8,37984]{1,0:T(8,128)(2,1)}, bf16[8,37984]{1,0:T(8,128)(2,1)S(1)}, u32[]{:S(2)}, u32[]{:S(2)}) collective-permute-start(bf16[8,37984]{1,0:T(8,128)(2,1)} %bitcast.28), channel_id=1, source_target_pairs={{0,4},{4,8},{8,12},{12,16},{16,20},{20,24},{24,28},{28,0},{1,5},{5... | collective-permute-start | bytes 1823240 | tf_op jit(solution)/shard_map/ppermute | solution.py:42
  5.6 5.5 %collective-permute-start = (bf16[32,2048]{1,0:T(8,128)(2,1)S(1)}, bf16[32,2048]{1,0:T(8,128)(2,1)S(1)}, u32[]{:S(2)}, u32[]{:S(2)}) collective-permute-start(bf16[32,2048]{1,0:T(8,128)(2,1)S(1)} %get-tuple-element.25.own), channel_id=1, source_target_pairs={{0,3},{1,2},{2,1},{3,0},{4,7},{5,6},{6,5},{7,4},{8,11},{9,10},{10,... | collective-permute-start | bytes 393224 | tf_op jit(solution)/shard_map/ppermute | solution.py:37
  8.2 0.7 %copy-start.3 = (bf16[32,2048]{1,0:T(8,128)(2,1)}, bf16[32,2048]{1,0:T(8,128)(2,1)S(1)}, u32[]{:S(2)}) copy-start(bf16[32,2048]{1,0:T(8,128)(2,1)S(1)} %get-tuple-element.35.refs_7_) | copy-start | bytes 393220
  11.1 5.3 %collective-permute-start.5 = (bf16[32,2048]{1,0:T(8,128)(2,1)S(1)}, bf16[32,2048]{1,0:T(8,128)(2,1)S(1)}, u32[]{:S(2)}, u32[]{:S(2)}) collective-permute-start(bf16[32,2048]{1,0:T(8,128)(2,1)S(1)} %get-tuple-element.30.own), channel_id=1, source_target_pairs={{0,3},{1,2},{2,1},{3,0},{4,7},{5,6},{6,5},{7,4},{8,11},{9,10},{10,... | collective-permute-start | bytes 393224 | tf_op jit(solution)/shard_map/ppermute | solution.py:37
  15.8 0.7 %copy-start.5 = (bf16[32,2048]{1,0:T(8,128)(2,1)}, bf16[32,2048]{1,0:T(8,128)(2,1)S(1)}, u32[]{:S(2)}) copy-start(bf16[32,2048]{1,0:T(8,128)(2,1)S(1)} %get-tuple-element.26.refs_0_) | copy-start | bytes 393220
  16.4 0.7 %copy-start.1 = (bf16[32,2048]{1,0:T(8,128)(2,1)}, bf16[32,2048]{1,0:T(8,128)(2,1)S(1)}, u32[]{:S(2)}) copy-start(bf16[32,2048]{1,0:T(8,128)(2,1)S(1)} %collective-permute-done.5.far) | copy-start | bytes 393220
  17.1 0.9 %copy-start.2 = (bf16[32,2048]{1,0:T(8,128)(2,1)S(1)}, bf16[32,2048]{1,0:T(8,128)(2,1)}, u32[]{:S(2)}) copy-start(bf16[32,2048]{1,0:T(8,128)(2,1)} %copy-done.1) | copy-start | bytes 393220
  18.0 5.4 %copy-start = (bf16[1,8,37984]{2,1,0:T(8,128)(2,1)S(1)}, bf16[1,8,37984]{2,1,0:T(8,128)(2,1)}, u32[]{:S(2)}) copy-start(bf16[1,8,37984]{2,1,0:T(8,128)(2,1)} %param.17) | copy-start | bytes 1823236
  20.9 0.6 %copy-start.7 = (bf16[32,2048]{1,0:T(8,128)(2,1)}, bf16[32,2048]{1,0:T(8,128)(2,1)S(1)}, u32[]{:S(2)}) copy-start(bf16[32,2048]{1,0:T(8,128)(2,1)S(1)} %get-tuple-element.32.refs_2_) | copy-start | bytes 393220
  21.6 10.4 %collective-permute-start.6 = (bf16[32,2048]{1,0:T(8,128)(2,1)}, bf16[32,2048]{1,0:T(8,128)(2,1)S(1)}, u32[]{:S(2)}, u32[]{:S(2)}) collective-permute-start(bf16[32,2048]{1,0:T(8,128)(2,1)} %get-tuple-element.33), channel_id=1, source_target_pairs={{0,3},{1,2},{2,1},{3,0},{4,7},{5,6},{6,5},{7,4},{8,11},{9,10},{10,... | collective-permute-start | bytes 393224 | tf_op jit(solution)/shard_map/ppermute | solution.py:37
  23.3 8.7 %collective-permute-start.4 = (bf16[32,2048]{1,0:T(8,128)(2,1)}, bf16[32,2048]{1,0:T(8,128)(2,1)S(1)}, u32[]{:S(2)}, u32[]{:S(2)}) collective-permute-start(bf16[32,2048]{1,0:T(8,128)(2,1)} %get-tuple-element.27), channel_id=1, source_target_pairs={{0,3},{1,2},{2,1},{3,0},{4,7},{5,6},{6,5},{7,4},{8,11},{9,10},{10,... | collective-permute-start | bytes 393224 | tf_op jit(solution)/shard_map/ppermute | solution.py:37
  24.5 5.2 %collective-permute-start.10 = (f32[16,128]{1,0:T(8,128)S(1)}, f32[16,128]{1,0:T(8,128)S(1)}, u32[]{:S(2)}, u32[]{:S(2)}) collective-permute-start(f32[16,128]{1,0:T(8,128)S(1)} %teacher.1.stats.own.refs_0_), channel_id=1, source_target_pairs={{0,3},{1,2},{2,1},{3,0},{4,7},{5,6},{6,5},{7,4},{8,11},{9,10},{10,... | collective-permute-start | bytes 24584 | tf_op jit(solution)/shard_map/ppermute | solution.py:37
  26.3 3.5 %collective-permute-start.8 = (f32[16,128]{1,0:T(8,128)S(1)}, f32[16,128]{1,0:T(8,128)S(1)}, u32[]{:S(2)}, u32[]{:S(2)}) collective-permute-start(f32[16,128]{1,0:T(8,128)S(1)} %teacher.1.stats.own.refs_0_), channel_id=1, source_target_pairs={{0,1},{1,0},{2,3},{3,2},{4,5},{5,4},{6,7},{7,6},{8,9},{9,8},{10,11... | collective-permute-start | bytes 24584 | tf_op jit(solution)/shard_map/ppermute | solution.py:37
  26.3 4.5 %collective-permute-start.9 = (f32[16,128]{1,0:T(8,128)S(1)}, f32[16,128]{1,0:T(8,128)S(1)}, u32[]{:S(2)}, u32[]{:S(2)}) collective-permute-start(f32[16,128]{1,0:T(8,128)S(1)} %teacher.1.stats.own.refs_0_), channel_id=1, source_target_pairs={{0,2},{1,3},{2,0},{3,1},{4,6},{5,7},{6,4},{7,5},{8,10},{9,11},{10,... | collective-permute-start | bytes 24584 | tf_op jit(solution)/shard_map/ppermute | solution.py:37
  30.7 1.2 %copy-start.4 = (bf16[32,2048]{1,0:T(8,128)(2,1)S(1)}, bf16[32,2048]{1,0:T(8,128)(2,1)}, u32[]{:S(2)}) copy-start(bf16[32,2048]{1,0:T(8,128)(2,1)} %copy-done.3) | copy-start | bytes 393220
  30.7 1.2 %copy-start.6 = (bf16[32,2048]{1,0:T(8,128)(2,1)S(1)}, bf16[32,2048]{1,0:T(8,128)(2,1)}, u32[]{:S(2)}) copy-start(bf16[32,2048]{1,0:T(8,128)(2,1)} %copy-done.5) | copy-start | bytes 393220
  30.7 1.3 %copy-start.8 = (bf16[32,2048]{1,0:T(8,128)(2,1)S(1)}, bf16[32,2048]{1,0:T(8,128)(2,1)}, u32[]{:S(2)}) copy-start(bf16[32,2048]{1,0:T(8,128)(2,1)} %copy-done.7) | copy-start | bytes 393220

commit v6 on v5

--- a/solution.py
+++ b/solution.py
@@ -192,14 +192,18 @@
 
     @pl.when(flag[0] >= 0)
     def _():
-        total[...] = forward_half(both(own, far), *held, act.at[0], nothing)
+        total[...] = rounded(forward_half(both(own, far), *held, act.at[0], nothing))
 
     @pl.when(flag[0] >= 0)
     def _():
-        out = total[...] + forward_half(both(own, far), *buffers, act.at[1], wait)
+        out = total[...] + rounded(forward_half(both(own, far), *buffers, act.at[1], wait))
         out = out.astype(jnp.bfloat16)
         keep[...] = out[:half]
         send[...] = out[half:]
+
+
+def rounded(value):
+    return value.astype(jnp.bfloat16).astype(jnp.float32)
 
 
 def both(own, far):
@@ -213,11 +217,11 @@
 
     @pl.when(flag[0] >= 0)
     def _():
-        total[...] = backward_half(both(own, far), act.at[0], *held, nothing)
+        total[...] = rounded(backward_half(both(own, far), act.at[0], *held, nothing))
 
     @pl.when(flag[0] >= 0)
     def _():
-        grad = total[...] + backward_half(both(own, far), act.at[1], *buffers, wait)
+        grad = total[...] + rounded(backward_half(both(own, far), act.at[1], *buffers, wait))
         grad = grad.astype(jnp.bfloat16)
         keep[...] = grad[:half]
         send[...] = grad[half:]
@@ -522,7 +526,7 @@
     )(*tiles)
 
 
-def final_kernel(student, teacher, hit, own, *refs):
+def final_kernel(flag, student, teacher, hit, own, *refs):
     tiles, (loss, grad, stage, loss_stage, sems) = refs[:-5], refs[-5:]
     rows, width = student.shape
     top, value = joined(tiles)
@@ -530,18 +534,33 @@
     scale = jnp.exp(own[:rows, :] - lse)
     scale_s = 2.0 * scale[:, 0:1]
     scale_t = scale[:, 1:2]
-    for at, span in chunks(0, width):
-        part = pl.ds(at, span)
-        result = student[:, part] * scale_s - teacher[:, part] * scale_t - hit[:, part]
-        stage[:, part] = result.astype(jnp.bfloat16)
-    grad_copy = pltpu.make_async_copy(stage, grad, sems.at[0])
-    grad_copy.start()
+    middle = CHUNK * (width // CHUNK // 2)
+
+    def fill(start, stop, k):
+        for at, span in chunks(start, stop - start):
+            part = pl.ds(at, span)
+            result = student[:, part] * scale_s - teacher[:, part] * scale_t - hit[:, part]
+            stage[:, part] = result.astype(jnp.bfloat16)
+        copy = written(start, stop, k)
+        copy.start()
+
+    def written(start, stop, k):
+        part = pl.ds(start, stop - start)
+        return pltpu.make_async_copy(stage.at[:, part], grad.at[:, part], sems.at[k])
+
+    fill(0, middle, 0)
+
+    @pl.when(flag[0] >= 0)
+    def _():
+        fill(middle, width, 2)
+
     picked, cross = value[:, 3:4], value[:, 2:3]
     total = 2.0 * lse[:, 0:1] - picked + cross / value[:, 1:2] - lse[:, 1:2]
     loss_stage[...] = jnp.sum(jnp.where(diagonal(rows), total, 0.0), axis=0, keepdims=True)
     loss_copy = pltpu.make_async_copy(loss_stage, loss, sems.at[1])
     loss_copy.start()
-    grad_copy.wait()
+    written(0, middle, 0).wait()
+    written(middle, width, 2).wait()
     loss_copy.wait()
 
 
@@ -605,16 +624,16 @@
             jax.ShapeDtypeStruct((1, rows), jnp.float32),
             jax.ShapeDtypeStruct(student.shape, jnp.bfloat16),
         ),
-        in_specs=vmem(len(kept) + len(tiles)),
+        in_specs=[pl.BlockSpec(memory_space=pltpu.SMEM)] + vmem(len(kept) + len(tiles)),
         out_specs=tuple(hbm(2)),
         scratch_shapes=[
             pltpu.VMEM(student.shape, jnp.bfloat16),
             pltpu.VMEM((1, rows), jnp.float32),
-            pltpu.SemaphoreType.DMA((2,)),
+            pltpu.SemaphoreType.DMA((3,)),
         ],
         compiler_params=params(8),
         name="final",
-    )(*kept, *tiles)
+    )(lax.axis_index("grp").astype(jnp.int32).reshape(1), *kept, *tiles)
 
 
 def between_blocks(value, n_window):

time: 33.5 us -> 33.4 us (level)
  no operation moved by 1% of the time
where the time goes in v6:
time: 33.4 us; the launch traced here: 33.2 us
  Pallas kernels  12.5 us (37%)
  starting transfers between devices  10.5 us (31%)
  waiting for transfers between devices  5.98 us (18%)
  local copies, waits for them, and re-layouts  3.51 us (11%)
  between operations  0.76 us (2%)
    ppermute x10, starting transfers between devices, swapped(): return lax.ppermute(value, axis, [(k, k ^ bits) for k in range(count)])  7.91 us
    ppermute x10, waiting for transfers between devices, swapped(): return lax.ppermute(value, axis, [(k, k ^ bits) for k in range(count)])  5.98 us
    unnamed x18, local copies, waits for them, and re-layouts  3.51 us
    pallas_call x1, Pallas kernels, forward(): pl.pallas_call(forward_kernel, out_shape=(part, part, act), in_specs=[pl....  3.08 us
    pallas_call x1, Pallas kernels, backward(): pl.pallas_call(backward_kernel, out_shape=(part, part), in_specs=[pl.Bloc...  2.91 us
    ppermute x1, starting transfers between devices, onward(): lax.ppermute(value, axis, [(k, (k + 1) % count) for k in range(count)])  2.58 us
    pallas_call x1, Pallas kernels, slot_rows(): pl.pallas_call(functools.partial(rows_kernel, n_window), out_shape=(jax.S...  1.29 us
    pallas_call x1, Pallas kernels, slot_scaled(): pl.pallas_call(functools.partial(scaled_kernel, n_window), out_shape=(wid...  1.29 us
  transfers between devices with their start and end apart: 11, of which 3 were waited for; matrix products, arithmetic and copies ran while one was open for 0% of the time, Pallas kernels for 34%

profile of v6, /device:TPU:0, one launch (start us, length us, event | category | flops | bytes accessed | tf_op | source)
XLA Modules:
  0.0 33.2 jit_solution(4468510661947003654)
XLA Ops:
  0.6 0.6 %collective-permute-start.1 = (bf16[176,2048]{1,0:T(8,128)(2,1)}, bf16[176,2048]{1,0:T(8,128)(2,1)S(1)}, u32[]{:S(2)}, u32[]{:S(2)}) collective-permute-start(bf16[176,2048]{1,0:T(8,128)(2,1)} %bitcast.17), channel_id=1, source_target_pairs={{0,1},{1,0},{2,3},{3,2},{4,5},{5,4},{6,7},{7,6},{8,9},{9,8},{10,11... | collective-permute-start | bytes 2162696 | tf_op jit(solution)/shard_map/ppermute | solution.py:37
  1.2 0.1 collective-permute-start.2
  1.3 0.4 %collective-permute-start.3 = (bf16[176,2048]{1,0:T(8,128)(2,1)}, bf16[176,2048]{1,0:T(8,128)(2,1)S(1)}, u32[]{:S(2)}, u32[]{:S(2)}) collective-permute-start(bf16[176,2048]{1,0:T(8,128)(2,1)} %bitcast.23), channel_id=1, source_target_pairs={{0,1},{1,0},{2,3},{3,2},{4,5},{5,4},{6,7},{7,6},{8,9},{9,8},{10,11... | collective-permute-start | bytes 2162696 | tf_op jit(solution)/shard_map/ppermute | solution.py:37
  1.7 2.6 %collective-permute-start.7 = (bf16[8,37984]{1,0:T(8,128)(2,1)}, bf16[8,37984]{1,0:T(8,128)(2,1)S(1)}, u32[]{:S(2)}, u32[]{:S(2)}) collective-permute-start(bf16[8,37984]{1,0:T(8,128)(2,1)} %bitcast.28), channel_id=1, source_target_pairs={{0,4},{4,8},{8,12},{12,16},{16,20},{20,24},{24,28},{28,0},{1,5},{5... | collective-permute-start | bytes 1823240 | tf_op jit(solution)/shard_map/ppermute | solution.py:42
  4.3 1.3 %slot_rows.1 = (bf16[32,2048]{1,0:T(8,128)(2,1)S(1)}, f32[32,128]{1,0:T(8,128)S(1)}, s32[4,128]{1,0:T(4,128)S(1)}) custom-call(s32[4,128]{1,0:T(4,128)} %bitcast.26, bf16[128,2048]{1,0:T(8,128)(2,1)} %tokens_hbm.1), custom_call_target="tpu_custom_call" | custom-call | tf_op jit(solution)/shard_map/slot_rows/pallas_call | solution.py:108
  5.6 1.3 %collective-permute-start = (bf16[32,2048]{1,0:T(8,128)(2,1)S(1)}, bf16[32,2048]{1,0:T(8,128)(2,1)S(1)}, u32[]{:S(2)}, u32[]{:S(2)}) collective-permute-start(bf16[32,2048]{1,0:T(8,128)(2,1)S(1)} %get-tuple-element.25.own), channel_id=1, source_target_pairs={{0,3},{1,2},{2,1},{3,0},{4,7},{5,6},{6,5},{7,4},{8,11},{9,10},{10,... | collective-permute-start | bytes 393224 | tf_op jit(solution)/shard_map/ppermute | solution.py:37
  6.9 1.3 %slot_scaled.1 = (bf16[32,2048]{1,0:T(8,128)(2,1)S(1)}, bf16[32,2048]{1,0:T(8,128)(2,1)S(1)}, f32[32,128]{1,0:T(8,128)S(1)}, s32[1,8]{1,0:T(1,128)S(1)}) custom-call(s32[4,128]{1,0:T(4,128)S(1)} %get-tuple-element.28.ids.refs_4_, f32[32,128]{1,0:T(8,128)S(1)} %get-tuple-element.29.select.refs_5_, f32[4,128]{1,0:T(4,128)} %bitcast.27, ...), custom_call_target="tpu_custom_call" | custom-call | tf_op jit(solution)/shard_map/slot_scaled/pallas_call | solution.py:129
  8.2 0.0 copy-start.3
  8.2 0.6 %copy-done.3 = bf16[32,2048]{1,0:T(8,128)(2,1)} copy-done((bf16[32,2048]{1,0:T(8,128)(2,1)}, bf16[32,2048]{1,0:T(8,128)(2,1)S(1)}, u32[]{:S(2)}) %copy-start.3) | copy-done | bytes 131096
  8.9 2.3 %collective-permute-done.far = bf16[32,2048]{1,0:T(8,128)(2,1)S(1)} collective-permute-done((bf16[32,2048]{1,0:T(8,128)(2,1)S(1)}, bf16[32,2048]{1,0:T(8,128)(2,1)S(1)}, u32[]{:S(2)}, u32[]{:S(2)}) %collective-permute-start) | collective-permute-done | bytes 131104 | tf_op jit(solution)/shard_map/ppermute | solution.py:37
  11.1 1.5 %collective-permute-start.5 = (bf16[32,2048]{1,0:T(8,128)(2,1)S(1)}, bf16[32,2048]{1,0:T(8,128)(2,1)S(1)}, u32[]{:S(2)}, u32[]{:S(2)}) collective-permute-start(bf16[32,2048]{1,0:T(8,128)(2,1)S(1)} %get-tuple-element.30.own), channel_id=1, source_target_pairs={{0,3},{1,2},{2,1},{3,0},{4,7},{5,6},{6,5},{7,4},{8,11},{9,10},{10,... | collective-permute-start | bytes 393224 | tf_op jit(solution)/shard_map/ppermute | solution.py:37
  12.7 0.0 collective-permute-done.1.refs_0_
  12.7 0.0 collective-permute-done.2.refs_1_
  12.7 0.0 collective-permute-done.3.refs_2_
  12.7 3.1 %forward.1 = (bf16[32,2048]{1,0:T(8,128)(2,1)S(1)}, bf16[32,2048]{1,0:T(8,128)(2,1)}, f32[2,2,64,176]{3,2,1,0:T(8,128)S(1)}) custom-call(s32[1]{0:T(128)} %bitcast.flag, bf16[32,2048]{1,0:T(8,128)(2,1)S(1)} %get-tuple-element.25.own, bf16[32,2048]{1,0:T(8,128)(2,1)S(1)} %collective-permute-done.far, bf16[176,2048]{1,0:T(8,128)(2,1)S(1)} %collective-permute-done.1.refs_0_, ...), custom_call_target="tpu_custom_call" | custom-call | tf_op jit(solution)/shard_map/forward/pallas_call | solution.py:240
  15.8 0.0 copy-start.5
  15.8 0.6 %copy-done.5 = bf16[32,2048]{1,0:T(8,128)(2,1)} copy-done((bf16[32,2048]{1,0:T(8,128)(2,1)}, bf16[32,2048]{1,0:T(8,128)(2,1)S(1)}, u32[]{:S(2)}) %copy-start.5) | copy-done | bytes 131096
  16.4 0.0 collective-permute-done.5.far
  16.4 0.0 copy-start.1
  16.4 0.7 %copy-done.1 = bf16[32,2048]{1,0:T(8,128)(2,1)} copy-done((bf16[32,2048]{1,0:T(8,128)(2,1)}, bf16[32,2048]{1,0:T(8,128)(2,1)S(1)}, u32[]{:S(2)}) %copy-start.1) | copy-done | bytes 131096
  17.1 0.0 copy-start.2
  17.1 0.9 %copy-done.2 = bf16[32,2048]{1,0:T(8,128)(2,1)S(1)} copy-done((bf16[32,2048]{1,0:T(8,128)(2,1)S(1)}, bf16[32,2048]{1,0:T(8,128)(2,1)}, u32[]{:S(2)}) %copy-start.2) | copy-done | bytes 131096
  18.0 0.0 copy-start
  18.0 2.9 %backward.1 = (bf16[32,2048]{1,0:T(8,128)(2,1)S(1)}, bf16[32,2048]{1,0:T(8,128)(2,1)}) custom-call(s32[1]{0:T(128)} %bitcast.flag, bf16[32,2048]{1,0:T(8,128)(2,1)S(1)} %get-tuple-element.30.own, bf16[32,2048]{1,0:T(8,128)(2,1)S(1)} %copy-done.2, f32[2,2,64,176]{3,2,1,0:T(8,128)S(1)} %get-tuple-element.31.act, ...), custom_call_target="tpu_custom_call" | custom-call | tf_op jit(solution)/shard_map/backward/pallas_call | solution.py:254
  20.9 0.0 copy-start.7
  20.9 0.6 %copy-done.7 = bf16[32,2048]{1,0:T(8,128)(2,1)} copy-done((bf16[32,2048]{1,0:T(8,128)(2,1)}, bf16[32,2048]{1,0:T(8,128)(2,1)S(1)}, u32[]{:S(2)}) %copy-start.7) | copy-done | bytes 131096
  21.6 1.7 %collective-permute-start.6 = (bf16[32,2048]{1,0:T(8,128)(2,1)}, bf16[32,2048]{1,0:T(8,128)(2,1)S(1)}, u32[]{:S(2)}, u32[]{:S(2)}) collective-permute-start(bf16[32,2048]{1,0:T(8,128)(2,1)} %get-tuple-element.33), channel_id=1, source_target_pairs={{0,3},{1,2},{2,1},{3,0},{4,7},{5,6},{6,5},{7,4},{8,11},{9,10},{10,... | collective-permute-start | bytes 393224 | tf_op jit(solution)/shard_map/ppermute | solution.py:37
  23.3 0.0 collective-permute-start.4
  23.3 0.1 label.1.label_tile
  23.4 0.0 copy-done
  23.4 0.7 %student.1 = (f32[16,128]{1,0:T(8,128)S(1)}, f32[8,37984]{1,0:T(8,128)S(1)}, f32[8,37984]{1,0:T(8,128)S(1)}) custom-call(s32[8,128]{1,0:T(8,128)S(1)} %label.1.label_tile, bf16[8,37984]{1,0:T(8,128)(2,1)S(1)} %bitcast.15), custom_call_target="tpu_custom_call" | custom-call | tf_op jit(solution)/shard_map/student/pallas_call | solution.py:592
  24.1 0.0 collective-permute-done.7.teacher
  24.1 0.5 %teacher.1.stats.own.refs_0_ = f32[16,128]{1,0:T(8,128)S(1)} custom-call(bf16[8,37984]{1,0:T(8,128)(2,1)S(1)} %bitcast.16, bf16[8,37984]{1,0:T(8,128)(2,1)S(1)} %collective-permute-done.7.teacher, f32[16,128]{1,0:T(8,128)S(1)} %get-tuple-element.41.student_stats), custom_call_target="tpu_custom_call" | custom-call | tf_op jit(solution)/shard_map/teacher/pallas_call | solution.py:608
  24.6 1.7 %collective-permute-start.10 = (f32[16,128]{1,0:T(8,128)S(1)}, f32[16,128]{1,0:T(8,128)S(1)}, u32[]{:S(2)}, u32[]{:S(2)}) collective-permute-start(f32[16,128]{1,0:T(8,128)S(1)} %teacher.1.stats.own.refs_0_), channel_id=1, source_target_pairs={{0,3},{1,2},{2,1},{3,0},{4,7},{5,6},{6,5},{7,4},{8,11},{9,10},{10,... | collective-permute-start | bytes 24584 | tf_op jit(solution)/shard_map/ppermute | solution.py:37
  26.3 0.0 collective-permute-start.8
  26.3 0.5 %collective-permute-start.9 = (f32[16,128]{1,0:T(8,128)S(1)}, f32[16,128]{1,0:T(8,128)S(1)}, u32[]{:S(2)}, u32[]{:S(2)}) collective-permute-start(f32[16,128]{1,0:T(8,128)S(1)} %teacher.1.stats.own.refs_0_), channel_id=1, source_target_pairs={{0,2},{1,3},{2,0},{3,1},{4,6},{5,7},{6,4},{7,5},{8,10},{9,11},{10,... | collective-permute-start | bytes 24584 | tf_op jit(solution)/shard_map/ppermute | solution.py:37
  26.8 0.2 power.1.teacher
  27.0 2.7 %collective-permute-done.10.refs_3_ = f32[16,128]{1,0:T(8,128)S(1)} collective-permute-done((f32[16,128]{1,0:T(8,128)S(1)}, f32[16,128]{1,0:T(8,128)S(1)}, u32[]{:S(2)}, u32[]{:S(2)}) %collective-permute-start.10) | collective-permute-done | bytes 8224 | tf_op jit(solution)/shard_map/ppermute | solution.py:37
  29.8 0.0 collective-permute-done.8.refs_1_
  29.8 1.0 %collective-permute-done.9.refs_2_ = f32[16,128]{1,0:T(8,128)S(1)} collective-permute-done((f32[16,128]{1,0:T(8,128)S(1)}, f32[16,128]{1,0:T(8,128)S(1)}, u32[]{:S(2)}, u32[]{:S(2)}) %collective-permute-start.9) | collective-permute-done | bytes 8224 | tf_op jit(solution)/shard_map/ppermute | solution.py:37
  30.7 0.0 copy-start.4
  30.7 0.0 copy-start.6
  30.7 0.0 copy-start.8
  30.7 1.1 %final.1 = (f32[1,8]{1,0:T(1,128)}, bf16[8,37984]{1,0:T(8,128)(2,1)}) custom-call(s32[1]{0:T(128)} %bitcast.flag, f32[8,37984]{1,0:T(8,128)S(1)} %get-tuple-element.40.student, f32[8,37984]{1,0:T(8,128)S(1)} %power.1.teacher, f32[8,37984]{1,0:T(8,128)S(1)} %get-tuple-element.42.hit, f32[16,128]{1,0:T(8,128)S(1)} %teacher.1.stats.own.refs_0_, ...), custom_call_target="tpu_custom_call" | custom-call | tf_op jit(solution)/shard_map/final/pallas_call | solution.py:621
  31.9 0.0 collective-permute-done.6.refs_3_
  31.9 0.0 collective-permute-done.4.refs_1_
  31.9 0.0 copy-done.4
  31.9 0.0 copy-done.6
  31.9 0.0 copy-done.8
  31.9 1.3 %combine.1 = (bf16[128,2048]{1,0:T(8,128)(2,1)}, bf16[128,2048]{1,0:T(8,128)(2,1)}, f32[4,128]{1,0:T(4,128)}) custom-call(bf16[32,2048]{1,0:T(8,128)(2,1)S(1)} %copy-done.6, bf16[32,2048]{1,0:T(8,128)(2,1)S(1)} %collective-permute-done.4.refs_1_, bf16[32,2048]{1,0:T(8,128)(2,1)S(1)} %copy-done.8, bf16[32,2048]{1,0:T(8,128)(2,1)S(1)} %collective-permute-done.6.refs_3_, ...), custom_call_target="tpu_custom_call" | custom-call | tf_op jit(solution)/shard_map/combine/pallas_call | solution.py:330
Async XLA Ops:
  0.6 12.0 %collective-permute-start.1 = (bf16[176,2048]{1,0:T(8,128)(2,1)}, bf16[176,2048]{1,0:T(8,128)(2,1)S(1)}, u32[]{:S(2)}, u32[]{:S(2)}) collective-permute-start(bf16[176,2048]{1,0:T(8,128)(2,1)} %bitcast.17), channel_id=1, source_target_pairs={{0,1},{1,0},{2,3},{3,2},{4,5},{5,4},{6,7},{7,6},{8,9},{9,8},{10,11... | collective-permute-start | bytes 2162696 | tf_op jit(solution)/shard_map/ppermute | solution.py:37
  1.2 11.5 %collective-permute-start.2 = (bf16[176,2048]{1,0:T(8,128)(2,1)}, bf16[176,2048]{1,0:T(8,128)(2,1)S(1)}, u32[]{:S(2)}, u32[]{:S(2)}) collective-permute-start(bf16[176,2048]{1,0:T(8,128)(2,1)} %bitcast.20), channel_id=1, source_target_pairs={{0,1},{1,0},{2,3},{3,2},{4,5},{5,4},{6,7},{7,6},{8,9},{9,8},{10,11... | collective-permute-start | bytes 2162696 | tf_op jit(solution)/shard_map/ppermute | solution.py:37
  1.3 11.4 %collective-permute-start.3 = (bf16[176,2048]{1,0:T(8,128)(2,1)}, bf16[176,2048]{1,0:T(8,128)(2,1)S(1)}, u32[]{:S(2)}, u32[]{:S(2)}) collective-permute-start(bf16[176,2048]{1,0:T(8,128)(2,1)} %bitcast.23), channel_id=1, source_target_pairs={{0,1},{1,0},{2,3},{3,2},{4,5},{5,4},{6,7},{7,6},{8,9},{9,8},{10,11... | collective-permute-start | bytes 2162696 | tf_op jit(solution)/shard_map/ppermute | solution.py:37
  1.7 22.4 %collective-permute-start.7 = (bf16[8,37984]{1,0:T(8,128)(2,1)}, bf16[8,37984]{1,0:T(8,128)(2,1)S(1)}, u32[]{:S(2)}, u32[]{:S(2)}) collective-permute-start(bf16[8,37984]{1,0:T(8,128)(2,1)} %bitcast.28), channel_id=1, source_target_pairs={{0,4},{4,8},{8,12},{12,16},{16,20},{20,24},{24,28},{28,0},{1,5},{5... | collective-permute-start | bytes 1823240 | tf_op jit(solution)/shard_map/ppermute | solution.py:42
  5.6 5.5 %collective-permute-start = (bf16[32,2048]{1,0:T(8,128)(2,1)S(1)}, bf16[32,2048]{1,0:T(8,128)(2,1)S(1)}, u32[]{:S(2)}, u32[]{:S(2)}) collective-permute-start(bf16[32,2048]{1,0:T(8,128)(2,1)S(1)} %get-tuple-element.25.own), channel_id=1, source_target_pairs={{0,3},{1,2},{2,1},{3,0},{4,7},{5,6},{6,5},{7,4},{8,11},{9,10},{10,... | collective-permute-start | bytes 393224 | tf_op jit(solution)/shard_map/ppermute | solution.py:37
  8.2 0.7 %copy-start.3 = (bf16[32,2048]{1,0:T(8,128)(2,1)}, bf16[32,2048]{1,0:T(8,128)(2,1)S(1)}, u32[]{:S(2)}) copy-start(bf16[32,2048]{1,0:T(8,128)(2,1)S(1)} %get-tuple-element.35.refs_7_) | copy-start | bytes 393220
  11.1 5.3 %collective-permute-start.5 = (bf16[32,2048]{1,0:T(8,128)(2,1)S(1)}, bf16[32,2048]{1,0:T(8,128)(2,1)S(1)}, u32[]{:S(2)}, u32[]{:S(2)}) collective-permute-start(bf16[32,2048]{1,0:T(8,128)(2,1)S(1)} %get-tuple-element.30.own), channel_id=1, source_target_pairs={{0,3},{1,2},{2,1},{3,0},{4,7},{5,6},{6,5},{7,4},{8,11},{9,10},{10,... | collective-permute-start | bytes 393224 | tf_op jit(solution)/shard_map/ppermute | solution.py:37
  15.8 0.7 %copy-start.5 = (bf16[32,2048]{1,0:T(8,128)(2,1)}, bf16[32,2048]{1,0:T(8,128)(2,1)S(1)}, u32[]{:S(2)}) copy-start(bf16[32,2048]{1,0:T(8,128)(2,1)S(1)} %get-tuple-element.26.refs_0_) | copy-start | bytes 393220
  16.4 0.7 %copy-start.1 = (bf16[32,2048]{1,0:T(8,128)(2,1)}, bf16[32,2048]{1,0:T(8,128)(2,1)S(1)}, u32[]{:S(2)}) copy-start(bf16[32,2048]{1,0:T(8,128)(2,1)S(1)} %collective-permute-done.5.far) | copy-start | bytes 393220
  17.1 0.9 %copy-start.2 = (bf16[32,2048]{1,0:T(8,128)(2,1)S(1)}, bf16[32,2048]{1,0:T(8,128)(2,1)}, u32[]{:S(2)}) copy-start(bf16[32,2048]{1,0:T(8,128)(2,1)} %copy-done.1) | copy-start | bytes 393220
  18.0 5.4 %copy-start = (bf16[1,8,37984]{2,1,0:T(8,128)(2,1)S(1)}, bf16[1,8,37984]{2,1,0:T(8,128)(2,1)}, u32[]{:S(2)}) copy-start(bf16[1,8,37984]{2,1,0:T(8,128)(2,1)} %param.17) | copy-start | bytes 1823236
  20.9 0.6 %copy-start.7 = (bf16[32,2048]{1,0:T(8,128)(2,1)}, bf16[32,2048]{1,0:T(8,128)(2,1)S(1)}, u32[]{:S(2)}) copy-start(bf16[32,2048]{1,0:T(8,128)(2,1)S(1)} %get-tuple-element.32.refs_2_) | copy-start | bytes 393220
  21.6 10.3 %collective-permute-start.6 = (bf16[32,2048]{1,0:T(8,128)(2,1)}, bf16[32,2048]{1,0:T(8,128)(2,1)S(1)}, u32[]{:S(2)}, u32[]{:S(2)}) collective-permute-start(bf16[32,2048]{1,0:T(8,128)(2,1)} %get-tuple-element.33), channel_id=1, source_target_pairs={{0,3},{1,2},{2,1},{3,0},{4,7},{5,6},{6,5},{7,4},{8,11},{9,10},{10,... | collective-permute-start | bytes 393224 | tf_op jit(solution)/shard_map/ppermute | solution.py:37
  23.3 8.6 %collective-permute-start.4 = (bf16[32,2048]{1,0:T(8,128)(2,1)}, bf16[32,2048]{1,0:T(8,128)(2,1)S(1)}, u32[]{:S(2)}, u32[]{:S(2)}) collective-permute-start(bf16[32,2048]{1,0:T(8,128)(2,1)} %get-tuple-element.27), channel_id=1, source_target_pairs={{0,3},{1,2},{2,1},{3,0},{4,7},{5,6},{6,5},{7,4},{8,11},{9,10},{10,... | collective-permute-start | bytes 393224 | tf_op jit(solution)/shard_map/ppermute | solution.py:37
  24.6 5.2 %collective-permute-start.10 = (f32[16,128]{1,0:T(8,128)S(1)}, f32[16,128]{1,0:T(8,128)S(1)}, u32[]{:S(2)}, u32[]{:S(2)}) collective-permute-start(f32[16,128]{1,0:T(8,128)S(1)} %teacher.1.stats.own.refs_0_), channel_id=1, source_target_pairs={{0,3},{1,2},{2,1},{3,0},{4,7},{5,6},{6,5},{7,4},{8,11},{9,10},{10,... | collective-permute-start | bytes 24584 | tf_op jit(solution)/shard_map/ppermute | solution.py:37
  26.3 3.5 %collective-permute-start.8 = (f32[16,128]{1,0:T(8,128)S(1)}, f32[16,128]{1,0:T(8,128)S(1)}, u32[]{:S(2)}, u32[]{:S(2)}) collective-permute-start(f32[16,128]{1,0:T(8,128)S(1)} %teacher.1.stats.own.refs_0_), channel_id=1, source_target_pairs={{0,1},{1,0},{2,3},{3,2},{4,5},{5,4},{6,7},{7,6},{8,9},{9,8},{10,11... | collective-permute-start | bytes 24584 | tf_op jit(solution)/shard_map/ppermute | solution.py:37
  26.3 4.5 %collective-permute-start.9 = (f32[16,128]{1,0:T(8,128)S(1)}, f32[16,128]{1,0:T(8,128)S(1)}, u32[]{:S(2)}, u32[]{:S(2)}) collective-permute-start(f32[16,128]{1,0:T(8,128)S(1)} %teacher.1.stats.own.refs_0_), channel_id=1, source_target_pairs={{0,2},{1,3},{2,0},{3,1},{4,6},{5,7},{6,4},{7,5},{8,10},{9,11},{10,... | collective-permute-start | bytes 24584 | tf_op jit(solution)/shard_map/ppermute | solution.py:37
  30.7 1.1 %copy-start.4 = (bf16[32,2048]{1,0:T(8,128)(2,1)S(1)}, bf16[32,2048]{1,0:T(8,128)(2,1)}, u32[]{:S(2)}) copy-start(bf16[32,2048]{1,0:T(8,128)(2,1)} %copy-done.3) | copy-start | bytes 393220
  30.7 1.2 %copy-start.6 = (bf16[32,2048]{1,0:T(8,128)(2,1)S(1)}, bf16[32,2048]{1,0:T(8,128)(2,1)}, u32[]{:S(2)}) copy-start(bf16[32,2048]{1,0:T(8,128)(2,1)} %copy-done.5) | copy-start | bytes 393220
  30.7 1.2 %copy-start.8 = (bf16[32,2048]{1,0:T(8,128)(2,1)S(1)}, bf16[32,2048]{1,0:T(8,128)(2,1)}, u32[]{:S(2)}) copy-start(bf16[32,2048]{1,0:T(8,128)(2,1)} %copy-done.7) | copy-start | bytes 393220

commit v7 on v6

--- a/solution.py
+++ b/solution.py
@@ -197,9 +197,8 @@
     @pl.when(flag[0] >= 0)
     def _():
         out = total[...] + rounded(forward_half(both(own, far), *buffers, act.at[1], wait))
-        out = out.astype(jnp.bfloat16)
         keep[...] = out[:half]
-        send[...] = out[half:]
+        send[...] = out[half:].astype(jnp.bfloat16)
 
 
 def rounded(value):
@@ -222,9 +221,8 @@
     @pl.when(flag[0] >= 0)
     def _():
         grad = total[...] + rounded(backward_half(both(own, far), act.at[1], *buffers, wait))
-        grad = grad.astype(jnp.bfloat16)
         keep[...] = grad[:half]
-        send[...] = grad[half:]
+        send[...] = grad[half:].astype(jnp.bfloat16)
 
 
 def buffers_of(weights):
@@ -239,7 +237,7 @@
     act = jax.ShapeDtypeStruct((2, 2, 2 * half, held[0].shape[0]), jnp.float32)
     return pl.pallas_call(
         forward_kernel,
-        out_shape=(part, part, act),
+        out_shape=(jax.ShapeDtypeStruct((half, width), jnp.float32), part, act),
         in_specs=[pl.BlockSpec(memory_space=pltpu.SMEM)] + vmem(5) + hbm(3),
         out_specs=tuple(vmem(3)),
         scratch_shapes=[pltpu.VMEM((2 * half, width), jnp.float32)] + buffers_of(fetched_w),
@@ -253,7 +251,7 @@
     part = jax.ShapeDtypeStruct((half, width), jnp.bfloat16)
     return pl.pallas_call(
         backward_kernel,
-        out_shape=(part, part),
+        out_shape=(jax.ShapeDtypeStruct((half, width), jnp.float32), part),
         in_specs=[pl.BlockSpec(memory_space=pltpu.SMEM)] + vmem(6) + hbm(3),
         out_specs=tuple(vmem(2)),
         scratch_shapes=[pltpu.VMEM((2 * half, width), jnp.float32)] + buffers_of(fetched_w),

time: 33.4 us -> 32.9 us (0.985)
  local copies, waits for them, and re-layouts: 3.51 us -> 2.04 us
  Pallas kernels: 12.5 us -> 13.4 us
    unnamed x18 -> x14, local copies, waits for them, and re-layouts: 3.51 us -> 2.04 us
    pallas_call x2, Pallas kernels: 6 us -> 6.92 us  [the longest x1 3.84 us: backward(): pl.pallas_call(backward_kernel, out_shape=(jax.ShapeDtypeStruct((half, wi...]
  transfers between devices with their start and end apart: 11 -> 11, of which waited for: 3 -> 3; matrix products, arithmetic and copies ran while one was open for 0% -> 0% of each run, Pallas kernels for 34% -> 37%
where the time goes in v7:
time: 32.9 us; the launch traced here: 32.7 us
  Pallas kernels  13.4 us (41%)
  starting transfers between devices  10.5 us (32%)
  waiting for transfers between devices  6.04 us (18%)
  local copies, waits for them, and re-layouts  2.04 us (6%)
  between operations  0.76 us (2%)
    ppermute x10, starting transfers between devices, swapped(): return lax.ppermute(value, axis, [(k, k ^ bits) for k in range(count)])  7.87 us
    ppermute x10, waiting for transfers between devices, swapped(): return lax.ppermute(value, axis, [(k, k ^ bits) for k in range(count)])  6.04 us
    pallas_call x1, Pallas kernels, backward(): pl.pallas_call(backward_kernel, out_shape=(jax.ShapeDtypeStruct((half, wi...  3.84 us
    pallas_call x1, Pallas kernels, forward(): pl.pallas_call(forward_kernel, out_shape=(jax.ShapeDtypeStruct((half, wid...  3.08 us
    ppermute x1, starting transfers between devices, onward(): lax.ppermute(value, axis, [(k, (k + 1) % count) for k in range(count)])  2.58 us
    unnamed x14, local copies, waits for them, and re-layouts  2.04 us
    pallas_call x1, Pallas kernels, slot_rows(): pl.pallas_call(functools.partial(rows_kernel, n_window), out_shape=(jax.S...  1.29 us
    pallas_call x1, Pallas kernels, slot_scaled(): pl.pallas_call(functools.partial(scaled_kernel, n_window), out_shape=(wid...  1.29 us
  transfers between devices with their start and end apart: 11, of which 3 were waited for; matrix products, arithmetic and copies ran while one was open for 0% of the time, Pallas kernels for 37%

profile of v7, /device:TPU:0, one launch (start us, length us, event | category | flops | bytes accessed | tf_op | source)
XLA Modules:
  0.0 32.7 jit_solution(5480719102153287832)
XLA Ops:
  0.6 0.6 %collective-permute-start.1 = (bf16[176,2048]{1,0:T(8,128)(2,1)}, bf16[176,2048]{1,0:T(8,128)(2,1)S(1)}, u32[]{:S(2)}, u32[]{:S(2)}) collective-permute-start(bf16[176,2048]{1,0:T(8,128)(2,1)} %bitcast.17), channel_id=1, source_target_pairs={{0,1},{1,0},{2,3},{3,2},{4,5},{5,4},{6,7},{7,6},{8,9},{9,8},{10,11... | collective-permute-start | bytes 2162696 | tf_op jit(solution)/shard_map/ppermute | solution.py:37
  1.2 0.1 collective-permute-start.2
  1.3 0.4 %collective-permute-start.3 = (bf16[176,2048]{1,0:T(8,128)(2,1)}, bf16[176,2048]{1,0:T(8,128)(2,1)S(1)}, u32[]{:S(2)}, u32[]{:S(2)}) collective-permute-start(bf16[176,2048]{1,0:T(8,128)(2,1)} %bitcast.23), channel_id=1, source_target_pairs={{0,1},{1,0},{2,3},{3,2},{4,5},{5,4},{6,7},{7,6},{8,9},{9,8},{10,11... | collective-permute-start | bytes 2162696 | tf_op jit(solution)/shard_map/ppermute | solution.py:37
  1.7 2.6 %collective-permute-start.7 = (bf16[8,37984]{1,0:T(8,128)(2,1)}, bf16[8,37984]{1,0:T(8,128)(2,1)S(1)}, u32[]{:S(2)}, u32[]{:S(2)}) collective-permute-start(bf16[8,37984]{1,0:T(8,128)(2,1)} %bitcast.28), channel_id=1, source_target_pairs={{0,4},{4,8},{8,12},{12,16},{16,20},{20,24},{24,28},{28,0},{1,5},{5... | collective-permute-start | bytes 1823240 | tf_op jit(solution)/shard_map/ppermute | solution.py:42
  4.3 1.3 %slot_rows.1 = (bf16[32,2048]{1,0:T(8,128)(2,1)S(1)}, f32[32,128]{1,0:T(8,128)S(1)}, s32[4,128]{1,0:T(4,128)S(1)}) custom-call(s32[4,128]{1,0:T(4,128)} %bitcast.26, bf16[128,2048]{1,0:T(8,128)(2,1)} %tokens_hbm.1), custom_call_target="tpu_custom_call" | custom-call | tf_op jit(solution)/shard_map/slot_rows/pallas_call | solution.py:108
  5.6 1.3 %collective-permute-start = (bf16[32,2048]{1,0:T(8,128)(2,1)S(1)}, bf16[32,2048]{1,0:T(8,128)(2,1)S(1)}, u32[]{:S(2)}, u32[]{:S(2)}) collective-permute-start(bf16[32,2048]{1,0:T(8,128)(2,1)S(1)} %get-tuple-element.25.own), channel_id=1, source_target_pairs={{0,3},{1,2},{2,1},{3,0},{4,7},{5,6},{6,5},{7,4},{8,11},{9,10},{10,... | collective-permute-start | bytes 393224 | tf_op jit(solution)/shard_map/ppermute | solution.py:37
  6.9 1.3 %slot_scaled.1 = (bf16[32,2048]{1,0:T(8,128)(2,1)S(1)}, bf16[32,2048]{1,0:T(8,128)(2,1)S(1)}, f32[32,128]{1,0:T(8,128)S(1)}, s32[1,8]{1,0:T(1,128)S(1)}) custom-call(s32[4,128]{1,0:T(4,128)S(1)} %get-tuple-element.28.ids.refs_4_, f32[32,128]{1,0:T(8,128)S(1)} %get-tuple-element.29.select.refs_5_, f32[4,128]{1,0:T(4,128)} %bitcast.27, ...), custom_call_target="tpu_custom_call" | custom-call | tf_op jit(solution)/shard_map/slot_scaled/pallas_call | solution.py:129
  8.2 0.0 copy-start.5
  8.2 0.6 %copy-done.5 = bf16[32,2048]{1,0:T(8,128)(2,1)} copy-done((bf16[32,2048]{1,0:T(8,128)(2,1)}, bf16[32,2048]{1,0:T(8,128)(2,1)S(1)}, u32[]{:S(2)}) %copy-start.5) | copy-done | bytes 131096
  8.8 2.3 %collective-permute-done.far = bf16[32,2048]{1,0:T(8,128)(2,1)S(1)} collective-permute-done((bf16[32,2048]{1,0:T(8,128)(2,1)S(1)}, bf16[32,2048]{1,0:T(8,128)(2,1)S(1)}, u32[]{:S(2)}, u32[]{:S(2)}) %collective-permute-start) | collective-permute-done | bytes 131104 | tf_op jit(solution)/shard_map/ppermute | solution.py:37
  11.1 1.5 %collective-permute-start.5 = (bf16[32,2048]{1,0:T(8,128)(2,1)S(1)}, bf16[32,2048]{1,0:T(8,128)(2,1)}, u32[]{:S(2)}, u32[]{:S(2)}) collective-permute-start(bf16[32,2048]{1,0:T(8,128)(2,1)S(1)} %get-tuple-element.30.own), channel_id=1, source_target_pairs={{0,3},{1,2},{2,1},{3,0},{4,7},{5,6},{6,5},{7,4},{8,11},{9,10},{10,... | collective-permute-start | bytes 393224 | tf_op jit(solution)/shard_map/ppermute | solution.py:37
  12.7 0.0 collective-permute-done.1.refs_0_
  12.7 0.0 collective-permute-done.2.refs_1_
  12.7 0.0 collective-permute-done.3.refs_2_
  12.7 3.1 %forward.1 = (f32[32,2048]{1,0:T(8,128)S(1)}, bf16[32,2048]{1,0:T(8,128)(2,1)}, f32[2,2,64,176]{3,2,1,0:T(8,128)S(1)}) custom-call(s32[1]{0:T(128)} %bitcast.flag, bf16[32,2048]{1,0:T(8,128)(2,1)S(1)} %get-tuple-element.25.own, bf16[32,2048]{1,0:T(8,128)(2,1)S(1)} %collective-permute-done.far, bf16[176,2048]{1,0:T(8,128)(2,1)S(1)} %collective-permute-done.1.refs_0_, ...), custom_call_target="tpu_custom_call" | custom-call | tf_op jit(solution)/shard_map/forward/pallas_call | solution.py:238
  15.8 0.0 copy-start.1
  15.8 0.7 %copy-done.1 = f32[32,2048]{1,0:T(8,128)} copy-done((f32[32,2048]{1,0:T(8,128)}, f32[32,2048]{1,0:T(8,128)S(1)}, u32[]{:S(2)}) %copy-start.1) | copy-done | bytes 262168
  16.5 0.0 collective-permute-done.5.far
  16.5 0.0 copy-start
  16.5 3.8 %backward.1 = (f32[32,2048]{1,0:T(8,128)S(1)}, bf16[32,2048]{1,0:T(8,128)(2,1)}) custom-call(s32[1]{0:T(128)} %bitcast.flag, bf16[32,2048]{1,0:T(8,128)(2,1)S(1)} %get-tuple-element.30.own, bf16[32,2048]{1,0:T(8,128)(2,1)} %collective-permute-done.5.far, f32[2,2,64,176]{3,2,1,0:T(8,128)S(1)} %get-tuple-element.31.act, ...), custom_call_target="tpu_custom_call" | custom-call | tf_op jit(solution)/shard_map/backward/pallas_call | solution.py:252
  20.3 0.0 copy-start.3
  20.3 0.7 %copy-done.3 = f32[32,2048]{1,0:T(8,128)} copy-done((f32[32,2048]{1,0:T(8,128)}, f32[32,2048]{1,0:T(8,128)S(1)}, u32[]{:S(2)}) %copy-start.3) | copy-done | bytes 262168
  21.0 1.7 %collective-permute-start.6 = (bf16[32,2048]{1,0:T(8,128)(2,1)}, bf16[32,2048]{1,0:T(8,128)(2,1)S(1)}, u32[]{:S(2)}, u32[]{:S(2)}) collective-permute-start(bf16[32,2048]{1,0:T(8,128)(2,1)} %get-tuple-element.33), channel_id=1, source_target_pairs={{0,3},{1,2},{2,1},{3,0},{4,7},{5,6},{6,5},{7,4},{8,11},{9,10},{10,... | collective-permute-start | bytes 393224 | tf_op jit(solution)/shard_map/ppermute | solution.py:37
  22.7 0.1 collective-permute-start.4
  22.8 0.1 label.1.label_tile
  22.9 0.0 copy-done
  22.9 0.7 %student.1 = (f32[16,128]{1,0:T(8,128)S(1)}, f32[8,37984]{1,0:T(8,128)S(1)}, f32[8,37984]{1,0:T(8,128)S(1)}) custom-call(s32[8,128]{1,0:T(8,128)S(1)} %label.1.label_tile, bf16[8,37984]{1,0:T(8,128)(2,1)S(1)} %bitcast.15), custom_call_target="tpu_custom_call" | custom-call | tf_op jit(solution)/shard_map/student/pallas_call | solution.py:590
  23.5 0.0 collective-permute-done.7.teacher
  23.5 0.5 %teacher.1.stats.own.refs_0_ = f32[16,128]{1,0:T(8,128)S(1)} custom-call(bf16[8,37984]{1,0:T(8,128)(2,1)S(1)} %bitcast.16, bf16[8,37984]{1,0:T(8,128)(2,1)S(1)} %collective-permute-done.7.teacher, f32[16,128]{1,0:T(8,128)S(1)} %get-tuple-element.41.student_stats), custom_call_target="tpu_custom_call" | custom-call | tf_op jit(solution)/shard_map/teacher/pallas_call | solution.py:606
  24.0 1.7 %collective-permute-start.10 = (f32[16,128]{1,0:T(8,128)S(1)}, f32[16,128]{1,0:T(8,128)S(1)}, u32[]{:S(2)}, u32[]{:S(2)}) collective-permute-start(f32[16,128]{1,0:T(8,128)S(1)} %teacher.1.stats.own.refs_0_), channel_id=1, source_target_pairs={{0,3},{1,2},{2,1},{3,0},{4,7},{5,6},{6,5},{7,4},{8,11},{9,10},{10,... | collective-permute-start | bytes 24584 | tf_op jit(solution)/shard_map/ppermute | solution.py:37
  25.7 0.0 collective-permute-start.8
  25.7 0.5 %collective-permute-start.9 = (f32[16,128]{1,0:T(8,128)S(1)}, f32[16,128]{1,0:T(8,128)S(1)}, u32[]{:S(2)}, u32[]{:S(2)}) collective-permute-start(f32[16,128]{1,0:T(8,128)S(1)} %teacher.1.stats.own.refs_0_), channel_id=1, source_target_pairs={{0,2},{1,3},{2,0},{3,1},{4,6},{5,7},{6,4},{7,5},{8,10},{9,11},{10,... | collective-permute-start | bytes 24584 | tf_op jit(solution)/shard_map/ppermute | solution.py:37
  26.2 0.2 power.1.teacher
  26.5 2.8 %collective-permute-done.10.refs_3_ = f32[16,128]{1,0:T(8,128)S(1)} collective-permute-done((f32[16,128]{1,0:T(8,128)S(1)}, f32[16,128]{1,0:T(8,128)S(1)}, u32[]{:S(2)}, u32[]{:S(2)}) %collective-permute-start.10) | collective-permute-done | bytes 8224 | tf_op jit(solution)/shard_map/ppermute | solution.py:37
  29.3 0.0 collective-permute-done.8.refs_1_
  29.3 0.9 %collective-permute-done.9.refs_2_ = f32[16,128]{1,0:T(8,128)S(1)} collective-permute-done((f32[16,128]{1,0:T(8,128)S(1)}, f32[16,128]{1,0:T(8,128)S(1)}, u32[]{:S(2)}, u32[]{:S(2)}) %collective-permute-start.9) | collective-permute-done | bytes 8224 | tf_op jit(solution)/shard_map/ppermute | solution.py:37
  30.2 0.0 copy-start.2
  30.2 0.0 copy-start.4
  30.2 0.0 copy-start.6
  30.2 1.1 %final.1 = (f32[1,8]{1,0:T(1,128)}, bf16[8,37984]{1,0:T(8,128)(2,1)}) custom-call(s32[1]{0:T(128)} %bitcast.flag, f32[8,37984]{1,0:T(8,128)S(1)} %get-tuple-element.40.student, f32[8,37984]{1,0:T(8,128)S(1)} %power.1.teacher, f32[8,37984]{1,0:T(8,128)S(1)} %get-tuple-element.42.hit, f32[16,128]{1,0:T(8,128)S(1)} %teacher.1.stats.own.refs_0_, ...), custom_call_target="tpu_custom_call" | custom-call | tf_op jit(solution)/shard_map/final/pallas_call | solution.py:619
  31.3 0.0 collective-permute-done.6.refs_3_
  31.3 0.0 collective-permute-done.4.refs_1_
  31.3 0.0 copy-done.2
  31.4 0.0 copy-done.4
  31.4 0.0 copy-done.6
  31.4 1.3 %combine.1 = (bf16[128,2048]{1,0:T(8,128)(2,1)}, bf16[128,2048]{1,0:T(8,128)(2,1)}, f32[4,128]{1,0:T(4,128)}) custom-call(f32[32,2048]{1,0:T(8,128)S(1)} %copy-done.2, bf16[32,2048]{1,0:T(8,128)(2,1)S(1)} %collective-permute-done.4.refs_1_, f32[32,2048]{1,0:T(8,128)S(1)} %copy-done.4, bf16[32,2048]{1,0:T(8,128)(2,1)S(1)} %collective-permute-done.6.refs_3_, ...), custom_call_target="tpu_custom_call" | custom-call | tf_op jit(solution)/shard_map/combine/pallas_call | solution.py:328
Async XLA Ops:
  0.6 12.0 %collective-permute-start.1 = (bf16[176,2048]{1,0:T(8,128)(2,1)}, bf16[176,2048]{1,0:T(8,128)(2,1)S(1)}, u32[]{:S(2)}, u32[]{:S(2)}) collective-permute-start(bf16[176,2048]{1,0:T(8,128)(2,1)} %bitcast.17), channel_id=1, source_target_pairs={{0,1},{1,0},{2,3},{3,2},{4,5},{5,4},{6,7},{7,6},{8,9},{9,8},{10,11... | collective-permute-start | bytes 2162696 | tf_op jit(solution)/shard_map/ppermute | solution.py:37
  1.2 11.5 %collective-permute-start.2 = (bf16[176,2048]{1,0:T(8,128)(2,1)}, bf16[176,2048]{1,0:T(8,128)(2,1)S(1)}, u32[]{:S(2)}, u32[]{:S(2)}) collective-permute-start(bf16[176,2048]{1,0:T(8,128)(2,1)} %bitcast.20), channel_id=1, source_target_pairs={{0,1},{1,0},{2,3},{3,2},{4,5},{5,4},{6,7},{7,6},{8,9},{9,8},{10,11... | collective-permute-start | bytes 2162696 | tf_op jit(solution)/shard_map/ppermute | solution.py:37
  1.3 11.4 %collective-permute-start.3 = (bf16[176,2048]{1,0:T(8,128)(2,1)}, bf16[176,2048]{1,0:T(8,128)(2,1)S(1)}, u32[]{:S(2)}, u32[]{:S(2)}) collective-permute-start(bf16[176,2048]{1,0:T(8,128)(2,1)} %bitcast.23), channel_id=1, source_target_pairs={{0,1},{1,0},{2,3},{3,2},{4,5},{5,4},{6,7},{7,6},{8,9},{9,8},{10,11... | collective-permute-start | bytes 2162696 | tf_op jit(solution)/shard_map/ppermute | solution.py:37
  1.7 21.8 %collective-permute-start.7 = (bf16[8,37984]{1,0:T(8,128)(2,1)}, bf16[8,37984]{1,0:T(8,128)(2,1)S(1)}, u32[]{:S(2)}, u32[]{:S(2)}) collective-permute-start(bf16[8,37984]{1,0:T(8,128)(2,1)} %bitcast.28), channel_id=1, source_target_pairs={{0,4},{4,8},{8,12},{12,16},{16,20},{20,24},{24,28},{28,0},{1,5},{5... | collective-permute-start | bytes 1823240 | tf_op jit(solution)/shard_map/ppermute | solution.py:42
  5.6 5.5 %collective-permute-start = (bf16[32,2048]{1,0:T(8,128)(2,1)S(1)}, bf16[32,2048]{1,0:T(8,128)(2,1)S(1)}, u32[]{:S(2)}, u32[]{:S(2)}) collective-permute-start(bf16[32,2048]{1,0:T(8,128)(2,1)S(1)} %get-tuple-element.25.own), channel_id=1, source_target_pairs={{0,3},{1,2},{2,1},{3,0},{4,7},{5,6},{6,5},{7,4},{8,11},{9,10},{10,... | collective-permute-start | bytes 393224 | tf_op jit(solution)/shard_map/ppermute | solution.py:37
  8.2 0.6 %copy-start.5 = (bf16[32,2048]{1,0:T(8,128)(2,1)}, bf16[32,2048]{1,0:T(8,128)(2,1)S(1)}, u32[]{:S(2)}) copy-start(bf16[32,2048]{1,0:T(8,128)(2,1)S(1)} %get-tuple-element.35.refs_7_) | copy-start | bytes 393220
  11.1 5.4 %collective-permute-start.5 = (bf16[32,2048]{1,0:T(8,128)(2,1)S(1)}, bf16[32,2048]{1,0:T(8,128)(2,1)}, u32[]{:S(2)}, u32[]{:S(2)}) collective-permute-start(bf16[32,2048]{1,0:T(8,128)(2,1)S(1)} %get-tuple-element.30.own), channel_id=1, source_target_pairs={{0,3},{1,2},{2,1},{3,0},{4,7},{5,6},{6,5},{7,4},{8,11},{9,10},{10,... | collective-permute-start | bytes 393224 | tf_op jit(solution)/shard_map/ppermute | solution.py:37
  15.8 0.7 %copy-start.1 = (f32[32,2048]{1,0:T(8,128)}, f32[32,2048]{1,0:T(8,128)S(1)}, u32[]{:S(2)}) copy-start(f32[32,2048]{1,0:T(8,128)S(1)} %get-tuple-element.26.refs_0_) | copy-start | bytes 786436
  16.5 6.4 %copy-start = (bf16[1,8,37984]{2,1,0:T(8,128)(2,1)S(1)}, bf16[1,8,37984]{2,1,0:T(8,128)(2,1)}, u32[]{:S(2)}) copy-start(bf16[1,8,37984]{2,1,0:T(8,128)(2,1)} %param.17) | copy-start | bytes 1823236
  20.3 0.7 %copy-start.3 = (f32[32,2048]{1,0:T(8,128)}, f32[32,2048]{1,0:T(8,128)S(1)}, u32[]{:S(2)}) copy-start(f32[32,2048]{1,0:T(8,128)S(1)} %get-tuple-element.32.refs_2_) | copy-start | bytes 786436
  21.0 10.3 %collective-permute-start.6 = (bf16[32,2048]{1,0:T(8,128)(2,1)}, bf16[32,2048]{1,0:T(8,128)(2,1)S(1)}, u32[]{:S(2)}, u32[]{:S(2)}) collective-permute-start(bf16[32,2048]{1,0:T(8,128)(2,1)} %get-tuple-element.33), channel_id=1, source_target_pairs={{0,3},{1,2},{2,1},{3,0},{4,7},{5,6},{6,5},{7,4},{8,11},{9,10},{10,... | collective-permute-start | bytes 393224 | tf_op jit(solution)/shard_map/ppermute | solution.py:37
  22.7 8.6 %collective-permute-start.4 = (bf16[32,2048]{1,0:T(8,128)(2,1)}, bf16[32,2048]{1,0:T(8,128)(2,1)S(1)}, u32[]{:S(2)}, u32[]{:S(2)}) collective-permute-start(bf16[32,2048]{1,0:T(8,128)(2,1)} %get-tuple-element.27), channel_id=1, source_target_pairs={{0,3},{1,2},{2,1},{3,0},{4,7},{5,6},{6,5},{7,4},{8,11},{9,10},{10,... | collective-permute-start | bytes 393224 | tf_op jit(solution)/shard_map/ppermute | solution.py:37
  24.0 5.3 %collective-permute-start.10 = (f32[16,128]{1,0:T(8,128)S(1)}, f32[16,128]{1,0:T(8,128)S(1)}, u32[]{:S(2)}, u32[]{:S(2)}) collective-permute-start(f32[16,128]{1,0:T(8,128)S(1)} %teacher.1.stats.own.refs_0_), channel_id=1, source_target_pairs={{0,3},{1,2},{2,1},{3,0},{4,7},{5,6},{6,5},{7,4},{8,11},{9,10},{10,... | collective-permute-start | bytes 24584 | tf_op jit(solution)/shard_map/ppermute | solution.py:37
  25.7 3.6 %collective-permute-start.8 = (f32[16,128]{1,0:T(8,128)S(1)}, f32[16,128]{1,0:T(8,128)S(1)}, u32[]{:S(2)}, u32[]{:S(2)}) collective-permute-start(f32[16,128]{1,0:T(8,128)S(1)} %teacher.1.stats.own.refs_0_), channel_id=1, source_target_pairs={{0,1},{1,0},{2,3},{3,2},{4,5},{5,4},{6,7},{7,6},{8,9},{9,8},{10,11... | collective-permute-start | bytes 24584 | tf_op jit(solution)/shard_map/ppermute | solution.py:37
  25.7 4.5 %collective-permute-start.9 = (f32[16,128]{1,0:T(8,128)S(1)}, f32[16,128]{1,0:T(8,128)S(1)}, u32[]{:S(2)}, u32[]{:S(2)}) collective-permute-start(f32[16,128]{1,0:T(8,128)S(1)} %teacher.1.stats.own.refs_0_), channel_id=1, source_target_pairs={{0,2},{1,3},{2,0},{3,1},{4,6},{5,7},{6,4},{7,5},{8,10},{9,11},{10,... | collective-permute-start | bytes 24584 | tf_op jit(solution)/shard_map/ppermute | solution.py:37
  30.2 1.1 %copy-start.2 = (f32[32,2048]{1,0:T(8,128)S(1)}, f32[32,2048]{1,0:T(8,128)}, u32[]{:S(2)}) copy-start(f32[32,2048]{1,0:T(8,128)} %copy-done.1) | copy-start | bytes 786436
  30.2 1.2 %copy-start.4 = (f32[32,2048]{1,0:T(8,128)S(1)}, f32[32,2048]{1,0:T(8,128)}, u32[]{:S(2)}) copy-start(f32[32,2048]{1,0:T(8,128)} %copy-done.3) | copy-start | bytes 786436
  30.2 1.2 %copy-start.6 = (bf16[32,2048]{1,0:T(8,128)(2,1)S(1)}, bf16[32,2048]{1,0:T(8,128)(2,1)}, u32[]{:S(2)}) copy-start(bf16[32,2048]{1,0:T(8,128)(2,1)} %copy-done.5) | copy-start | bytes 393220
